TPU v7x, 32 devices: a whole 2x2x4 slice. The times are simulated.
32 devices in a mesh: group: 4 (over z), ctx: 2 (over x), wshard: 4 (over y, core).
Axes of the slice: x: 2, y: 2, z: 4, core: 2. Of those that a mesh axis runs over, the one named last changes fastest.
Arguments:
- words: bfloat16 [16, 2048, 512], P(('group', 'wshard'), 'ctx'), may hold values from -6 to 6
- qkv_weight: bfloat16 [512, 1536], P('wshard'), may hold values from -0.25 to 0.25
- out_weight: bfloat16 [512, 512], P('wshard'), may hold values from -4 to 4
- up_weight: bfloat16 [512, 2048], P('wshard'), may hold values from -0.25 to 0.25
- down_weight: bfloat16 [2048, 512], P('wshard'), may hold values from -0.125 to 0.125
- norm1_gain: bfloat16 [512], P('wshard'), may hold values from 0.5 to 1.5
- norm1_bias: bfloat16 [512], P('wshard'), may hold values from -3 to 3
- norm2_gain: bfloat16 [512], P('wshard'), may hold values from 0.5 to 1.5
- norm2_bias: bfloat16 [512], P('wshard'), may hold values from -3 to 3
- up_bias: bfloat16 [2048], P('wshard'), may hold values from -3 to 3
- down_bias: bfloat16 [512], P('wshard'), may hold values from -3 to 3
- cotangent: bfloat16 [16, 2048, 512], P(('group', 'wshard'), 'ctx'), may hold values from -6 to 6
- seg_map: int32 [16, 4], P(('group', 'wshard')), may hold values from 0 to 1, as said below
- off_map: int32 [16, 4], P(('group', 'wshard')), may hold values from 0 to 1, as said below
Outputs:
- output: bfloat16 [16, 2048, 512], P(('group', 'wshard'), 'ctx')
- words_grad: float32 [16, 2048, 512], P(('group', 'wshard'), 'ctx')
- qkv_weight_grad: float32 [512, 1536], P('wshard')
- out_weight_grad: float32 [512, 512], P('wshard')
- up_weight_grad: float32 [512, 2048], P('wshard')
- down_weight_grad: float32 [2048, 512], P('wshard')
- norm1_gain_grad: float32 [512], P('wshard')
- norm1_bias_grad: float32 [512], P('wshard')
- norm2_gain_grad: float32 [512], P('wshard')
- norm2_bias_grad: float32 [512], P('wshard')
- up_bias_grad: float32 [2048], P('wshard')
- down_bias_grad: float32 [512], P('wshard')
Inputs may be any that keep to these rules, and one draw needn't show every extreme that they name: `seg_map`: in each row, 2 blocks carry 0 and each of the continuations 1 to 1 has 2 blocks, placed in any order. `off_map`: the prompt's blocks carry 0 to 1, each once; each continuation's blocks carry 0 to 1, each once.
All inputs are finite; a program needn't handle non-finite values.
Results may differ from a plain program's by a relative error of at most 0.04.
Values may be sent and summed in bfloat16 or wider, within the bound.
A program may use at most 128 MiB of HBM per device.

v0:
```python
import jax
import jax.numpy as jnp
from jax import lax
from jax.sharding import PartitionSpec as P

HEADS = 8
HEAD_DIM = 64
BLK = 512


eps = 1e-05
neg_big = -1e30


def passed_along(value, axis, by):
    peers = lax.axis_size(axis)
    return lax.ppermute(value, axis, [(i, (i + by) % peers) for i in range(peers)])


def layer_norm(features, norm_gain, norm_shift):
    row_mean = jnp.mean(features, axis=-1, keepdims=True)
    centred = features - row_mean
    inv_scale = lax.rsqrt(jnp.mean(centred * centred, axis=-1, keepdims=True) + eps)
    return centred * inv_scale * norm_gain + norm_shift


def gelu_tanh(features):
    return jax.nn.gelu(features, approximate=True)


def rows_of(array, block_id):
    return lax.dynamic_slice_in_dim(array, block_id * BLK, BLK, 0)


def cols_of(array, block_id):
    return lax.dynamic_slice_in_dim(array, block_id * BLK, BLK, 1)


def add_rows(array, update, block_id):
    return lax.dynamic_update_slice_in_dim(
        array, rows_of(array, block_id) + update, block_id * BLK, 0
    )


def put_rows(array, update, block_id):
    return lax.dynamic_update_slice_in_dim(array, update, block_id * BLK, 0)


def put_cols(array, update, block_id):
    return lax.dynamic_update_slice_in_dim(array, update, block_id * BLK, 1)


def block_info(seg_row, off_row, block_id):
    segment = lax.dynamic_index_in_dim(seg_row, block_id, 0, keepdims=False)
    position = lax.dynamic_index_in_dim(off_row, block_id, 0, keepdims=False)
    return (segment, position)


def pair_live(seg_row, off_row, query_block, key_block):
    query_seg, query_offset = block_info(seg_row, off_row, query_block)
    key_seg, key_offset = block_info(seg_row, off_row, key_block)
    return (query_seg == key_seg) & (key_offset <= query_offset) | (key_seg == 0) & (query_seg != 0)


def pair_mask(seg_row, off_row, query_block, key_block):
    query_seg, query_offset = block_info(seg_row, off_row, query_block)
    key_seg, key_offset = block_info(seg_row, off_row, key_block)
    row_ids = lax.broadcasted_iota(jnp.int32, (BLK, BLK), 0)
    col_ids = lax.broadcasted_iota(jnp.int32, (BLK, BLK), 1)
    query_pos = query_offset * BLK + row_ids
    key_pos = key_offset * BLK + col_ids
    return (query_seg == key_seg) & (key_pos <= query_pos) | (key_seg == 0) & (query_seg != 0)


def split_heads(tile_rows):
    return tile_rows.reshape(tile_rows.shape[0], HEADS, HEAD_DIM)


def tile_scores(query_tile, key_tile, allowed):
    raw_scores = jnp.einsum(
        "qhd,khd->hqk",
        split_heads(query_tile),
        split_heads(key_tile),
        preferred_element_type=jnp.float32,
    )
    return jnp.where(allowed[None], raw_scores * HEAD_DIM ** (-0.5), neg_big)


def tile_back(query_tile, key_tile, value_tile, grad_tile, norm_tile, delta_tile, allowed):
    scores = tile_scores(query_tile, key_tile, allowed)
    exp_terms = jnp.where(allowed[None], jnp.exp(scores - norm_tile[:, :, None]), 0.0)
    d_probs = jnp.einsum(
        "qhd,khd->hqk",
        split_heads(grad_tile),
        split_heads(value_tile),
        preferred_element_type=jnp.float32,
    )
    d_scores = (exp_terms * (d_probs - delta_tile[:, :, None])).astype(jnp.bfloat16)
    return (exp_terms.astype(jnp.bfloat16), d_scores)


def query_grad(d_scores, key_tile):
    part_rows = jnp.einsum(
        "hqk,khd->qhd", d_scores, split_heads(key_tile), preferred_element_type=jnp.float32
    )
    return part_rows.reshape(BLK, -1) * HEAD_DIM ** (-0.5)


def key_grad(d_scores, query_tile):
    part_rows = jnp.einsum(
        "hqk,qhd->khd", d_scores, split_heads(query_tile), preferred_element_type=jnp.float32
    )
    return part_rows.reshape(BLK, -1) * HEAD_DIM ** (-0.5)


def value_grad(probs_low, grad_tile):
    part_rows = jnp.einsum(
        "hqk,qhd->khd", probs_low, split_heads(grad_tile), preferred_element_type=jnp.float32
    )
    return part_rows.reshape(BLK, -1)


def unchanged(running):
    return running


def on_device(
    words,
    qkv_weight,
    out_weight,
    up_weight,
    down_weight,
    norm1_gain,
    norm1_bias,
    norm2_gain,
    norm2_bias,
    up_bias,
    down_bias,
    cotangent,
    seg_map,
    off_map,
):
    gathered = (
        lax.all_gather(qkv_weight, "wshard", axis=0, tiled=True),
        lax.all_gather(out_weight, "wshard", axis=0, tiled=True),
        lax.all_gather(up_weight, "wshard", axis=0, tiled=True),
        lax.all_gather(down_weight, "wshard", axis=0, tiled=True),
        lax.all_gather(norm1_gain, "wshard", axis=0, tiled=True),
        lax.all_gather(norm1_bias, "wshard", axis=0, tiled=True),
        lax.all_gather(norm2_gain, "wshard", axis=0, tiled=True),
        lax.all_gather(norm2_bias, "wshard", axis=0, tiled=True),
        lax.all_gather(up_bias, "wshard", axis=0, tiled=True),
        lax.all_gather(down_bias, "wshard", axis=0, tiled=True),
    )
    w_qkv, w_out, w_up, w_down = (gathered[0], gathered[1], gathered[2], gathered[3])
    gain1 = gathered[4].astype(jnp.float32)
    shift1 = gathered[5].astype(jnp.float32)
    gain2 = gathered[6].astype(jnp.float32)
    shift2 = gathered[7].astype(jnp.float32)
    bias_up = gathered[8].astype(jnp.float32)
    bias_down = gathered[9].astype(jnp.float32)
    seg_row = seg_map[0]
    off_row = off_map[0]
    cycle_place = lax.axis_index("ctx")
    cycle_count = lax.axis_size("ctx")
    inputs = words[0].astype(jnp.float32)
    local_rows = inputs.shape[0]
    local_blocks = local_rows // BLK
    first_block = cycle_place * local_blocks
    width = inputs.shape[1]
    normed1, pull_norm1 = jax.vjp(layer_norm, inputs, gain1, shift1)
    act1 = normed1.astype(jnp.bfloat16)
    qkv = jnp.dot(act1, w_qkv, preferred_element_type=jnp.float32)
    query_rows = qkv[:, :width].astype(jnp.bfloat16)
    key_rows = qkv[:, width : 2 * width].astype(jnp.bfloat16)
    value_rows = qkv[:, 2 * width :].astype(jnp.bfloat16)
    start_state = (
        jnp.full((HEADS, local_rows), neg_big, jnp.float32),
        jnp.zeros((HEADS, local_rows), jnp.float32),
        jnp.zeros((local_rows, width), jnp.float32),
    )
    shard_keys = lax.all_gather(key_rows, "ctx", axis=0, tiled=True)
    shard_values = lax.all_gather(value_rows, "ctx", axis=0, tiled=True)
    key_blocks = shard_keys.shape[0] // BLK

    def online_visit_pair(pair_index, state):
        row_block = pair_index // key_blocks
        col_block = pair_index % key_blocks
        query_block = first_block + row_block
        key_block = col_block

        def online_update_tile(state):
            run_max, run_sum, accum = state
            allowed = pair_mask(seg_row, off_row, query_block, key_block)
            scores = tile_scores(
                rows_of(query_rows, row_block), rows_of(shard_keys, col_block), allowed
            )
            old_max = cols_of(run_max, row_block)
            old_sum = cols_of(run_sum, row_block)
            new_max = jnp.maximum(old_max, jnp.max(scores, axis=-1))
            exp_terms = jnp.where(allowed[None], jnp.exp(scores - new_max[:, :, None]), 0.0)
            factor = jnp.exp(old_max - new_max)
            new_sum = old_sum * factor + jnp.sum(exp_terms, axis=-1)
            part_rows = jnp.einsum(
                "hqk,khd->qhd",
                exp_terms.astype(jnp.bfloat16),
                split_heads(rows_of(shard_values, col_block)),
                preferred_element_type=jnp.float32,
            )
            old_rows = rows_of(accum, row_block).reshape(BLK, HEADS, HEAD_DIM)
            new_rows = (old_rows * factor.T[:, :, None] + part_rows).reshape(BLK, -1)
            return (
                put_cols(run_max, new_max, row_block),
                put_cols(run_sum, new_sum, row_block),
                put_rows(accum, new_rows, row_block),
            )

        return lax.cond(
            pair_live(seg_row, off_row, query_block, key_block),
            online_update_tile,
            unchanged,
            state,
        )

    run_max, run_sum, accum = lax.fori_loop(
        0, local_blocks * key_blocks, online_visit_pair, start_state
    )
    log_norm = run_max + jnp.log(run_sum)
    attended = (accum.reshape(local_rows, HEADS, HEAD_DIM) / run_sum.T[:, :, None]).reshape(
        local_rows, width
    )
    attended_low = attended.astype(jnp.bfloat16)
    middle = inputs + jnp.dot(attended_low, w_out, preferred_element_type=jnp.float32)
    normed2, pull_norm2 = jax.vjp(layer_norm, middle, gain2, shift2)
    act2 = normed2.astype(jnp.bfloat16)
    hidden = jnp.dot(act2, w_up, preferred_element_type=jnp.float32) + bias_up
    gelu_out, pull_gelu = jax.vjp(gelu_tanh, hidden)
    gelu_low = gelu_out.astype(jnp.bfloat16)
    output = (
        middle + jnp.dot(gelu_low, w_down, preferred_element_type=jnp.float32) + bias_down
    ).astype(jnp.bfloat16)
    upstream = cotangent[0]
    upstream_f = upstream.astype(jnp.float32)
    grad_down = jnp.einsum("nf,nd->fd", gelu_low, upstream, preferred_element_type=jnp.float32)
    grad_bias_down = jnp.sum(upstream_f, axis=0)
    d_gelu = jnp.einsum("nd,fd->nf", upstream, w_down, preferred_element_type=jnp.float32)
    d_hidden = pull_gelu(d_gelu)[0].astype(jnp.bfloat16)
    grad_up = jnp.einsum("nd,nf->df", act2, d_hidden, preferred_element_type=jnp.float32)
    grad_bias_up = jnp.sum(d_hidden.astype(jnp.float32), axis=0)
    d_act2 = jnp.einsum("nf,df->nd", d_hidden, w_up, preferred_element_type=jnp.float32)
    d_middle_norm, grad_gain2, grad_shift2 = pull_norm2(d_act2)
    d_middle = (upstream_f + d_middle_norm).astype(jnp.bfloat16)
    grad_out = jnp.einsum("nd,ne->de", attended_low, d_middle, preferred_element_type=jnp.float32)
    d_attended = jnp.einsum(
        "ne,de->nd", d_middle, w_out, preferred_element_type=jnp.float32
    ).astype(jnp.bfloat16)
    row_delta = jnp.sum(
        (d_attended.astype(jnp.float32) * attended).reshape(local_rows, HEADS, HEAD_DIM), axis=-1
    ).T
    zero_rows = jnp.zeros((local_rows, width), jnp.float32)

    def attend_back(cycle_turn, cycle_state):
        held_keys, held_values, held_dk, held_dv, d_query = cycle_state
        source = (cycle_place - cycle_turn) % cycle_count

        def attend_visit_pair(pair_index, partial_value):
            row_block = pair_index // local_blocks
            col_block = pair_index % local_blocks
            query_block = first_block + row_block
            key_block = source * local_blocks + col_block

            def attend_update_tile(partial_value):
                dk_acc, dv_acc, dq_acc = partial_value
                query_tile = rows_of(query_rows, row_block)
                key_tile = rows_of(held_keys, col_block)
                grad_tile = rows_of(d_attended, row_block)
                allowed = pair_mask(seg_row, off_row, query_block, key_block)
                probs_low, d_scores = tile_back(
                    query_tile,
                    key_tile,
                    rows_of(held_values, col_block),
                    grad_tile,
                    cols_of(log_norm, row_block),
                    cols_of(row_delta, row_block),
                    allowed,
                )
                dq_acc = add_rows(dq_acc, query_grad(d_scores, key_tile), row_block)
                dk_acc = add_rows(dk_acc, key_grad(d_scores, query_tile), col_block)
                dv_acc = add_rows(dv_acc, value_grad(probs_low, grad_tile), col_block)
                return (dk_acc, dv_acc, dq_acc)

            return lax.cond(
                pair_live(seg_row, off_row, query_block, key_block),
                attend_update_tile,
                unchanged,
                partial_value,
            )

        held_dk, held_dv, d_query = lax.fori_loop(
            0, local_blocks * local_blocks, attend_visit_pair, (held_dk, held_dv, d_query)
        )
        return (held_keys, held_values, held_dk, held_dv, d_query)

    def pass_grads(held_dk, held_dv):
        return (
            passed_along(held_dk.astype(jnp.bfloat16), "ctx", 1).astype(held_dk.dtype),
            passed_along(held_dv.astype(jnp.bfloat16), "ctx", 1).astype(held_dv.dtype),
        )

    def turn_step(cycle_turn, cycle_state):
        held_keys, held_values, held_dk, held_dv, d_query = attend_back(cycle_turn, cycle_state)
        held_keys, held_values = passed_along((held_keys, held_values), "ctx", 1)
        held_dk, held_dv = pass_grads(held_dk, held_dv)
        return (held_keys, held_values, held_dk, held_dv, d_query)

    cycle_state = lax.fori_loop(
        0, cycle_count - 1, turn_step, (key_rows, value_rows, zero_rows, zero_rows, zero_rows)
    )
    cycle_state = attend_back(cycle_count - 1, cycle_state)
    d_keys, d_values = pass_grads(cycle_state[2], cycle_state[3])
    d_query = cycle_state[4]
    d_qkv = jnp.concatenate(
        [d_query.astype(jnp.bfloat16), d_keys.astype(jnp.bfloat16), d_values.astype(jnp.bfloat16)],
        axis=1,
    )
    grad_qkv = jnp.einsum("nd,nf->df", act1, d_qkv, preferred_element_type=jnp.float32)
    d_act1 = jnp.einsum("nf,df->nd", d_qkv, w_qkv, preferred_element_type=jnp.float32)
    d_inputs_norm, grad_gain1, grad_shift1 = pull_norm1(d_act1)
    words_grad = d_middle.astype(jnp.float32) + d_inputs_norm
    shards = (
        lax.psum_scatter(
            grad_qkv.astype(jnp.bfloat16), "wshard", scatter_dimension=0, tiled=True
        ).astype(jnp.float32),
        lax.psum_scatter(
            grad_out.astype(jnp.bfloat16), "wshard", scatter_dimension=0, tiled=True
        ).astype(jnp.float32),
        lax.psum_scatter(
            grad_up.astype(jnp.bfloat16), "wshard", scatter_dimension=0, tiled=True
        ).astype(jnp.float32),
        lax.psum_scatter(
            grad_down.astype(jnp.bfloat16), "wshard", scatter_dimension=0, tiled=True
        ).astype(jnp.float32),
        lax.psum_scatter(
            grad_gain1.astype(jnp.bfloat16), "wshard", scatter_dimension=0, tiled=True
        ).astype(jnp.float32),
        lax.psum_scatter(
            grad_shift1.astype(jnp.bfloat16), "wshard", scatter_dimension=0, tiled=True
        ).astype(jnp.float32),
        lax.psum_scatter(
            grad_gain2.astype(jnp.bfloat16), "wshard", scatter_dimension=0, tiled=True
        ).astype(jnp.float32),
        lax.psum_scatter(
            grad_shift2.astype(jnp.bfloat16), "wshard", scatter_dimension=0, tiled=True
        ).astype(jnp.float32),
        lax.psum_scatter(
            grad_bias_up.astype(jnp.bfloat16), "wshard", scatter_dimension=0, tiled=True
        ).astype(jnp.float32),
        lax.psum_scatter(
            grad_bias_down.astype(jnp.bfloat16), "wshard", scatter_dimension=0, tiled=True
        ).astype(jnp.float32),
    )
    totals = lax.psum(
        (
            shards[0],
            shards[1],
            shards[2],
            shards[3],
            shards[4],
            shards[5],
            shards[6],
            shards[7],
            shards[8],
            shards[9],
        ),
        ("group", "ctx"),
    )
    return (
        output[None],
        words_grad[None],
        totals[0],
        totals[1],
        totals[2],
        totals[3],
        totals[4],
        totals[5],
        totals[6],
        totals[7],
        totals[8],
        totals[9],
    )


def solution(mesh):
    return jax.shard_map(
        on_device,
        mesh=mesh,
        in_specs=(
            P(("group", "wshard"), "ctx", None),
            P("wshard", None),
            P("wshard", None),
            P("wshard", None),
            P("wshard", None),
            P("wshard"),
            P("wshard"),
            P("wshard"),
            P("wshard"),
            P("wshard"),
            P("wshard"),
            P(("group", "wshard"), "ctx", None),
            P(("group", "wshard"), None),
            P(("group", "wshard"), None),
        ),
        out_specs=(
            P(("group", "wshard"), "ctx", None),
            P(("group", "wshard"), "ctx", None),
            P("wshard", None),
            P("wshard", None),
            P("wshard", None),
            P("wshard", None),
            P("wshard"),
            P("wshard"),
            P("wshard"),
            P("wshard"),
            P("wshard"),
            P("wshard"),
        ),
        check_vma=False,
    )
```

profile of v0, /device:TPU:0, one launch (start us, length us, event | category | flops | bytes accessed | tf_op | source)
XLA Modules:
  0.0 759.4 jit_solution(17969878101253650071)
XLA Ops:
  8.0 6.2 all-gather
  14.1 5.4 all-gather.1
  22.2 9.8 %all-gather.12.cloned.1.call-done = bf16[512,1536]{1,0:T(8,128)(2,1)} async-done(((bf16[128,1536]{1,0:T(8,128)(2,1)}), bf16[512,1536]{1,0:T(8,128)(2,1)}) %all-gather.12.cloned.1.call-update) | async-done | bytes 1572880 | tf_op jit(solution)/shard_map/all_gather | solution.py:144
  55.6 8.2 %all_gather.41 = bf16[512,512]{1,0:T(8,128)(2,1)} all-gather(bf16[128,512]{1,0:T(8,128)(2,1)S(1)} %copy-done.34), channel_id=1, replica_groups=mesh['group'=4,'ctx'=2,'wshard'=4] {'wshard'}, dimensions={0}, use_global_device_ids=true | all-gather | bytes 655360 | tf_op jit(solution)/shard_map/all_gather | solution.py:145
  64.3 6.0 all-gather.16.cloned.1.call-done
  74.2 31.3 %all-gather.14.cloned.1.call-done = bf16[2048,512]{1,0:T(8,128)(2,1)} async-done(((bf16[1024,512]{1,0:T(8,128)(2,1)}), bf16[2048,512]{1,0:T(8,128)(2,1)}) %all-gather.14.cloned.1.call-update) | async-done | bytes 2097168 | tf_op jit(solution)/shard_map/all_gather | solution.py:182
  110.1 108.6 %while.71 = (s32[]{:T(128)}, f32[8,1024]{1,0:T(8,128)S(1)}, f32[8,1024]{1,0:T(8,128)S(1)}, f32[1024,512]{0,1:T(8,128)S(1)}, s32[]{:T(128)}, /*index=5*/s32[4]{0:...) while((s32[]{:T(128)}, f32[8,1024]{1,0:T(8,128)S(1)}, ...), condition=%wide.region_7.8_spmd, body=%wide.region_2.7_spmd.sunk | while | flops 565457920 | bytes 37479280 | solution.py:225
  114.5 12.2 %conditional.6 = ((f32[8,1024]{1,0:T(8,128)S(1)}, f32[8,1024]{1,0:T(8,128)S(1)}, f32[1024,512]{0,1:T(8,128)S(1)})) conditional(s32[]{:T(128)} %bitcast.172, (f32[8,1024]{1,0:T(8,128)S(1)}, f32[8,1024]{1,0:T(8,128)S(1)}, f32[1024,512]{0,1:T(8,128)S(1)}) %tuple.180, (s32[]{:T(128)}, f32[8,1024]{1,0:T(8,128)S(1)}, s32[]{:T(128)}, s32[4]{0:T(128)S(1)}, ...), branch_computations={%region_3.3_spmd, %region_4.6_spmd} | conditional | flops 565457920 | bytes 37478720 | solution.py:218
  140.0 12.2 %conditional.6 = ((f32[8,1024]{1,0:T(8,128)S(1)}, f32[8,1024]{1,0:T(8,128)S(1)}, f32[1024,512]{0,1:T(8,128)S(1)})) conditional(s32[]{:T(128)} %bitcast.172, (f32[8,1024]{1,0:T(8,128)S(1)}, f32[8,1024]{1,0:T(8,128)S(1)}, f32[1024,512]{0,1:T(8,128)S(1)}) %tuple.180, (s32[]{:T(128)}, f32[8,1024]{1,0:T(8,128)S(1)}, s32[]{:T(128)}, s32[4]{0:T(128)S(1)}, ...), branch_computations={%region_3.3_spmd, %region_4.6_spmd} | conditional | flops 565457920 | bytes 37478720 | solution.py:218
  156.6 12.2 %conditional.6 = ((f32[8,1024]{1,0:T(8,128)S(1)}, f32[8,1024]{1,0:T(8,128)S(1)}, f32[1024,512]{0,1:T(8,128)S(1)})) conditional(s32[]{:T(128)} %bitcast.172, (f32[8,1024]{1,0:T(8,128)S(1)}, f32[8,1024]{1,0:T(8,128)S(1)}, f32[1024,512]{0,1:T(8,128)S(1)}) %tuple.180, (s32[]{:T(128)}, f32[8,1024]{1,0:T(8,128)S(1)}, s32[]{:T(128)}, s32[4]{0:T(128)S(1)}, ...), branch_computations={%region_3.3_spmd, %region_4.6_spmd} | conditional | flops 565457920 | bytes 37478720 | solution.py:218
  173.2 12.2 %conditional.6 = ((f32[8,1024]{1,0:T(8,128)S(1)}, f32[8,1024]{1,0:T(8,128)S(1)}, f32[1024,512]{0,1:T(8,128)S(1)})) conditional(s32[]{:T(128)} %bitcast.172, (f32[8,1024]{1,0:T(8,128)S(1)}, f32[8,1024]{1,0:T(8,128)S(1)}, f32[1024,512]{0,1:T(8,128)S(1)}) %tuple.180, (s32[]{:T(128)}, f32[8,1024]{1,0:T(8,128)S(1)}, s32[]{:T(128)}, s32[4]{0:T(128)S(1)}, ...), branch_computations={%region_3.3_spmd, %region_4.6_spmd} | conditional | flops 565457920 | bytes 37478720 | solution.py:218
  189.9 12.2 %conditional.6 = ((f32[8,1024]{1,0:T(8,128)S(1)}, f32[8,1024]{1,0:T(8,128)S(1)}, f32[1024,512]{0,1:T(8,128)S(1)})) conditional(s32[]{:T(128)} %bitcast.172, (f32[8,1024]{1,0:T(8,128)S(1)}, f32[8,1024]{1,0:T(8,128)S(1)}, f32[1024,512]{0,1:T(8,128)S(1)}) %tuple.180, (s32[]{:T(128)}, f32[8,1024]{1,0:T(8,128)S(1)}, s32[]{:T(128)}, s32[4]{0:T(128)S(1)}, ...), branch_computations={%region_3.3_spmd, %region_4.6_spmd} | conditional | flops 565457920 | bytes 37478720 | solution.py:218
  206.5 12.2 %conditional.6 = ((f32[8,1024]{1,0:T(8,128)S(1)}, f32[8,1024]{1,0:T(8,128)S(1)}, f32[1024,512]{0,1:T(8,128)S(1)})) conditional(s32[]{:T(128)} %bitcast.172, (f32[8,1024]{1,0:T(8,128)S(1)}, f32[8,1024]{1,0:T(8,128)S(1)}, f32[1024,512]{0,1:T(8,128)S(1)}) %tuple.180, (s32[]{:T(128)}, f32[8,1024]{1,0:T(8,128)S(1)}, s32[]{:T(128)}, s32[4]{0:T(128)S(1)}, ...), branch_computations={%region_3.3_spmd, %region_4.6_spmd} | conditional | flops 565457920 | bytes 37478720 | solution.py:218
  222.7 11.4 %multiply_convert_fusion.2 = (bf16[1024,2048]{1,0:T(8,128)(2,1)}, f32[1024,2048]{1,0:T(8,128)}) fusion(f32[2048]{0:T(1024)S(1)} %bitcast.209, bf16[512,2048]{1,0:T(8,128)(2,1)} %all-gather.18.cloned.1.call-done, f32[1024,512]{0,1:T(8,128)} %copy-done, f32[512]{0:T(512)S(1)} %bitcast.213, f32[512]{0:T(512)S(1)} %bitcast.199, f32[1024]{0:T(1024)S(1)} %fusion.57, ...), kind=kOutput, calls=%fused_computation.84 | convolution fusion | flops 2171076608 | bytes 16797696 | tf_op jit(solution)/shard_map/dot_general | solution.py:236
  234.2 11.0 %fusion.80 = (bf16[2048]{0:T(1024)(128)(2,1)}, bf16[1024,2048]{1,0:T(8,128)(2,1)S(1)}) fusion(f32[1024,2048]{1,0:T(8,128)} %get-tuple-element.1444, f32[2048]{0:T(1024)S(1)} %bitcast.210, bf16[2048,512]{1,0:T(8,128)(2,1)} %all-gather.20.cloned.1.call-done, bf16[1,1024,512]{2,1,0:T(8,128)(2,1)} %param.37), kind=kOutput, calls=%fused_computation.162 | convolution fusion | flops 2193618944 | bytes 15740928 | tf_op jit(solution)/shard_map/nd,fd->nf/dot_general | solution.py:246
  260.7 6.2 convolution_convert_fusion.1
  267.2 6.6 convolution_convert_fusion.2
  287.2 83.1 %while.72 = (s32[]{:T(128)}, f32[1024,512]{0,1:T(8,128)}, f32[1024,512]{0,1:T(8,128)}, f32[1024,512]{0,1:T(8,128)S(1)}, s32[]{:T(128)}, /*index=5*/s32[4]{0:T(12...) while((s32[]{:T(128)}, f32[1024,512]{0,1:T(8,128)}, ...), condition=%wide.region_16.17_spmd, body=%wide.region_13.16_spmd.sunk | while | flops 1369441280 | bytes 101049456 | solution.py:299
  291.6 21.7 %conditional.7 = ((f32[1024,512]{0,1:T(8,128)}, f32[1024,512]{0,1:T(8,128)}, f32[1024,512]{0,1:T(8,128)S(1)})) conditional(s32[]{:T(128)} %bitcast.173, (f32[1024,512]{0,1:T(8,128)}, f32[1024,512]{0,1:T(8,128)}, f32[1024,512]{0,1:T(8,128)S(1)}) %tuple.184, (s32[]{:T(128)}, f32[1024,512]{0,1:T(8,128)}, s32[]{:T(128)}, ...), branch_computations={%region_14.14_spmd, %region_15.15_spmd} | conditional | flops 1369441280 | bytes 101048824 | solution.py:292
  322.2 22.0 %conditional.7 = ((f32[1024,512]{0,1:T(8,128)}, f32[1024,512]{0,1:T(8,128)}, f32[1024,512]{0,1:T(8,128)S(1)})) conditional(s32[]{:T(128)} %bitcast.173, (f32[1024,512]{0,1:T(8,128)}, f32[1024,512]{0,1:T(8,128)}, f32[1024,512]{0,1:T(8,128)S(1)}) %tuple.184, (s32[]{:T(128)}, f32[1024,512]{0,1:T(8,128)}, s32[]{:T(128)}, ...), branch_computations={%region_14.14_spmd, %region_15.15_spmd} | conditional | flops 1369441280 | bytes 101048824 | solution.py:292
  348.6 21.7 %conditional.7 = ((f32[1024,512]{0,1:T(8,128)}, f32[1024,512]{0,1:T(8,128)}, f32[1024,512]{0,1:T(8,128)S(1)})) conditional(s32[]{:T(128)} %bitcast.173, (f32[1024,512]{0,1:T(8,128)}, f32[1024,512]{0,1:T(8,128)}, f32[1024,512]{0,1:T(8,128)S(1)}) %tuple.184, (s32[]{:T(128)}, f32[1024,512]{0,1:T(8,128)}, s32[]{:T(128)}, ...), branch_computations={%region_14.14_spmd, %region_15.15_spmd} | conditional | flops 1369441280 | bytes 101048824 | solution.py:292
  381.0 9.1 %collective-permute-done.1 = bf16[1024,512]{0,1:T(8,128)(2,1)} collective-permute-done((bf16[1024,512]{0,1:T(8,128)(2,1)}, bf16[1024,512]{0,1:T(8,128)(2,1)}, u32[]{:S(2)}, u32[]{:S(2)}) %collective-permute-start.1) | collective-permute-done | bytes 1048608 | tf_op jit(solution)/shard_map/while/body/eval_jaxpr/ppermute | solution.py:17
  392.9 19.6 %collective-permute-done = bf16[1024,512]{0,1:T(8,128)(2,1)} collective-permute-done((bf16[1024,512]{0,1:T(8,128)(2,1)}, bf16[1024,512]{0,1:T(8,128)(2,1)}, u32[]{:S(2)}, u32[]{:S(2)}) %collective-permute-start) | collective-permute-done | bytes 1048608 | tf_op jit(solution)/shard_map/while/body/eval_jaxpr/ppermute | solution.py:17
  415.4 82.8 %while.73 = (s32[]{:T(128)}, f32[1024,512]{0,1:T(8,128)}, f32[1024,512]{0,1:T(8,128)}, f32[1024,512]{0,1:T(8,128)S(1)}, s32[]{:T(128)}, /*index=5*/s32[4]{0:T(12...) while((s32[]{:T(128)}, f32[1024,512]{0,1:T(8,128)}, ...), condition=%wide.region_20.21_spmd, body=%wide.region_17.20_spmd.sunk | while | flops 1369441280 | bytes 101049456 | solution.py:299
  424.7 21.6 %conditional.8 = ((f32[1024,512]{0,1:T(8,128)}, f32[1024,512]{0,1:T(8,128)}, f32[1024,512]{0,1:T(8,128)S(1)})) conditional(s32[]{:T(128)} %bitcast.174, (f32[1024,512]{0,1:T(8,128)}, f32[1024,512]{0,1:T(8,128)}, f32[1024,512]{0,1:T(8,128)S(1)}) %tuple.188, (s32[]{:T(128)}, f32[1024,512]{0,1:T(8,128)}, s32[]{:T(128)}, ...), branch_computations={%region_18.18_spmd, %region_19.19_spmd} | conditional | flops 1369441280 | bytes 101048824 | solution.py:292
  450.7 21.6 %conditional.8 = ((f32[1024,512]{0,1:T(8,128)}, f32[1024,512]{0,1:T(8,128)}, f32[1024,512]{0,1:T(8,128)S(1)})) conditional(s32[]{:T(128)} %bitcast.174, (f32[1024,512]{0,1:T(8,128)}, f32[1024,512]{0,1:T(8,128)}, f32[1024,512]{0,1:T(8,128)S(1)}) %tuple.188, (s32[]{:T(128)}, f32[1024,512]{0,1:T(8,128)}, s32[]{:T(128)}, ...), branch_computations={%region_18.18_spmd, %region_19.19_spmd} | conditional | flops 1369441280 | bytes 101048824 | solution.py:292
  476.6 21.6 %conditional.8 = ((f32[1024,512]{0,1:T(8,128)}, f32[1024,512]{0,1:T(8,128)}, f32[1024,512]{0,1:T(8,128)S(1)})) conditional(s32[]{:T(128)} %bitcast.174, (f32[1024,512]{0,1:T(8,128)}, f32[1024,512]{0,1:T(8,128)}, f32[1024,512]{0,1:T(8,128)S(1)}) %tuple.188, (s32[]{:T(128)}, f32[1024,512]{0,1:T(8,128)}, s32[]{:T(128)}, ...), branch_computations={%region_18.18_spmd, %region_19.19_spmd} | conditional | flops 1369441280 | bytes 101048824 | solution.py:292
  506.4 33.5 %all-gather.5 = bf16[4,1,128]{2,1,0:T(2,128)(2,1)S(1)} all-gather(bf16[1,1,128]{2,1,0:T(2,128)(2,1)S(1)} %bitcast.220), channel_id=1, replica_groups=mesh['group'=4,'ctx'=2,'wshard'=4] {'wshard'}, dimensions={0}, use_global_device_ids=true | all-gather | bytes 1280 | tf_op jit(solution)/shard_map/all_gather | solution.py:153
  545.8 5.2 fusion.50
  566.8 22.8 %all-reduce.7 = (bf16[512]{0:T(512)(128)(2,1)S(1)}, bf16[512]{0:T(512)(128)(2,1)S(1)}, bf16[512]{0:T(512)(128)(2,1)S(1)}, bf16[512]{0:T(512)(128)(2,1)S(1)}, bf1...) all-reduce(bf16[512]{0:T(512)(128)(2,1)S(1)} %get-tuple-element.130, ...), channel_id=6, replica_groups=mesh['group'=4,'ctx'=2,'wshard'=4] {'wshard'}, use_global_device_ids=true, to_apply=%region_32.33.clone | all-reduce | flops 4608 | bytes 18432
  589.9 32.8 %reduce-scatter.5.cloned.1.call-done = bf16[128,1536]{1,0:T(8,128)(2,1)} async-done(((bf16[512,1536]{1,0:T(8,128)(2,1)}), bf16[128,1536]{1,0:T(8,128)(2,1)}) %reduce-scatter.5.cloned.1.call-update) | async-done | bytes 393232 | tf_op jit(solution)/shard_map/reduce_scatter | solution.py:331
  622.6 130.1 %all-reduce.9 = (f32[128,1536]{1,0:T(8,128)}, f32[128,512]{1,0:T(8,128)}, f32[128,2048]{1,0:T(8,128)}, f32[512,512]{1,0:T(8,128)}, f32[128]{0:T(128)}, /*index=5...) all-reduce(bf16[128,1536]{1,0:T(8,128)(2,1)} %reduce-scatter.5.clon, ...), channel_id=1, replica_groups=mesh['group'=4,'ctx'=2,'wshard'=4] {'group','ctx'}, use_global_device_ids=true, to_apply=%region_24.25 | all-reduce | flops 787584 | bytes 4727808 | tf_op jit(solution)/shard_map/psum | solution.py:362
  (468 shorter events, 280.7 us)
Async XLA Ops:
  7.2 24.8 %all-gather.12.cloned.1.call-start = ((), (), s32[]{:S(2)}) async-start(), calls=%async_computation.4 | async-start | bytes 1966080 | tf_op jit(solution)/shard_map/all_gather | solution.py:144
  7.9 62.4 %all-gather.16.cloned.1.call-start = ((), (), s32[]{:S(2)}) async-start(), calls=%async_computation.6 | async-start | bytes 3145728 | tf_op jit(solution)/shard_map/all_gather | solution.py:183
  14.1 17.8 %copy-start.42 = (f32[4,1,128]{2,1,0:T(1,128)}, f32[4,1,128]{2,1,0:T(1,128)S(1)}, u32[]{:S(2)}) copy-start(f32[4,1,128]{2,1,0:T(1,128)S(1)} %convert_element_type.247) | copy-start | bytes 6148
  19.5 12.4 %copy-start.46 = (f32[4,1,128]{2,1,0:T(1,128)}, f32[4,1,128]{2,1,0:T(1,128)S(1)}, u32[]{:S(2)}) copy-start(f32[4,1,128]{2,1,0:T(1,128)S(1)} %convert_element_type.248) | copy-start | bytes 6148
  21.1 14.3 %copy-start.3 = (bf16[1,1024,512]{1,2,0:T(8,128)(2,1)}, bf16[1,1024,512]{1,2,0:T(8,128)(2,1)S(1)}, u32[]{:S(2)}) copy-start(bf16[1,1024,512]{1,2,0:T(8,128)(2,1)S(1)} %copy.46) | copy-start | bytes 3145732
  21.3 10.7 %copy-start.36 = (f32[1024]{0:T(1024)}, f32[1024]{0:T(1024)S(1)}, u32[]{:S(2)}) copy-start(f32[1024]{0:T(1024)S(1)} %broadcast_multiply_fusion.1) | copy-start | bytes 12292
  22.2 9.8 %copy-start.40 = (f32[1024]{0:T(1024)}, f32[1024]{0:T(1024)S(1)}, u32[]{:S(2)}) copy-start(f32[1024]{0:T(1024)S(1)} %fusion.56) | copy-start | bytes 12292
  37.0 7.0 copy-start.51
  37.0 12.1 %copy-start.48 = (bf16[512]{0:T(512)(128)(2,1)S(1)}, bf16[512]{0:T(512)(128)(2,1)}, u32[]{:S(2)}) copy-start(bf16[512]{0:T(512)(128)(2,1)} %param.35) | copy-start | bytes 3076
  37.0 17.3 %copy-start.25 = (bf16[1,1024,512]{2,1,0:T(8,128)(2,1)S(1)}, bf16[1,1024,512]{2,1,0:T(8,128)(2,1)}, u32[]{:S(2)}) copy-start(bf16[1,1024,512]{2,1,0:T(8,128)(2,1)} %param.37) | copy-start | bytes 3145732
  37.0 68.5 %all-gather.14.cloned.1.call-start = ((), (), s32[]{:S(2)}) async-start(), calls=%async_computation.5 | async-start | bytes 3145728 | tf_op jit(solution)/shard_map/all_gather | solution.py:182
  37.1 18.5 %copy-start.34 = (bf16[128,512]{1,0:T(8,128)(2,1)S(1)}, bf16[128,512]{1,0:T(8,128)(2,1)}, u32[]{:S(2)}) copy-start(bf16[128,512]{1,0:T(8,128)(2,1)} %param.28) | copy-start | bytes 393220
  37.7 185.0 %all-gather.18.cloned.1.call-start = ((), (), s32[]{:S(2)}) async-start(), calls=%async_computation.7 | async-start | bytes 2621440 | tf_op jit(solution)/shard_map/all_gather | solution.py:146
  38.3 195.8 %all-gather.20.cloned.1.call-start = ((), (), s32[]{:S(2)}) async-start(), calls=%async_computation.8 | async-start | bytes 2621440 | tf_op jit(solution)/shard_map/all_gather | solution.py:147
  38.9 513.6 %reduce-scatter.7.cloned.1.call-start = ((), (), s32[]{:S(2)}) async-start(), calls=%async_computation.10 | async-start | bytes 655360 | tf_op jit(solution)/shard_map/reduce_scatter | solution.py:334
  234.2 11.0 %copy-start.53 = (bf16[512,2048]{1,0:T(8,128)(2,1)S(1)}, bf16[512,2048]{1,0:T(8,128)(2,1)}, u32[]{:S(2)}) copy-start(bf16[512,2048]{1,0:T(8,128)(2,1)} %all-gather.18.cloned.1.call-done) | copy-start | bytes 6291460
  260.7 329.2 %reduce-scatter.11.cloned.1.call-start = ((), (), s32[]{:S(2)}) async-start(), calls=%async_computation.12 | async-start | bytes 2621440 | tf_op jit(solution)/shard_map/reduce_scatter | solution.py:340
  267.0 322.9 %reduce-scatter.9.cloned.1.call-start = ((), (), s32[]{:S(2)}) async-start(), calls=%async_computation.11 | async-start | bytes 2621440 | tf_op jit(solution)/shard_map/reduce_scatter | solution.py:337
  273.9 348.7 %reduce-scatter.5.cloned.1.call-start = ((), (), s32[]{:S(2)}) async-start(), calls=%async_computation.9 | async-start | bytes 1966080 | tf_op jit(solution)/shard_map/reduce_scatter | solution.py:331
  278.5 97.9 %collective-permute-start.3 = (bf16[1024,512]{1,0:T(8,128)(2,1)}, bf16[1024,512]{1,0:T(8,128)(2,1)}, u32[]{:S(2)}, u32[]{:S(2)}) collective-permute-start(bf16[1024,512]{1,0:T(8,128)(2,1)} %get-tuple-element.1438), channel_id=1, source_target_pairs={{0,4},{4,0},{1,5},{5,1},{2,6},{6,2},{3,7},{7,3},{8,12},{12,8},{9,1... | collective-permute-start | bytes 3145736 | tf_op jit(solution)/shard_map/while/body/eval_jaxpr/ppermute | solution.py:17
  278.5 100.2 %collective-permute-start.2 = (bf16[1024,512]{1,0:T(8,128)(2,1)}, bf16[1024,512]{1,0:T(8,128)(2,1)}, u32[]{:S(2)}, u32[]{:S(2)}) collective-permute-start(bf16[1024,512]{1,0:T(8,128)(2,1)} %get-tuple-element.1439), channel_id=1, source_target_pairs={{0,4},{4,0},{1,5},{5,1},{2,6},{6,2},{3,7},{7,3},{8,12},{12,8},{9,1... | collective-permute-start | bytes 3145736 | tf_op jit(solution)/shard_map/while/body/eval_jaxpr/ppermute | solution.py:17
  348.7 6.8 copy-start.21
  373.2 16.8 %collective-permute-start.1 = (bf16[1024,512]{0,1:T(8,128)(2,1)}, bf16[1024,512]{0,1:T(8,128)(2,1)}, u32[]{:S(2)}, u32[]{:S(2)}) collective-permute-start(bf16[1024,512]{0,1:T(8,128)(2,1)} %convert_element_type.221), channel_id=1, source_target_pairs={{0,4},{4,0},{1,5},{5,1},{2,6},{6,2},{3,7},{7,3},{8,12},{12,8},{9,1... | collective-permute-start | bytes 3145736 | tf_op jit(solution)/shard_map/while/body/eval_jaxpr/ppermute | solution.py:17
  374.4 38.1 %collective-permute-start = (bf16[1024,512]{0,1:T(8,128)(2,1)}, bf16[1024,512]{0,1:T(8,128)(2,1)}, u32[]{:S(2)}, u32[]{:S(2)}) collective-permute-start(bf16[1024,512]{0,1:T(8,128)(2,1)} %convert_element_type.219), channel_id=1, source_target_pairs={{0,4},{4,0},{1,5},{5,1},{2,6},{6,2},{3,7},{7,3},{8,12},{12,8},{9,1... | collective-permute-start | bytes 3145736 | tf_op jit(solution)/shard_map/while/body/eval_jaxpr/ppermute | solution.py:17
  502.2 37.9 %collective-permute-start.5 = (bf16[1024,512]{0,1:T(8,128)(2,1)}, bf16[1024,512]{0,1:T(8,128)(2,1)}, u32[]{:S(2)}, u32[]{:S(2)}) collective-permute-start(bf16[1024,512]{0,1:T(8,128)(2,1)} %convert_element_type.225), channel_id=1, source_target_pairs={{0,4},{4,0},{1,5},{5,1},{2,6},{6,2},{3,7},{7,3},{8,12},{12,8},{9,1... | collective-permute-start | bytes 3145736 | tf_op jit(solution)/shard_map/ppermute | solution.py:17
  502.2 37.9 %collective-permute-start.4 = (bf16[1024,512]{0,1:T(8,128)(2,1)}, bf16[1024,512]{0,1:T(8,128)(2,1)}, u32[]{:S(2)}, u32[]{:S(2)}) collective-permute-start(bf16[1024,512]{0,1:T(8,128)(2,1)} %convert_element_type.224), channel_id=1, source_target_pairs={{0,4},{4,0},{1,5},{5,1},{2,6},{6,2},{3,7},{7,3},{8,12},{12,8},{9,1... | collective-permute-start | bytes 3145736 | tf_op jit(solution)/shard_map/ppermute | solution.py:17
  506.1 34.9 %copy-start.37 = (f32[1024]{0:T(1024)S(1)}, f32[1024]{0:T(1024)}, u32[]{:S(2)}) copy-start(f32[1024]{0:T(1024)} %copy-done.36) | copy-start | bytes 12292
  506.1 34.9 %copy-start.41 = (f32[1024]{0:T(1024)S(1)}, f32[1024]{0:T(1024)}, u32[]{:S(2)}) copy-start(f32[1024]{0:T(1024)} %copy-done.40) | copy-start | bytes 12292
  506.2 34.9 %copy-start.43 = (f32[4,1,128]{2,1,0:T(1,128)S(1)}, f32[4,1,128]{2,1,0:T(1,128)}, u32[]{:S(2)}) copy-start(f32[4,1,128]{2,1,0:T(1,128)} %copy-done.42) | copy-start | bytes 6148
  506.2 34.9 %copy-start.47 = (f32[4,1,128]{2,1,0:T(1,128)S(1)}, f32[4,1,128]{2,1,0:T(1,128)}, u32[]{:S(2)}) copy-start(f32[4,1,128]{2,1,0:T(1,128)} %copy-done.46) | copy-start | bytes 6148
  506.4 34.7 %copy-start.5 = (bf16[1,1024,512]{1,2,0:T(8,128)(2,1)S(1)}, bf16[1,1024,512]{1,2,0:T(8,128)(2,1)}, u32[]{:S(2)}) copy-start(bf16[1,1024,512]{1,2,0:T(8,128)(2,1)} %copy-done.3) | copy-start | bytes 3145732
  563.8 58.8 %copy-start.35 = (bf16[128,512]{1,0:T(8,128)(2,1)S(1)}, bf16[128,512]{1,0:T(8,128)(2,1)}, u32[]{:S(2)}) copy-start(bf16[128,512]{1,0:T(8,128)(2,1)} %reduce-scatter.7.cloned.1.call-done) | copy-start | bytes 393220
  (63 other events, 173.5 us)
Sparse Core Ops, SparseCore 0:
  9.6 22.3 all-gather.11
  37.1 33.0 all-gather.15
  72.4 33.1 all-gather.13
  107.0 22.5 all-gather.17
  131.0 22.6 all-gather.19
  260.8 33.8 reduce-scatter.6
  297.4 31.4 reduce-scatter.10
  331.5 31.4 reduce-scatter.8
  545.9 76.6 reduce-scatter.4
where the time goes:
time: 767 us; the launch traced here: 759 us
  blocking collectives  221 us (29%)
  matrix products  144 us (19%)
  waiting for transfers between devices  111 us (14%)
  loops' own time  108 us (14%)
  local copies, waits for them, and re-layouts  107 us (14%)
  other arithmetic  45 us (6%)
  between operations  15.8 us (2%)
    psum x1, blocking collectives, on_device(): lax.psum((shards[0], shards[1], shards[2], shards[3], shards[4], shards[5...  130 us
    all_gather x1, blocking collectives, on_device(): lax.all_gather(down_bias, 'wshard', axis=0, tiled=True)  33.5 us
    reduce_scatter x1, waiting for transfers between devices, on_device(): lax.psum_scatter(grad_qkv.astype(jnp.bfloat16), 'wshard', scatter_dimensi...  32.8 us
    all_gather x1, waiting for transfers between devices, on_device(): shard_keys = lax.all_gather(key_rows, 'ctx', axis=0, tiled=True)  31.3 us
    another operation x2, loops' own time, attend_back(): lax.fori_loop(0, local_blocks * local_blocks, attend_visit_pair, (held_dk...  30.6 us
    another operation x1, loops' own time, on_device(): lax.fori_loop(0, local_blocks * key_blocks, online_visit_pair, start_state)  29.9 us
    ppermute x6, waiting for transfers between devices, passed_along(): lax.ppermute(value, axis, [(i, (i + by) % peers) for i in range(peers)])  28.8 us
    cond x72, local copies, waits for them, and re-layouts  25.7 us
  transfers between devices with their start and end apart: 15, of which 6 were waited for; matrix products, arithmetic and copies ran while one was open for 31% of the time, Pallas kernels for 0%

commit v1 on v0

--- a/solution.py
+++ b/solution.py
@@ -1,11 +1,660 @@
+import functools
 import jax
 import jax.numpy as jnp
 from jax import lax
+from jax.experimental import pallas as pl
+from jax.experimental.pallas import tpu as pltpu
 from jax.sharding import PartitionSpec as P
+
+BLK = 512
+HD = 64
+EPS = 1e-5
+F32 = jnp.float32
+BF16 = jnp.bfloat16
+K0 = 0.7978845608
+K1 = 0.044715
+LIVE = ((0,), (0, 1), (0, 1, 2), (0, 1, 2, 3))
+MESH = pl.DeviceIdType.MESH
+VLIM = 63 * 1024 * 1024
+CHUNKS = (1024, 1024, 1024, 1024, 512, 768, 768)
+STARTS = (0, 1024, 2048, 3072, 4096, 4608, 5376)
+ROWS = 6144
+
+
+def dg(a, b, ca, cb):
+    return lax.dot_general(a, b, (((ca,), (cb,)), ((), ())), preferred_element_type=F32)
+
+
+def colsum(v):
+    return jnp.sum(v, axis=0, keepdims=True)
+
+
+def rowmean(v):
+    return jnp.mean(v, axis=-1, keepdims=True)
+
+
+def tri(n):
+    k = lax.broadcasted_iota(jnp.int32, (n, n), 0)
+    q = lax.broadcasted_iota(jnp.int32, (n, n), 1)
+    return k <= q
+
+
+def al(v, n):
+    return pl.multiple_of(v, n)
+
+
+def scratch(nz):
+    ne = 2 * nz
+    V = lambda *s, t=BF16: pltpu.VMEM(s, t)
+    d = dict(
+        xs=V(1024, 512), dys=V(1024, 512), wt=V(1536, 512), wo=V(512, 512), wu=V(4, 512, 512), wd=V(4, 512, 512),
+        vec=V(4, 16, 128, t=F32), so=V(2, 8, 128, t=jnp.int32), sm=pltpu.SMEM((8, 128), jnp.int32),
+        a1=V(1024, 512), qkv=V(4, 768, 512), qst=V(4, 768, 256), o=V(4, 256, 512, t=F32), lse=V(4, 8, 512, t=F32),
+        ost=V(2, 256, 512), ot=V(2, 512, 512), n2=V(1024, 512, t=F32), rs=V(1024, 128, t=F32), a2=V(1024, 512),
+        a2t=V(512, 1024), dyt=V(512, 1024), ya=V(1024, 512, t=F32), da=V(1024, 512, t=F32),
+        act=V(1024, 512), dup=V(1024, 512), do=V(4, 256, 512), dst=V(2, 256, 512), dq=V(4, 768, 512),
+        xst=V(2, 2, 384, 512), dqt=V(2, 768, 1024),
+        gv=V(4, 16, 128, t=F32), gvr=V(2, 16, 128, t=F32), gvy=V(16, 128, t=F32), gva=V(ne, 16, 128, t=F32),
+        gg=V(8, 512, t=F32), gbu=V(4, 8, 512, t=F32),
+        D=pltpu.SemaphoreType.DMA,
+    )
+    for k, r in enumerate(CHUNKS):
+        d[f"G{k}"] = V(4, r, 128)
+        d[f"A{k}"] = V(2, r, 128)
+        d[f"B{k}"] = V(r, 128)
+        d[f"C{k}"] = V(ne - 1, r // ne, 128)
+        d[f"S{k}"] = V(r // ne, 128)
+    del d["D"]
+    return d
+
+
+NSEM = 224
+
+
+class Sems:
+    def __init__(self, send, recv):
+        self.send, self.recv, self.n = send, recv, 0
+
+    def take(self, k=1):
+        i = self.n
+        self.n += k
+        assert self.n <= NSEM
+        return i
+
+
+def body(nz, names, *args):
+    ins = args[:8]
+    y_out, wg_out, red_out, vec_out = args[8:12]
+    S = dict(zip(names, args[12:12 + len(names)]))
+    send, recv = args[12 + len(names):]
+    words_h, cot_h, wqt_h, wo_h, wu_h, wd_h, vec_h, so_h = ins
+    (xs, dys, wt, wo, wu, wd, vec, so, sm, a1, qkv, qst, o, lse, ost, ot, n2, rs, a2, a2t, dyt, ya, da, act, dup, do,
+     dst, dq, xst, dqt, gv, gvr, gvy, gva, gg, gbu) = [S[n] for n in names[:36]]
+    sems = Sems(send, recv)
+    ne = 2 * nz
+    g, x, w = lax.axis_index("group"), lax.axis_index("ctx"), lax.axis_index("wshard")
+    yi, c = w // 2, w % 2
+    oc = 1 - c
+    e = x * nz + g
+    sib = (g, x, 2 * yi + oc)
+    yn = (g, x, 2 * (1 - yi) + c)
+    diag = (g, x, 2 * (1 - yi) + oc)
+    sw = (g, c, 2 * yi + x)
+    stay = x == c
+
+    def peer(d):
+        q = (e + d) % ne
+        return q, (q % nz, q // nz, w)
+
+    def remote(src, dst_, dev, i):
+        return pltpu.make_async_remote_copy(src_ref=src, dst_ref=dst_, send_sem=send.at[i], recv_sem=recv.at[i],
+                                            device_id=dev, device_id_type=MESH)
+
+    def local(src, dst_, i):
+        return pltpu.make_async_copy(src, dst_, send.at[i])
+
+    sends = []
+    locs = []
+
+    bar = pltpu.get_barrier_semaphore()
+    peers = [sib, yn, diag] + [peer(d)[1] for d in range(1, ne)]
+    for p in peers:
+        pl.semaphore_signal(bar, inc=1, device_id=p, device_id_type=MESH)
+
+    @pl.when(jnp.logical_not(stay))
+    def _():
+        pl.semaphore_signal(bar, inc=1, device_id=sw, device_id_type=MESH)
+
+    def swap_start(src, dst_, i):
+        for t in range(4):
+            rows = pl.ds(t * 256, 256)
+
+            @pl.when(stay)
+            def _():
+                local(src.at[rows], dst_.at[rows], i + t).start()
+
+            @pl.when(jnp.logical_not(stay))
+            def _():
+                remote(src.at[rows], dst_.at[rows], sw, i + t).start()
+
+    def swap_piece_wait(src, dst_, i, t, send_too=False):
+        rows = pl.ds(al(t * 256, 256), 256)
+
+        @pl.when(stay)
+        def _():
+            local(src.at[rows], dst_.at[rows], i + t).wait()
+
+        @pl.when(jnp.logical_not(stay))
+        def _():
+            remote(src.at[rows], dst_.at[rows], sw, i + t).wait()
+
+    ix, idy = sems.take(4), sems.take(4)
+    own = []
+    wsl = dict(
+        wt=lambda s: wt.at[:, pl.ds(al(s * 128, 128), 128)],
+        wo=lambda s: wo.at[pl.ds(al(s * 128, 128), 128), :],
+        wu=lambda s: wu.at[:, pl.ds(al(s * 128, 128), 128), :],
+        wd=lambda s: wd.at[:, pl.ds(al(s * 128, 128), 128), :],
+        vec=lambda s: vec.at[s])
+    srcs = dict(wt=wqt_h, wo=wo_h, wu=wu_h, wd=wd_h, vec=vec_h)
+    for n in ("wt", "wo", "wu", "wd", "vec"):
+        cp = local(srcs[n], wsl[n](w), sems.take())
+        cp.start()
+        own.append(cp)
+    so_own = local(so_h, so.at[0], sems.take())
+    so_own.start()
+
+    pl.semaphore_wait(bar, len(peers) + jnp.where(stay, 0, 1))
+
+    gath = {}
+    for n in ("wt", "wo", "wu", "wd"):
+        dv = wsl[n]
+        gath[n] = (remote(srcs[n], dv(w), sib, sems.take()), remote(srcs[n], dv(w), yn, sems.take()),
+                   remote(dv(2 * (1 - yi) + c), dv(2 * (1 - yi) + c), sib, sems.take()))
+
+    def g_start(n):
+        gath[n][0].start()
+        gath[n][1].start()
+
+    def g_forward(n):
+        gath[n][1].wait_recv()
+        gath[n][2].start()
+
+    def g_done(n):
+        gath[n][0].wait()
+        gath[n][1].wait_send()
+        gath[n][2].wait()
+
+    vcs = [remote(vec_h, vec.at[w], p, sems.take()) for p in (sib, yn, diag)]
+    so_x = remote(so_h, so.at[1], sib, sems.take())
+    g_start("wt")
+    swap_start(words_h, xs, ix)
+    for v in vcs:
+        v.start()
+    so_x.start()
+    gg[...] = jnp.zeros_like(gg)
+    gbu[...] = jnp.zeros_like(gbu)
+    gv[...] = jnp.zeros_like(gv)
+    for cp in own:
+        cp.wait()
+    so_own.wait()
+    for v in vcs:
+        v.wait()
+    so_x.wait()
+    so[0] = jnp.where(stay, so[0], so[1])
+    so_s = local(so.at[0], sm, sems.take())
+    so_s.start()
+
+    def row(k):
+        return jnp.concatenate([vec[s, k:k + 1, :] for s in range(4)], axis=1)
+
+    g_forward("wt")
+    for n in ("wo", "wu", "wd"):
+        g_start(n)
+    g1, b1 = row(0), row(1)
+    g_done("wt")
+    so_s.wait()
+
+    iq = sems.take(4)
+
+    def q_piece(t):
+        return remote(qst.at[t], qkv.at[2 * c + t // 2, :, pl.ds(al((t % 2) * 256, 256), 256)], sib, iq + t)
+
+    def a_tile(t, _):
+        rows = pl.ds(al(t * 256, 256), 256)
+        swap_piece_wait(words_h, xs, ix, t)
+        xv = xs[rows, :].astype(F32)
+        xc = xv - rowmean(xv)
+        r = lax.rsqrt(rowmean(xc * xc) + EPS)
+        av = (xc * r * g1 + b1).astype(BF16)
+        a1[rows, :] = av
+        for who in (1, 0):
+            for hp in range(2):
+                cc = oc if who else c
+                res = dg(wt[pl.ds(al((hp * 2 + cc) * 384, 128), 384), :], av, 1, 1)
+                res = jnp.concatenate([res[0:128] * 0.125, res[128:]], axis=0).astype(BF16)
+                if who:
+                    qst[t, hp * 384:(hp + 1) * 384, :] = res
+                else:
+                    qkv[2 * c + t // 2, hp * 384:(hp + 1) * 384, pl.ds(al((t % 2) * 256, 256), 256)] = res
+            if who:
+                q_piece(t).start()
+        return 0
+
+    lax.fori_loop(0, 4, a_tile, 0)
+    swap_start(cot_h, dys, idy)
+    canon = [sm[0, b] for b in range(4)]
+    phys = [jnp.minimum(sum(jnp.where(canon[b] == k, b, 0) for b in range(1, 4)), 3) for k in range(4)]
+
+    def canon_of(p):
+        return jnp.clip(sm[0, p], 0, 3)
+
+    def q_wait(t, _):
+        q_piece(t).wait()
+        return 0
+
+    lax.fori_loop(0, 4, q_wait, 0)
+
+    def rows_of(h, part):
+        return pl.ds(al((h // 2) * 384 + part * 128 + (h % 2) * HD, HD), HD)
+
+    def fwd_head(h, _):
+        kn = [qkv[phys[j], rows_of(h, 1), :].T for j in range(4)]
+        vt = [qkv[phys[j], rows_of(h, 2), :] for j in range(4)]
+        for i in range(4):
+            q = qkv[phys[i], rows_of(h, 0), :]
+            s = []
+            for j in LIVE[i]:
+                sj = dg(kn[j], q, 1, 0)
+                s.append(jnp.where(tri(BLK), sj, -1e30) if j == i else sj)
+            m = functools.reduce(jnp.maximum, [jnp.max(sj, axis=0, keepdims=True) for sj in s])
+            acc = l = None
+            for j, sj in zip(LIVE[i], s):
+                p = jnp.exp(sj - m)
+                lj = colsum(p)
+                oj = dg(vt[j], p.astype(BF16), 1, 0)
+                acc = oj if acc is None else acc + oj
+                l = lj if l is None else l + lj
+            o[i, pl.ds(al(h * HD, HD), HD), :] = acc / l
+            lse[i, pl.ds(h, 1), :] = m + jnp.log(l)
+
+        @pl.when(h == 1)
+        def _():
+            g_forward("wo")
+
+        @pl.when(h == 3)
+        def _():
+            g_forward("wu")
+        return 0
+
+    lax.fori_loop(0, 4, fwd_head, 0)
+    ox = []
+    for b in range(2):
+        ost[b] = o[canon_of(2 * oc + b)].astype(BF16)
+        cp = remote(ost.at[b], ot.at[b, pl.ds(al(c * 256, 256), 256), :], sib, sems.take())
+        cp.start()
+        ox.append(cp)
+    for b in range(2):
+        ot[b, pl.ds(al(c * 256, 256), 256), :] = o[canon_of(2 * c + b)].astype(BF16)
+    g_forward("wd")
+    for cp in ox:
+        cp.wait()
+    for n in ("wo", "wu", "wd"):
+        g_done(n)
+
+    isem = [sems.take(4 + 2 * (ne - 1)) for _ in CHUNKS]
+
+    def r_core(k, q):
+        return remote(S[f"G{k}"].at[2 * q + oc], S[f"A{k}"].at[q], sib, isem[k] + q)
+
+    def r_y(k):
+        return remote(S[f"G{k}"].at[2 * (1 - yi) + c], S[f"B{k}"], yn, isem[k] + 2)
+
+    def r_rs(k):
+        p = CHUNKS[k] // ne
+        for d in range(1, ne):
+            q, dev = peer(d)
+            yield remote(S[f"G{k}"].at[w, pl.ds(al(q * p, 16), p), :], S[f"C{k}"].at[ne - 1 - d], dev, isem[k] + 3 + d)
+
+    def r_ag(k):
+        p = CHUNKS[k] // ne
+        for d in range(1, ne):
+            yield remote(S[f"S{k}"], red_out.at[pl.ds(al(STARTS[k] + e * p, 16), p), :], peer(d)[1],
+                         isem[k] + 2 + ne + d)
+
+    def r_mine(k):
+        p = CHUNKS[k] // ne
+        return local(S[f"S{k}"], red_out.at[pl.ds(al(STARTS[k] + e * p, 16), p), :], isem[k] + 3)
+
+    def s0(k):
+        for q in range(2):
+            r_core(k, q).start()
+
+    def s1(k):
+        G, A = S[f"G{k}"], S[f"A{k}"]
+        for q in range(2):
+            r_core(k, q).wait()
+        for q in range(2):
+            G[2 * q + c] = (G[2 * q + c].astype(F32) + A[q].astype(F32)).astype(BF16)
+        r_y(k).start()
+
+    def s2(k):
+        G, B = S[f"G{k}"], S[f"B{k}"]
+        r_y(k).wait()
+        G[w] = (G[w].astype(F32) + B[...].astype(F32)).astype(BF16)
+        for cp in r_rs(k):
+            cp.start()
+
+    def s3(k):
+        G, C, T = S[f"G{k}"], S[f"C{k}"], S[f"S{k}"]
+        p = CHUNKS[k] // ne
+        for cp in r_rs(k):
+            cp.wait()
+        tot = G[w, pl.ds(al(e * p, 16), p), :].astype(F32)
+        for d in range(ne - 1):
+            tot = tot + C[d].astype(F32)
+        T[...] = tot.astype(BF16)
+        for cp in r_ag(k):
+            cp.start()
+        r_mine(k).start()
+
+    def s4(k):
+        for cp in r_ag(k):
+            cp.wait()
+        r_mine(k).wait()
+
+    g2, b2, bd = row(2), row(3), row(4)
+
+    def c1(t, _):
+        rows = pl.ds(al(t * 256, 256), 256)
+        swap_piece_wait(cot_h, dys, idy, t)
+        mid = xs[rows, :].astype(F32) + dg(ot[t // 2, :, pl.ds(al((t % 2) * 256, 256), 256)], wo[...], 0, 0)
+        xc = mid - rowmean(mid)
+        r = lax.rsqrt(rowmean(xc * xc) + EPS)
+        nv = xc * r
+        n2[rows, :] = nv
+        rs[rows, :] = jnp.broadcast_to(r, (256, 128))
+        av = (nv * g2 + b2).astype(BF16)
+        a2[rows, :] = av
+        a2t[:, rows] = av.T
+        dyv = dys[rows, :]
+        dyt[:, rows] = dyv.T
+        gg[4:5, :] += colsum(dyv.astype(F32))
+        ya[rows, :] = mid + bd
+        da[rows, :] = jnp.zeros((256, 512), F32)
+        return 0
+
+    lax.fori_loop(0, 4, c1, 0)
+
+    for f in range(4):
+        bu = row(5 + f)
+
+        def c2(t, _):
+            rows = pl.ds(al(t * 256, 256), 256)
+            up = dg(a2[rows, :], wu[f], 1, 0) + bu
+            u2 = up * up
+            th = jnp.tanh(up * (K0 + (K0 * K1) * u2))
+            hp = 0.5 + 0.5 * th
+            av = (up * hp).astype(BF16)
+            act[rows, :] = av
+            ya[rows, :] += dg(av, wd[f], 1, 0)
+            dact = dg(dys[rows, :], wd[f], 1, 1)
+            gp = hp + (0.5 * up) * (1.0 - th * th) * (K0 + (3 * K0 * K1) * u2)
+            dv = (dact * gp).astype(BF16)
+            dup[rows, :] = dv
+            gbu[f, 0:1, :] += colsum(dv.astype(F32))
+            da[rows, :] += dg(dv, wu[f], 1, 1)
+            return 0
+
+        lax.fori_loop(0, 4, c2, 0)
+        G = S[f"G{f}"]
+        gd = dg(dyt[...], act[...], 1, 0).astype(BF16)
+        for s in range(4):
+            G[s, 0:512, :] = gd[:, s * 128:(s + 1) * 128]
+        gu = dg(a2t[...], dup[...], 1, 0).astype(BF16)
+        for s in range(4):
+            for b in range(4):
+                G[s, 512 + b * 128:640 + b * 128, :] = gu[s * 128:(s + 1) * 128, b * 128:(b + 1) * 128]
+        s0(f)
+        if f >= 1:
+            s1(f - 1)
+        if f >= 2:
+            s2(f - 2)
+        if f >= 3:
+            s3(f - 3)
+
+    yst, dmid = dup, act
+    iy = sems.take(4)
+    idx = sems.take(4)
+
+    def out_start(src, dst_, i, t):
+        rows = pl.ds(al(t * 256, 256), 256)
+
+        @pl.when(stay)
+        def _():
+            local(src.at[rows], dst_.at[rows], i + t).start()
+
+        @pl.when(jnp.logical_not(stay))
+        def _():
+            remote(src.at[rows], dst_.at[rows], sw, i + t).start()
+
+    def d_piece(t):
+        cols = pl.ds(al((t % 2) * 256, 256), 256)
+        return remote(dst.at[t // 2, :, cols], do.at[2 * c + t // 2, :, cols], sib, idx + t)
+
+    def c3(t, _):
+        rows = pl.ds(al(t * 256, 256), 256)
+        cols = pl.ds(al((t % 2) * 256, 256), 256)
+        yst[rows, :] = ya[rows, :].astype(BF16)
+        out_start(yst, y_out, iy, t)
+        dav, nv, r = da[rows, :], n2[rows, :], rs[rows, 0:1]
+        gg[2:3, :] += colsum(dav * nv)
+        gg[3:4, :] += colsum(dav)
+        gr = dav * g2
+        dn = r * (gr - rowmean(gr) - nv * rowmean(gr * nv))
+        dm = (dys[rows, :].astype(F32) + dn).astype(BF16)
+        dmid[rows, :] = dm
+        dst[t // 2, :, cols] = dg(wo[pl.ds(al(oc * 256, 256), 256), :], dm, 1, 1).astype(BF16)
+        d_piece(t).start()
+        do[2 * c + t // 2, :, cols] = dg(wo[pl.ds(al(c * 256, 256), 256), :], dm, 1, 1).astype(BF16)
+        return 0
+
+    lax.fori_loop(0, 4, c3, 0)
+    go = (dg(ot[0], dmid[0:512, :], 1, 0) + dg(ot[1], dmid[512:1024, :], 1, 0)).astype(BF16)
+    for s in range(4):
+        for b in range(4):
+            S["G4"][s, b * 128:(b + 1) * 128, :] = go[s * 128:(s + 1) * 128, b * 128:(b + 1) * 128]
+    s0(4)
+    s1(3)
+    s2(2)
+    s3(1)
+
+    def d_wait(t, _):
+        d_piece(t).wait()
+        return 0
+
+    lax.fori_loop(0, 4, d_wait, 0)
+
+    ixq = sems.take(4)
+
+    def x_piece(hp, b):
+        return remote(xst.at[hp, b], dqt.at[hp, pl.ds(al(c * 384, 128), 384), pl.ds(b * 512, 512)], sib, ixq + hp * 2 + b)
+
+    def x_start(hp):
+        for b in range(2):
+            xst[hp, b] = dq[canon_of(2 * oc + b), hp * 384:(hp + 1) * 384, :]
+            x_piece(hp, b).start()
+        for b in range(2):
+            dqt[hp, pl.ds(al(c * 384, 128), 384), b * 512:(b + 1) * 512] = dq[canon_of(2 * c + b), hp * 384:(hp + 1) * 384, :]
+
+    def gq_stage(hp):
+        for b in range(2):
+            x_piece(hp, b).wait()
+        G = S[f"G{5 + hp}"]
+        gq = dg(dqt[hp], a1[...], 1, 0).astype(BF16)
+        for s in range(4):
+            G[s] = gq[:, s * 128:(s + 1) * 128]
+        s0(5 + hp)
+
+    def bwd_head(h, _):
+        kt = [qkv[phys[j], rows_of(h, 1), :] for j in range(4)]
+        kn = [kj.T for kj in kt]
+        vn = [qkv[phys[j], rows_of(h, 2), :].T for j in range(4)]
+        dk = [None] * 4
+        dv = [None] * 4
+        hr = pl.ds(al(h * HD, HD), HD)
+        for i in range(4):
+            q = qkv[phys[i], rows_of(h, 0), :]
+            gr = do[phys[i], hr, :]
+            ls = lse[i, pl.ds(h, 1), :]
+            delta = colsum(gr.astype(F32) * o[i, hr, :])
+            dqa = None
+            for j in LIVE[i]:
+                p = jnp.exp(dg(kn[j], q, 1, 0) - ls)
+                if j == i:
+                    p = jnp.where(tri(BLK), p, 0.0)
+                dp = dg(vn[j], gr, 1, 0)
+                ds = (p * (dp - delta)).astype(BF16)
+                p = p.astype(BF16)
+                dqj = dg(kt[j], ds, 1, 0)
+                dkj = dg(q, ds, 1, 1)
+                dvj = dg(gr, p, 1, 1)
+                dqa = dqj if dqa is None else dqa + dqj
+                dk[j] = dkj if dk[j] is None else dk[j] + dkj
+                dv[j] = dvj if dv[j] is None else dv[j] + dvj
+            dq[i, rows_of(h, 0), :] = (dqa * 0.125).astype(BF16)
+        for j in range(4):
+            dq[j, rows_of(h, 1), :] = dk[j].astype(BF16)
+            dq[j, rows_of(h, 2), :] = dv[j].astype(BF16)
+
+        @pl.when(h == 0)
+        def _():
+            s1(4)
+            s2(3)
+            s3(2)
+
+        @pl.when(h == 1)
+        def _():
+            x_start(0)
+            s2(4)
+            s3(3)
+
+        @pl.when(h == 2)
+        def _():
+            gq_stage(0)
+            s3(4)
+
+        @pl.when(h == 3)
+        def _():
+            s1(5)
+        return 0
+
+    lax.fori_loop(0, 4, bwd_head, 0)
+    x_start(1)
+    s2(5)
+    gq_stage(1)
+    wgst = dys
+    iw = sems.take(4)
+
+    def e_tile(t, _):
+        rows = pl.ds(al(t * 256, 256), 256)
+        xv = xs[rows, :].astype(F32)
+        xc = xv - rowmean(xv)
+        r = lax.rsqrt(rowmean(xc * xc) + EPS)
+        nv = xc * r
+        dav = dg(dqt[0, :, rows], wt[0:768, :], 0, 0) + dg(dqt[1, :, rows], wt[768:1536, :], 0, 0)
+        gg[0:1, :] += colsum(dav * nv)
+        gg[1:2, :] += colsum(dav)
+        gr = dav * g1
+        dn = r * (gr - rowmean(gr) - nv * rowmean(gr * nv))
+        wgst[rows, :] = (dmid[rows, :].astype(F32) + dn).astype(BF16)
+        out_start(wgst, wg_out, iw, t)
+
+        @pl.when(t == 0)
+        def _():
+            s1(6)
+        return 0
+
+    lax.fori_loop(0, 4, e_tile, 0)
+    for s in range(4):
+        for k in range(5):
+            gv[s, k:k + 1, :] = gg[k:k + 1, s * 128:(s + 1) * 128]
+        for f in range(4):
+            gv[s, 5 + f:6 + f, :] = gbu[f, 0:1, s * 128:(s + 1) * 128]
+    vx = [remote(gv.at[2 * q + oc], gvr.at[q], sib, sems.take()) for q in range(2)]
+    vy = remote(gv.at[2 * (1 - yi) + c], gvy, yn, sems.take())
+    iv = sems.take(ne - 1)
+    va = [remote(gv.at[w], gva.at[e], peer(d)[1], iv + d - 1) for d in range(1, ne)]
+    for cp in vx:
+        cp.start()
+    s3(5)
+    s2(6)
+    for cp in vx:
+        cp.wait()
+    for q in range(2):
+        gv[2 * q + c] = gv[2 * q + c] + gvr[q]
+    vy.start()
+    vy.wait()
+    gv[w] = gv[w] + gvy[...]
+    gva[e] = gv[w]
+    for cp in va:
+        cp.start()
+    s3(6)
+    for cp in va:
+        cp.wait()
+    tot = gva[0]
+    for d in range(1, ne):
+        tot = tot + gva[d]
+    vec_out[...] = tot
+    for k in range(len(CHUNKS)):
+        s4(k)
+
+    def fin(t, _):
+        swap_piece_wait(yst, y_out, iy, t)
+        swap_piece_wait(wgst, wg_out, iw, t)
+        return 0
+
+    lax.fori_loop(0, 4, fin, 0)
+
+
+def mega(nz, words, cot, wqt, wo, wu, wd, vec, so):
+    sc = scratch(nz)
+    names = tuple(sc)
+    sd = jax.ShapeDtypeStruct
+    any_ = pl.BlockSpec(memory_space=pl.ANY)
+    return pl.pallas_call(
+        functools.partial(body, nz, names),
+        out_shape=(sd((1024, 512), BF16), sd((1024, 512), BF16), sd((ROWS, 128), BF16), sd((16, 128), F32)),
+        in_specs=[any_] * 8,
+        out_specs=(any_, any_, any_, pl.BlockSpec(memory_space=pltpu.VMEM)),
+        scratch_shapes=[sc[n] for n in names] + [pltpu.SemaphoreType.DMA((NSEM,)), pltpu.SemaphoreType.DMA((NSEM,))],
+        compiler_params=pltpu.CompilerParams(collective_id=0, has_side_effects=True, vmem_limit_bytes=VLIM),
+        name="layer",
+    )(words, cot, wqt, wo, wu, wd, vec, so)
+
+
+def on_chip(words, qkv_weight, out_weight, up_weight, down_weight, norm1_gain, norm1_bias, norm2_gain,
+            norm2_bias, up_bias, down_bias, cotangent, seg_map, off_map):
+    nz = lax.axis_size("group")
+    wqt = qkv_weight.reshape(128, 3, 2, 2, 128).transpose(3, 2, 1, 4, 0).reshape(1536, 128)
+    wu = up_weight.reshape(128, 4, 4, 128).transpose(2, 0, 1, 3).reshape(4, 128, 512)
+    wd = down_weight.reshape(4, 128, 512)
+    vec = jnp.concatenate([norm1_gain, norm1_bias, norm2_gain, norm2_bias, down_bias, up_bias]).astype(F32)
+    vec = jnp.pad(vec.reshape(9, 128), ((0, 7), (0, 0)))
+    so = jnp.pad(seg_map * 2 + off_map, ((0, 7), (0, 124)))
+    y, wg, red, gvec = mega(nz, words[0], cotangent[0], wqt, out_weight, wu, wd, vec, so)
+    red = red.astype(F32)
+    ff = red[:4096].reshape(4, 1024, 128)
+    gdown = ff[:, :512].transpose(0, 2, 1).reshape(512, 512)
+    gup = ff[:, 512:].reshape(4, 4, 128, 128).transpose(2, 1, 0, 3).reshape(128, 2048)
+    gout = red[4096:4608].reshape(4, 128, 128).transpose(1, 0, 2).reshape(128, 512)
+    gqkv = red[4608:].reshape(2, 2, 3, 128, 128).transpose(4, 2, 1, 0, 3).reshape(128, 1536)
+    return (y[None], wg.astype(F32)[None], gqkv, gout, gup, gdown, gvec[0], gvec[1], gvec[2], gvec[3],
+            gvec[5:9].reshape(512), gvec[4])
+
 
 HEADS = 8
 HEAD_DIM = 64
-BLK = 512
 
 
 eps = 1e-05
@@ -391,8 +1040,9 @@
 
 
 def solution(mesh):
+    chip = mesh.shape["ctx"] == 2 and mesh.shape["wshard"] == 4
     return jax.shard_map(
-        on_device,
+        on_chip if chip else on_device,
         mesh=mesh,
         in_specs=(
             P(("group", "wshard"), "ctx", None),

time: 767 us -> 185 us (0.24)
  blocking collectives: 221 us -> 0 us
  Pallas kernels: 0 us -> 158 us
  matrix products: 144 us -> 0 us
  waiting for transfers between devices: 111 us -> 0 us
  loops' own time: 108 us -> 0 us
  local copies, waits for them, and re-layouts: 107 us -> 23.1 us
  other arithmetic: 45 us -> 2.89 us
  between operations: 15.8 us -> 0.71 us
    pallas_call x0 -> x1, Pallas kernels: none -> 158 us  [mega(): pl.pallas_call(functools.partial(body, nz, names), out_shape=(sd((1024, 5...]
    dot_general x54 -> x0, matrix products: 144 us -> none  [the longest x6 22.3 us: tile_back(): jnp.einsum('qhd,khd->hqk', split_heads(grad_tile), split_heads(value_tile...]
    psum x1 -> x0, blocking collectives: 130 us -> none  [on_device(): lax.psum((shards[0], shards[1], shards[2], shards[3], shards[4], shards[5...]
    another operation x19 -> x0, loops' own time: 108 us -> none  [the longest x2 30.6 us: attend_back(): lax.fori_loop(0, local_blocks * local_blocks, attend_visit_pair, (held_dk...]
    all_gather x7 -> x0, blocking collectives: 68.5 us -> none  [the longest x1 33.5 us: on_device(): lax.all_gather(down_bias, 'wshard', axis=0, tiled=True)]
    all_gather x5 -> x0, waiting for transfers between devices: 47.1 us -> none  [the longest x1 31.3 us: on_device(): shard_keys = lax.all_gather(key_rows, 'ctx', axis=0, tiled=True)]
    dynamic_slice x88 -> x0, local copies, waits for them, and re-layouts: 38.4 us -> none  [the longest x42 15.8 us: rows_of(): return lax.dynamic_slice_in_dim(array, block_id * BLK, BLK, 0)]
    reduce_scatter x4 -> x0, waiting for transfers between devices: 32.8 us -> none  [the longest x1 32.8 us: on_device(): lax.psum_scatter(grad_qkv.astype(jnp.bfloat16), 'wshard', scatter_dimensi...]
  transfers between devices with their start and end apart: 15 -> 0, of which waited for: 6 -> 0; matrix products, arithmetic and copies ran while one was open for 31% -> 0% of each run, Pallas kernels for 0% -> 0%
where the time goes in v1:
time: 185 us
  Pallas kernels  158 us (85%)
  local copies, waits for them, and re-layouts  23.1 us (12%)
  other arithmetic  2.89 us (2%)
    pallas_call x1, Pallas kernels, mega(): pl.pallas_call(functools.partial(body, nz, names), out_shape=(sd((1024, 5...  158 us
    unnamed x12, local copies, waits for them, and re-layouts  5.15 us

profile of v1, /device:TPU:0, one launch (start us, length us, event | category | flops | bytes accessed | tf_op | source)
XLA Modules:
  0.0 185.0 jit_solution(10225759326012803376)
XLA Ops:
  0.6 0.7 multiply_add_fusion
  1.3 0.6 pad.12.args_7_
  1.9 0.8 dynamic-update-slice
  2.8 0.8 dynamic-update-slice.1
  3.6 0.8 dynamic-update-slice.2
  4.4 0.8 dynamic-update-slice.3
  5.3 0.8 dynamic-update-slice.4
  6.1 0.9 dynamic-update-slice.5
  6.9 0.6 pad_convert_fusion.args_6_
  7.6 1.1 reshape.70
  8.6 1.3 copy.26
  9.9 1.4 reshape.72
  11.3 0.2 copy.37
  11.5 1.0 reshape.73.args_4_
  12.5 158.3 %layer.1 = (bf16[1024,512]{1,0:T(8,128)(2,1)}, bf16[1024,512]{1,0:T(8,128)(2,1)}, bf16[6144,128]{1,0:T(8,128)(2,1)}, f32[16,128]{1,0:T(8,128)}) custom-call(bf16[1024,512]{1,0:T(8,128)(2,1)} %bitcast.53, bf16[1024,512]{1,0:T(8,128)(2,1)} %bitcast.54, bf16[1536,128]{1,0:T(8,128)(2,1)} %bitcast.49, bf16[128,512]{1,0:T(8,128)(2,1)} %args_3_.4, ...), custom_call_target="tpu_custom_call" | custom-call | tf_op jit(solution)/shard_map/layer/pallas_call | solution.py:625
  170.8 1.3 slice_bitcast_fusion.1
  172.1 1.4 slice_bitcast_fusion.2
  173.5 0.9 slice.45
  174.4 0.7 copy.38
  175.2 1.2 slice.44
  176.3 0.9 copy.28
  177.2 1.5 reshape.76
  178.7 0.0 copy-done
  178.7 0.1 slice.46
  178.9 0.1 slice_bitcast_fusion
  179.0 1.3 copy.31
  180.3 0.7 copy.36
  181.0 1.4 reshape.81
  182.4 0.0 copy-done.1
  182.4 1.6 bitcast_convert_fusion
  184.0 0.0 copy-done.2
  184.0 1.0 copy.46
  (4 shorter events, 0.0 us)
Async XLA Ops:
  175.2 3.6 %copy-start = (bf16[6144,128]{1,0:T(8,128)(2,1)S(1)}, bf16[6144,128]{1,0:T(8,128)(2,1)}, u32[]{:S(2)}) copy-start(bf16[6144,128]{1,0:T(8,128)(2,1)} %get-tuple-element.18) | copy-start | bytes 4718596
  180.3 2.1 %copy-start.1 = (bf16[1024,512]{1,0:T(8,128)(2,1)S(1)}, bf16[1024,512]{1,0:T(8,128)(2,1)}, u32[]{:S(2)}) copy-start(bf16[1024,512]{1,0:T(8,128)(2,1)} %get-tuple-element.17) | copy-start | bytes 3145732
  182.4 1.6 copy-start.2

commit v2 on v0

--- a/solution.py
+++ b/solution.py
@@ -1,11 +1,883 @@
+import functools
 import jax
 import jax.numpy as jnp
 from jax import lax
+from jax.experimental import pallas as pl
+from jax.experimental.pallas import tpu as pltpu
 from jax.sharding import PartitionSpec as P
+
+BLK = 512
+HD = 64
+EPS = 1e-5
+F32 = jnp.float32
+BF16 = jnp.bfloat16
+K0 = 0.7978845608
+K1 = 0.044715
+MESH = pl.DeviceIdType.MESH
+VLIM = 63 * 1024 * 1024
+FROWS, OROWS, QROWS = 1024, 512, 384
+OSTART, QSTART, ROWS = 4096, 4608, 6144
+NSEM = 240
+
+
+def dg(a, b, ca, cb):
+    return lax.dot_general(a, b, (((ca,), (cb,)), ((), ())), preferred_element_type=F32)
+
+
+def colsum(v):
+    return jnp.sum(v, axis=0, keepdims=True)
+
+
+def rowmean(v):
+    return jnp.mean(v, axis=-1, keepdims=True)
+
+
+def key_le_query(n, key_axis):
+    k = lax.broadcasted_iota(jnp.int32, (n, n), key_axis)
+    q = lax.broadcasted_iota(jnp.int32, (n, n), 1 - key_axis)
+    return k <= q
+
+
+def al(v, n):
+    return pl.multiple_of(v, n)
+
+
+def scratch(nz):
+    ne = 2 * nz
+    V = lambda *s, t=BF16: pltpu.VMEM(s, t)
+    return dict(
+        xs=V(1024, 512), dys=V(1024, 512), wqr=V(128, 1536), wur=V(128, 2048), wt=V(1536, 512), wo=V(512, 512),
+        wu=V(4, 512, 512), wd=V(4, 512, 512), vown=V(16, 128, t=F32), vec=V(4, 16, 128, t=F32),
+        so=V(2, 8, 128, t=jnp.int32), sm=pltpu.SMEM((8, 128), jnp.int32),
+        a1=V(4, 512, 512), qkv=V(4, 768, 512), o=V(4, 256, 512, t=F32), lse=V(4, 8, 512, t=F32),
+        ost=V(2, 256, 512), ot=V(2, 512, 512), n2=V(1024, 512, t=F32), rs=V(1024, 128, t=F32), a2=V(1024, 512),
+        a2t=V(512, 1024), dyt=V(512, 1024), ya=V(1024, 512, t=F32), da=V(1024, 512, t=F32),
+        act=V(1024, 512), dup=V(1024, 512), do=V(4, 256, 512), dst=V(2, 256, 512), dq=V(4, 768, 512),
+        dkv=V(128, 2048, t=F32), xst=V(4, 2, 192, 512), dqt=V(1536, 1024),
+        gv=V(4, 16, 128, t=F32), gvr=V(2, 16, 128, t=F32), gvy=V(16, 128, t=F32), gva=V(ne, 16, 128, t=F32),
+        gg=V(8, 512, t=F32), gbu=V(4, 8, 512, t=F32),
+        FG=V(4, 4, FROWS, 128), FA=V(4, 2, FROWS, 128), FB=V(4, FROWS, 128), FX=V(4, FROWS // 2, 128),
+        FZ=V(4, nz - 1, FROWS // ne, 128), FT=V(4, FROWS // ne, 128), FH=V(4, FROWS // 2, 128),
+        OG=V(1, 4, OROWS, 128), OA=V(1, 2, OROWS, 128), OB=V(1, OROWS, 128), OX=V(1, OROWS // 2, 128),
+        OZ=V(1, nz - 1, OROWS // ne, 128), OT=V(1, OROWS // ne, 128), OH=V(1, OROWS // 2, 128),
+        QS=V(4, 4, 192, 128), QG=V(4, 2, QROWS, 128), QB=V(4, QROWS, 128), QC=V(4, ne - 1, QROWS // ne, 128),
+        QT=V(4, QROWS // ne, 128),
+    )
+
+
+class Count:
+    def __init__(self):
+        self.n = 0
+
+    def take(self, k=1):
+        self.n += k
+        assert self.n <= NSEM
+        return self.n - k
+
+
+class Ns:
+    def __init__(self, d):
+        self.__dict__.update(d)
+
+
+def body(nz, names, *args):
+    (words_h, cot_h, wq_h, wo_h, wu_h, wd_h, n1g, n1b, n2g, n2b, bdr, bur, seg_r, off_r) = args[:14]
+    y_out, wg_out, red_out, vec_out = args[14:18]
+    m = Ns(dict(zip(names, args[18:18 + len(names)])))
+    send, recv = args[18 + len(names):]
+    ct = Count()
+    ne = 2 * nz
+    g, x, w = lax.axis_index("group"), lax.axis_index("ctx"), lax.axis_index("wshard")
+    yi, c = w // 2, w % 2
+    oc, oy, ox = 1 - c, 1 - yi, 1 - x
+    e = x * nz + g
+    sib = (g, x, 2 * yi + oc)
+    yn = (g, x, 2 * oy + c)
+    diag = (g, x, 2 * oy + oc)
+    xn = (g, ox, w)
+    zp = (g + 1 - 2 * (g % 2), x, w)
+    sw = (g, c, 2 * yi + x)
+    stay = x == c
+    moves = jnp.logical_not(stay)
+
+    def peer(d):
+        q = (e + d) % ne
+        return q, (q % nz, q // nz, w)
+
+    def zpeer(d):
+        q = (g + d) % nz
+        return q, (q, x, w)
+
+    def remote(src, dst_, dev, i):
+        return pltpu.make_async_remote_copy(src_ref=src, dst_ref=dst_, send_sem=send.at[i], recv_sem=recv.at[i],
+                                            device_id=dev, device_id_type=MESH)
+
+    def local(src, dst_, i):
+        return pltpu.make_async_copy(src, dst_, send.at[i])
+
+    def begin(src, dst_):
+        cp = local(src, dst_, ct.take())
+        cp.start()
+        return cp
+
+    l_wq = begin(wq_h, m.wqr)
+    l_wo = begin(wo_h, m.wo.at[pl.ds(al(w * 128, 128), 128), :])
+    l_wu = begin(wu_h, m.wur)
+    l_wd = begin(wd_h, m.wd.at[:, pl.ds(al(w * 128, 128), 128), :])
+    bar = pltpu.get_barrier_semaphore()
+    peers = [sib, yn, diag] + [peer(d)[1] for d in range(1, ne)]
+    for p in peers:
+        pl.semaphore_signal(bar, inc=1, device_id=p, device_id_type=MESH)
+
+    @pl.when(moves)
+    def _():
+        pl.semaphore_signal(bar, inc=1, device_id=sw, device_id_type=MESH)
+
+    m.vown[...] = jnp.zeros_like(m.vown)
+    for k, r in enumerate((n1g, n1b, n2g, n2b, bdr)):
+        m.vown[k:k + 1, :] = r[...].astype(F32)
+    m.vown[5:9, :] = bur[...].astype(F32)
+    m.so[0] = jnp.zeros((8, 128), jnp.int32)
+    m.so[0, 0:1, 0:4] = seg_r[...] * 2 + off_r[...]
+    m.gg[...] = jnp.zeros_like(m.gg)
+    m.gbu[...] = jnp.zeros_like(m.gbu)
+    m.gv[...] = jnp.zeros_like(m.gv)
+    pl.semaphore_wait(bar, len(peers) + jnp.where(stay, 0, 1))
+
+    def swap(src, dst_, i, t, what):
+        rows = pl.ds(al(t * 256, 256), 256)
+
+        @pl.when(stay)
+        def _():
+            cp = local(src.at[rows], dst_.at[rows], i + t)
+            cp.start() if what == "start" else cp.wait()
+
+        @pl.when(moves)
+        def _():
+            cp = remote(src.at[rows], dst_.at[rows], sw, i + t)
+            cp.start() if what == "start" else cp.wait()
+
+    ix, idy, iy, iw = ct.take(4), ct.take(4), ct.take(4), ct.take(4)
+    for t in range(4):
+        swap(words_h, m.xs, ix, t, "start")
+    so_x = remote(m.so.at[0], m.so.at[1], sib, ct.take())
+    so_x.start()
+    vcs = [remote(m.vown, m.vec.at[w], p, ct.take()) for p in (sib, yn, diag)]
+    for v in vcs:
+        v.start()
+    m.vec[w] = m.vown[...]
+
+    mine = pl.ds(al(w * 128, 128), 128)
+    l_wq.wait()
+    for cc in range(2):
+        for hp in range(2):
+            for part in range(3):
+                b = (part * 4 + cc * 2 + hp) * 128
+                blk = m.wqr[:, b:b + 128].T
+                if part == 0:
+                    blk = (blk.astype(F32) * 0.125).astype(BF16)
+                r = cc * 768 + hp * 384 + part * 64
+                m.wt[r:r + 64, mine] = blk[:64]
+                m.wt[r + 192:r + 256, mine] = blk[64:]
+
+    other = 2 * oy + c
+    hs = g % 2
+    sl = dict(
+        wt=lambda s, f=None: m.wt.at[:, pl.ds(al(s * 128, 128), 128)],
+        wo=lambda s, f=None: m.wo.at[pl.ds(al(s * 128, 128), 128), :],
+        wu=lambda s, f=None: m.wu.at[:, pl.ds(al(s * 128, 128), 128), :] if f is None else
+        m.wu.at[pl.ds(2 * f, 2), pl.ds(al(s * 128, 128), 128), :],
+        wd=lambda s, f=None: m.wd.at[:, pl.ds(al(s * 128, 128), 128), :] if f is None else
+        m.wd.at[pl.ds(2 * f, 2), pl.ds(al(s * 128, 128), 128), :])
+    gath = {}
+    for n in ("wt", "wo"):
+        gath[n] = [remote(sl[n](w), sl[n](w), sib, ct.take()), remote(sl[n](w), sl[n](w), yn, ct.take()),
+                   remote(sl[n](other), sl[n](other), sib, ct.take())]
+    for n in ("wu", "wd"):
+        gath[n] = [remote(sl[n](w), sl[n](w), sib, ct.take()), remote(sl[n](w, hs), sl[n](w, hs), yn, ct.take()),
+                   remote(sl[n](other, hs), sl[n](other, hs), zp, ct.take()),
+                   remote(sl[n](other), sl[n](other), sib, ct.take())]
+
+    def g_start(n):
+        gath[n][0].start()
+        gath[n][1].start()
+
+    def g_z(n):
+        gath[n][1].wait_recv()
+        gath[n][2].start()
+
+    def g_forward(n):
+        gath[n][-2].wait_recv()
+        gath[n][-1].start()
+
+    def g_done(n):
+        gath[n][0].wait()
+        gath[n][1].wait_send()
+        if len(gath[n]) == 4:
+            gath[n][2].wait_send()
+        gath[n][-1].wait()
+
+    g_start("wt")
+    l_wu.wait()
+    for f in range(4):
+        for s in range(4):
+            m.wu[f, mine, s * 128:(s + 1) * 128] = m.wur[:, s * 512 + f * 128:s * 512 + (f + 1) * 128]
+    l_wo.wait()
+    l_wd.wait()
+    for v in vcs:
+        v.wait()
+    so_x.wait()
+    m.so[0] = jnp.where(stay, m.so[0], m.so[1])
+    so_s = local(m.so.at[0], m.sm, ct.take())
+    so_s.start()
+
+    def row(k):
+        return jnp.concatenate([m.vec[s, k:k + 1, :] for s in range(4)], axis=1)
+
+    g1, b1 = row(0), row(1)
+
+    ia = ct.take(4)
+
+    def a_slot(core, t):
+        return m.a1.at[2 * core + t // 2, pl.ds(al((t % 2) * 256, 256), 256), :]
+
+    def a_piece(t):
+        return remote(a_slot(c, t), a_slot(c, t), sib, ia + t)
+
+    def norm1(t, _=0):
+        rows = pl.ds(al(t * 256, 256), 256)
+        swap(words_h, m.xs, ix, t, "wait")
+        xv = m.xs[rows, :].astype(F32)
+        xc = xv - rowmean(xv)
+        r = lax.rsqrt(rowmean(xc * xc) + EPS)
+        a_slot(c, t)[...] = (xc * r * g1 + b1).astype(BF16)
+        a_piece(t).start()
+        return 0
+
+    wrows = pl.ds(al(c * 768, 256), 768)
+
+    def project(t, _=0):
+        a_piece(t).wait()
+        cols = pl.ds(al((t % 2) * 256, 256), 256)
+        av = jnp.concatenate([a_slot(0, t)[...], a_slot(1, t)[...]], axis=0)
+        res = dg(m.wt[wrows, :], av, 1, 1).astype(BF16)
+        m.qkv[t // 2, :, cols] = res[:, :256]
+        m.qkv[2 + t // 2, :, cols] = res[:, 256:]
+        return 0
+
+    lax.fori_loop(0, 3, norm1, 0)
+    g_forward("wt")
+    g_start("wo")
+    g_start("wu")
+    g_done("wt")
+    lax.fori_loop(0, 2, project, 0)
+    norm1(3)
+    lax.fori_loop(2, 4, project, 0)
+    for t in range(4):
+        swap(cot_h, m.dys, idy, t, "start")
+    so_s.wait()
+    canon = [m.sm[0, b] for b in range(4)]
+    phys = [jnp.minimum(sum(jnp.where(canon[b] == k, b, 0) for b in range(1, 4)), 3) for k in range(4)]
+
+    def canon_of(p):
+        return jnp.clip(m.sm[0, p], 0, 3)
+
+    def rows_of(h, part):
+        return pl.ds(al(h * 192 + part * 64, 64), 64)
+
+    def fwd_head(h, _):
+        kn = [m.qkv[phys[j], rows_of(h, 1), :].T for j in range(4)]
+        q = jnp.concatenate([m.qkv[phys[j], rows_of(h, 0), :] for j in range(4)], axis=1)
+        tri = key_le_query(BLK, 0)
+        s = []
+        for j in range(4):
+            sj = dg(kn[j], q[:, j * BLK:], 1, 0)
+            sd = jnp.where(tri, sj[:, :BLK], -1e30)
+            s.append(sd if j == 3 else jnp.concatenate([sd, sj[:, BLK:]], axis=1))
+        mx = [jnp.max(sj, axis=0, keepdims=True) for sj in s]
+        top = mx[0]
+        for j in range(1, 4):
+            top = jnp.concatenate([top[:, :j * BLK], jnp.maximum(top[:, j * BLK:], mx[j])], axis=1)
+        acc = tot = None
+        for j in range(4):
+            p = jnp.exp(s[j] - top[:, j * BLK:])
+            lj = colsum(p)
+            a = dg(m.qkv[phys[j], rows_of(h, 2), :], p.astype(BF16), 1, 0)
+            acc = a if acc is None else jnp.concatenate([acc[:, :j * BLK], acc[:, j * BLK:] + a], axis=1)
+            tot = lj if tot is None else jnp.concatenate([tot[:, :j * BLK], tot[:, j * BLK:] + lj], axis=1)
+        ov = acc * (1.0 / tot)
+        ls = top + jnp.log(tot)
+        for i in range(4):
+            m.o[i, pl.ds(al(h * HD, HD), HD), :] = ov[:, i * BLK:(i + 1) * BLK]
+            m.lse[i, pl.ds(h, 1), :] = ls[:, i * BLK:(i + 1) * BLK]
+
+        @pl.when(h == 0)
+        def _():
+            g_forward("wo")
+            g_start("wd")
+
+        @pl.when(h == 2)
+        def _():
+            g_z("wu")
+
+        @pl.when(h == 3)
+        def _():
+            g_z("wd")
+        return 0
+
+    lax.fori_loop(0, 4, fwd_head, 0)
+    oxc = []
+    for b in range(2):
+        m.ost[b] = m.o[canon_of(2 * oc + b)].astype(BF16)
+        cp = remote(m.ost.at[b], m.ot.at[b, pl.ds(al(c * 256, 256), 256), :], sib, ct.take())
+        cp.start()
+        oxc.append(cp)
+    for b in range(2):
+        m.ot[b, pl.ds(al(c * 256, 256), 256), :] = m.o[canon_of(2 * c + b)].astype(BF16)
+    g_forward("wu")
+    g_done("wo")
+    for cp in oxc:
+        cp.wait()
+
+    class Chunk:
+        def __init__(self, tag, rows, start, count):
+            for q in "GABXZTH":
+                setattr(self, q, getattr(m, tag + q))
+            self.rows, self.start, self.half, self.p = rows, start, rows // 2, rows // ne
+            self.n = 6 + 2 * nz
+            self.i = ct.take(self.n * count)
+
+        def core(self, k, q):
+            return remote(self.G.at[k, 2 * q + oc], self.A.at[k, q], sib, self.i + k * self.n + q)
+
+        def y(self, k):
+            return remote(self.G.at[k, other], self.B.at[k], yn, self.i + k * self.n + 2)
+
+        def x(self, k):
+            return remote(self.G.at[k, w, pl.ds(al(ox * self.half, 64), self.half), :], self.X.at[k], xn,
+                          self.i + k * self.n + 3)
+
+        def z(self, k, d):
+            q, dev = zpeer(d)
+            return remote(self.G.at[k, w, pl.ds(al(x * self.half + q * self.p, 16), self.p), :],
+                          self.Z.at[k, nz - 1 - d], dev, self.i + k * self.n + 3 + d)
+
+        def back(self, k, d):
+            return remote(self.T.at[k], self.H.at[k, pl.ds(al(g * self.p, 16), self.p), :], zpeer(d)[1],
+                          self.i + k * self.n + 2 + nz + d)
+
+        def at(self, k):
+            return red_out.at[pl.ds(al(self.start + k * self.rows + x * self.half, 16), self.half), :]
+
+        def xback(self, k):
+            return remote(self.H.at[k], self.at(k), xn, self.i + k * self.n + 2 + 2 * nz)
+
+        def keep(self, k):
+            return local(self.H.at[k], self.at(k), self.i + k * self.n + 3 + 2 * nz)
+
+        def s0(self, k):
+            for q in range(2):
+                self.core(k, q).start()
+
+        def s1(self, k):
+            for q in range(2):
+                self.core(k, q).wait()
+            self.G[k, other] = (self.G[k, other].astype(F32) + self.A[k, oy].astype(F32)).astype(BF16)
+            self.y(k).start()
+            self.G[k, w] = (self.G[k, w].astype(F32) + self.A[k, yi].astype(F32)).astype(BF16)
+
+        def s2(self, k):
+            self.y(k).wait()
+            self.G[k, w] = (self.G[k, w].astype(F32) + self.B[k].astype(F32)).astype(BF16)
+            self.x(k).start()
+
+        def s3(self, k):
+            self.x(k).wait()
+            hrows = pl.ds(al(x * self.half, 64), self.half)
+            self.G[k, w, hrows, :] = (self.G[k, w, hrows, :].astype(F32) + self.X[k].astype(F32)).astype(BF16)
+            for d in range(1, nz):
+                self.z(k, d).start()
+
+        def s4(self, k):
+            for d in range(1, nz):
+                self.z(k, d).wait()
+            tot = self.G[k, w, pl.ds(al(x * self.half + g * self.p, 16), self.p), :].astype(F32)
+            for d in range(nz - 1):
+                tot = tot + self.Z[k, d].astype(F32)
+            tot = tot.astype(BF16)
+            self.T[k] = tot
+            self.H[k, pl.ds(al(g * self.p, 16), self.p), :] = tot
+            for d in range(1, nz):
+                self.back(k, d).start()
+
+        def s5(self, k):
+            for d in range(1, nz):
+                self.back(k, d).wait()
+            self.xback(k).start()
+            self.keep(k).start()
+
+        def s6(self, k):
+            self.xback(k).wait()
+            self.keep(k).wait()
+
+    qi = ct.take(4 * (4 + 2 * ne))
+    qn, qp = 4 + 2 * ne, QROWS // ne
+
+    def q_core(k, q):
+        return remote(m.QS.at[k, 2 * q + oc], m.QG.at[k, q, pl.ds(al(c * 192, 64), 192), :], sib, qi + k * qn + q)
+
+    def q_y(k):
+        return remote(m.QG.at[k, oy], m.QB.at[k], yn, qi + k * qn + 2)
+
+    def q_rs(k, d):
+        q, dev = peer(d)
+        return remote(m.QG.at[k, yi, pl.ds(al(q * qp, 16), qp), :], m.QC.at[k, ne - 1 - d], dev, qi + k * qn + 3 + d)
+
+    def q_at(k):
+        return red_out.at[pl.ds(al(QSTART + k * QROWS + e * qp, 16), qp), :]
+
+    def q_ag(k, d):
+        return remote(m.QT.at[k], q_at(k), peer(d)[1], qi + k * qn + 2 + ne + d)
+
+    def q_keep(k):
+        return local(m.QT.at[k], q_at(k), qi + k * qn + 3)
+
+    def q0(k):
+        for q in range(2):
+            q_core(k, q).start()
+        for q in range(2):
+            m.QG[k, q, pl.ds(al(c * 192, 64), 192), :] = m.QS[k, 2 * q + c]
+
+    def q1(k):
+        for q in range(2):
+            q_core(k, q).wait()
+        q_y(k).start()
+
+    def q2(k):
+        q_y(k).wait()
+        m.QG[k, yi] = (m.QG[k, yi].astype(F32) + m.QB[k].astype(F32)).astype(BF16)
+        for d in range(1, ne):
+            q_rs(k, d).start()
+
+    def q3(k):
+        for d in range(1, ne):
+            q_rs(k, d).wait()
+        tot = m.QG[k, yi, pl.ds(al(e * qp, 16), qp), :].astype(F32)
+        for d in range(ne - 1):
+            tot = tot + m.QC[k, d].astype(F32)
+        m.QT[k] = tot.astype(BF16)
+        for d in range(1, ne):
+            q_ag(k, d).start()
+        q_keep(k).start()
+
+    def q4(k):
+        for d in range(1, ne):
+            q_ag(k, d).wait()
+        q_keep(k).wait()
+
+    FC = Chunk("F", FROWS, 0, 4)
+    OC = Chunk("O", OROWS, OSTART, 1)
+
+    g2, b2, bd = row(2), row(3), row(4)
+
+    def c1(t, _):
+        rows = pl.ds(al(t * 512, 512), 512)
+        for u in range(2):
+            swap(cot_h, m.dys, idy, 2 * t + u, "wait")
+        mid = m.xs[rows, :].astype(F32) + dg(m.ot[t], m.wo[...], 0, 0)
+        xc = mid - rowmean(mid)
+        r = lax.rsqrt(rowmean(xc * xc) + EPS)
+        nv = xc * r
+        m.n2[rows, :] = nv
+        m.rs[rows, :] = jnp.broadcast_to(r, (512, 128))
+        av = (nv * g2 + b2).astype(BF16)
+        m.a2[rows, :] = av
+        m.a2t[:, rows] = av.T
+        dyv = m.dys[rows, :]
+        m.dyt[:, rows] = dyv.T
+        m.gg[4:5, :] += colsum(dyv.astype(F32))
+        m.ya[rows, :] = mid + bd
+        m.da[rows, :] = jnp.zeros((512, 512), F32)
+        return 0
+
+    lax.fori_loop(0, 2, c1, 0)
+    g_forward("wd")
+    g_done("wu")
+    g_done("wd")
+
+    def c2(f, _):
+        bu = jnp.concatenate([m.vec[s, pl.ds(5 + f, 1), :] for s in range(4)], axis=1)
+        wuf, wdf = m.wu[f], m.wd[f]
+        up = dg(m.a2[...], wuf, 1, 0) + bu
+        u2 = up * up
+        th = jnp.tanh(up * (K0 + (K0 * K1) * u2))
+        hp = 0.5 + 0.5 * th
+        av = (up * hp).astype(BF16)
+        m.act[...] = av
+        m.ya[...] += dg(av, wdf, 1, 0)
+        dact = dg(m.dys[...], wdf, 1, 1)
+        gp = hp + (0.5 * up) * (1.0 - th * th) * (K0 + (3 * K0 * K1) * u2)
+        dv = (dact * gp).astype(BF16)
+        m.dup[...] = dv
+        m.gbu[f, 0:1, :] = colsum(dv.astype(F32))
+        m.da[...] += dg(dv, wuf, 1, 1)
+
+        @pl.when(f > 0)
+        def _():
+            FC.s1(f - 1)
+
+        @pl.when(f == 3)
+        def _():
+            FC.s2(0)
+
+        gd = dg(m.dyt[...], m.act[...], 1, 0).astype(BF16)
+        for s in range(4):
+            m.FG[f, s, 0:512, :] = gd[:, s * 128:(s + 1) * 128]
+        gu = dg(m.a2t[...], m.dup[...], 1, 0).astype(BF16)
+        for s in range(4):
+            for b in range(4):
+                m.FG[f, s, 512 + b * 128:640 + b * 128, :] = gu[s * 128:(s + 1) * 128, b * 128:(b + 1) * 128]
+        FC.s0(f)
+        return 0
+
+    lax.fori_loop(0, 4, c2, 0)
+    yst, dmid = m.dup, m.act
+    idx = ct.take(2)
+
+    def d_piece(t):
+        return remote(m.dst.at[t], m.do.at[2 * c + t], sib, idx + t)
+
+    def c3(t, _):
+        rows = pl.ds(al(t * 512, 512), 512)
+        yst[rows, :] = m.ya[rows, :].astype(BF16)
+        for u in range(2):
+            swap(yst, y_out, iy, 2 * t + u, "start")
+        dav, nv, r = m.da[rows, :], m.n2[rows, :], m.rs[rows, 0:1]
+        m.gg[2:3, :] += colsum(dav * nv)
+        m.gg[3:4, :] += colsum(dav)
+        gr = dav * g2
+        dn = r * (gr - rowmean(gr) - nv * rowmean(gr * nv))
+        dm = (m.dys[rows, :].astype(F32) + dn).astype(BF16)
+        dmid[rows, :] = dm
+        m.dst[t] = dg(m.wo[pl.ds(al(oc * 256, 256), 256), :], dm, 1, 1).astype(BF16)
+        d_piece(t).start()
+        m.do[2 * c + t] = dg(m.wo[pl.ds(al(c * 256, 256), 256), :], dm, 1, 1).astype(BF16)
+
+        @pl.when(t == 0)
+        def _():
+            FC.s1(3)
+        return 0
+
+    lax.fori_loop(0, 2, c3, 0)
+    go = (dg(m.ot[0], dmid[0:512, :], 1, 0) + dg(m.ot[1], dmid[512:1024, :], 1, 0)).astype(BF16)
+    for s in range(4):
+        for b in range(4):
+            m.OG[0, s, b * 128:(b + 1) * 128, :] = go[s * 128:(s + 1) * 128, b * 128:(b + 1) * 128]
+    OC.s0(0)
+    FC.s2(1)
+    FC.s3(0)
+    for t in range(2):
+        d_piece(t).wait()
+
+    ixq = ct.take(8)
+
+    def x_piece(h, b):
+        return remote(m.xst.at[h, b], m.dqt.at[pl.ds(al(c * 768 + h * 192, 64), 192), pl.ds(b * 512, 512)], sib,
+                      ixq + h * 2 + b)
+
+    def x_start(h):
+        hrows = pl.ds(al(h * 192, 64), 192)
+        for b in range(2):
+            m.xst[h, b] = m.dq[canon_of(2 * oc + b), hrows, :]
+            x_piece(h, b).start()
+        for b in range(2):
+            m.dqt[pl.ds(al(c * 768 + h * 192, 64), 192), b * 512:(b + 1) * 512] = m.dq[canon_of(2 * c + b), hrows, :]
+
+    def q_grad(h):
+        hrows = pl.ds(al(h * 192, 64), 192)
+        gq = None
+        for i in range(4):
+            part = dg(m.dq[i, hrows, :], m.a1[phys[i]], 1, 0)
+            gq = part if gq is None else gq + part
+        gq = gq.astype(BF16)
+        for s in range(4):
+            m.QS[h, s] = gq[:, s * 128:(s + 1) * 128]
+        q0(h)
+
+    def bwd_head(h, _):
+        hr = pl.ds(al(h * HD, HD), HD)
+        kt = jnp.concatenate([m.qkv[phys[j], rows_of(h, 1), :] for j in range(4)], axis=1)
+        vt = jnp.concatenate([m.qkv[phys[j], rows_of(h, 2), :] for j in range(4)], axis=1)
+        kn = kt.T
+        tri = key_le_query(256, 1)
+        for i in reversed(range(8)):
+            L, b, cs = (i + 1) * 256, i // 2, slice((i % 2) * 256, (i % 2) * 256 + 256)
+            q = m.qkv[phys[b], rows_of(h, 0), cs]
+            gr = m.do[phys[b], hr, cs]
+            ls = m.lse[b, pl.ds(h, 1), cs]
+            delta = colsum(gr.astype(F32) * m.o[b, hr, cs])
+            lsb = jnp.broadcast_to(ls, (128, 256)).T[:, 0:1]
+            deb = jnp.broadcast_to(delta, (128, 256)).T[:, 0:1]
+            p = jnp.exp(dg(q.T, kt[:, :L], 1, 0) - lsb)
+            pd = jnp.where(tri, p[:, L - 256:], 0.0)
+            p = jnp.concatenate([p[:, :L - 256], pd], axis=1) if i else pd
+            dp = dg(gr.T, vt[:, :L], 1, 0)
+            ds = (p * (dp - deb)).astype(BF16)
+            p = p.astype(BF16)
+            m.dq[b, rows_of(h, 0), cs] = dg(ds, kn[:L], 1, 0).T.astype(BF16)
+            dk, dv = dg(q, ds, 1, 0), dg(gr, p, 1, 0)
+            if i == 7:
+                m.dkv[0:64, :] = dk
+                m.dkv[64:128, :] = dv
+            else:
+                m.dkv[0:64, :L] += dk
+                m.dkv[64:128, :L] += dv
+        for j in range(4):
+            m.dq[j, rows_of(h, 1), :] = m.dkv[0:64, j * BLK:(j + 1) * BLK].astype(BF16)
+            m.dq[j, rows_of(h, 2), :] = m.dkv[64:128, j * BLK:(j + 1) * BLK].astype(BF16)
+        x_start(h)
+        q_grad(h)
+
+        @pl.when(h > 0)
+        def _():
+            FC.s5(h - 1)
+            q1(h - 1)
+
+        FC.s4(h)
+
+        @pl.when(h < 3)
+        def _():
+            FC.s3(h + 1)
+
+        @pl.when(h < 2)
+        def _():
+            FC.s2(h + 2)
+
+        @pl.when(h > 1)
+        def _():
+            q2(h - 2)
+
+        @pl.when(h == 0)
+        def _():
+            OC.s1(0)
+
+        @pl.when(h == 1)
+        def _():
+            OC.s2(0)
+
+        @pl.when(h == 2)
+        def _():
+            OC.s3(0)
+
+        @pl.when(h == 3)
+        def _():
+            OC.s4(0)
+            q3(0)
+        return 0
+
+    lax.fori_loop(0, 4, bwd_head, 0)
+
+    def e0(t, _):
+        rows = pl.ds(al(t * 256, 256), 256)
+        xv = m.xs[rows, :].astype(F32)
+        xc = xv - rowmean(xv)
+        r = lax.rsqrt(rowmean(xc * xc) + EPS)
+        m.n2[rows, :] = xc * r
+        m.rs[rows, :] = jnp.broadcast_to(r, (256, 128))
+        return 0
+
+    lax.fori_loop(0, 4, e0, 0)
+    q1(3)
+
+    def x_wait(h, _):
+        for b in range(2):
+            x_piece(h, b).wait()
+        return 0
+
+    lax.fori_loop(0, 4, x_wait, 0)
+    wgst = m.dys
+
+    def e1(t, _):
+        rows = pl.ds(al(t * 256, 256), 256)
+        dav = dg(m.dqt[:, rows], m.wt[...], 0, 0)
+        nv, r = m.n2[rows, :], m.rs[rows, 0:1]
+        m.gg[0:1, :] += colsum(dav * nv)
+        m.gg[1:2, :] += colsum(dav)
+        gr = dav * g1
+        dn = r * (gr - rowmean(gr) - nv * rowmean(gr * nv))
+        wgst[rows, :] = (dmid[rows, :].astype(F32) + dn).astype(BF16)
+        swap(wgst, wg_out, iw, t, "start")
+
+        @pl.when(t == 0)
+        def _():
+            q2(2)
+            q3(1)
+
+        @pl.when(t == 1)
+        def _():
+            FC.s5(3)
+            OC.s5(0)
+
+        @pl.when(t == 2)
+        def _():
+            q2(3)
+            q3(2)
+        return 0
+
+    lax.fori_loop(0, 4, e1, 0)
+    for s in range(4):
+        for k in range(5):
+            m.gv[s, k:k + 1, :] = m.gg[k:k + 1, s * 128:(s + 1) * 128]
+        for f in range(4):
+            m.gv[s, 5 + f:6 + f, :] = m.gbu[f, 0:1, s * 128:(s + 1) * 128]
+    vx = [remote(m.gv.at[2 * q + oc], m.gvr.at[q], sib, ct.take()) for q in range(2)]
+    vy = remote(m.gv.at[other], m.gvy, yn, ct.take())
+    iv = ct.take(ne - 1)
+    va = [remote(m.gv.at[w], m.gva.at[e], peer(d)[1], iv + d - 1) for d in range(1, ne)]
+    for cp in vx:
+        cp.start()
+    for cp in vx:
+        cp.wait()
+    for q in range(2):
+        m.gv[2 * q + c] = m.gv[2 * q + c] + m.gvr[q]
+    vy.start()
+    q3(3)
+    vy.wait()
+    m.gv[w] = m.gv[w] + m.gvy[...]
+    m.gva[e] = m.gv[w]
+    for cp in va:
+        cp.start()
+    for cp in va:
+        cp.wait()
+    tot = m.gva[0]
+    for d in range(1, ne):
+        tot = tot + m.gva[d]
+    vec_out[...] = tot
+    OC.s6(0)
+
+    def fin(t, _):
+        FC.s6(t)
+        q4(t)
+        swap(yst, y_out, iy, t, "wait")
+        swap(wgst, wg_out, iw, t, "wait")
+        return 0
+
+    lax.fori_loop(0, 4, fin, 0)
+
+
+def layer(nz, *ops):
+    sc = scratch(nz)
+    names = tuple(sc)
+    sd = jax.ShapeDtypeStruct
+    any_ = pl.BlockSpec(memory_space=pl.ANY)
+    vm = pl.BlockSpec(memory_space=pltpu.VMEM)
+    return pl.pallas_call(
+        functools.partial(body, nz, names),
+        out_shape=(sd((1024, 512), BF16), sd((1024, 512), BF16), sd((ROWS, 128), BF16), sd((16, 128), F32)),
+        in_specs=[any_] * 6 + [vm] * 8,
+        out_specs=(any_, any_, any_, vm),
+        scratch_shapes=[sc[n] for n in names] + [pltpu.SemaphoreType.DMA((NSEM,)), pltpu.SemaphoreType.DMA((NSEM,))],
+        compiler_params=pltpu.CompilerParams(collective_id=0, has_side_effects=True, vmem_limit_bytes=VLIM),
+        name="layer",
+    )(*ops)
+
+
+def finish_body(y_h, wg_h, red_h, v, yo_h, wgo_h, gq_h, go_h, gu_h, gd_h, v1, v2, v3, v4, vu, vd,
+                wg, red, wgo, yv, gq, go, gu, gd, sem):
+    def cp(a, b, i):
+        return pltpu.make_async_copy(a, b, sem.at[i])
+
+    def red_in(k):
+        return cp(red_h.at[pl.ds(k * 1024, 1024)], red.at[pl.ds(k * 1024, 1024)], k)
+
+    def wg_in(k):
+        return cp(wg_h.at[pl.ds(k * 256, 256)], wg.at[pl.ds(k * 256, 256)], 6 + k)
+
+    outs = []
+
+    def put(a, b):
+        o = cp(a, b, 10 + len(outs))
+        o.start()
+        outs.append(o)
+
+    def y_in(k):
+        return cp(y_h.at[pl.ds(k * 512, 512)], yv.at[pl.ds(k * 512, 512)], 22 + k)
+
+    for k in range(4):
+        wg_in(k).start()
+    for k in range(2):
+        y_in(k).start()
+    for k in range(6):
+        red_in(k).start()
+    for r, k in ((v1, 0), (v2, 1), (v3, 2), (v4, 3), (vd, 4)):
+        r[...] = v[k:k + 1, :]
+    vu[...] = v[5:9, :]
+    for k in range(4):
+        wg_in(k).wait()
+        rows = slice(k * 256, (k + 1) * 256)
+        wgo[rows, :] = wg[rows, :].astype(F32)
+        put(wgo.at[rows], wgo_h.at[rows])
+    for k in range(2):
+        y_in(k).wait()
+        put(yv.at[pl.ds(k * 512, 512)], yo_h.at[pl.ds(k * 512, 512)])
+    for f in range(4):
+        red_in(f).wait()
+        gd[f * 128:(f + 1) * 128, :] = red[f * 1024:f * 1024 + 512, :].astype(F32).T
+        put(gd.at[f * 128:(f + 1) * 128], gd_h.at[f * 128:(f + 1) * 128])
+        for s in range(4):
+            gu[:, s * 512 + f * 128:s * 512 + (f + 1) * 128] = red[f * 1024 + 512 + s * 128:f * 1024 + 640 + s * 128, :].astype(F32)
+    put(gu, gu_h)
+    red_in(4).wait()
+    for b in range(4):
+        go[:, b * 128:(b + 1) * 128] = red[OSTART + b * 128:OSTART + (b + 1) * 128, :].astype(F32)
+    put(go, go_h)
+    red_in(5).wait()
+    for hp in range(2):
+        for cc in range(2):
+            for part in range(3):
+                r = QSTART + hp * 768 + cc * 192 + part * 64
+                blk = jnp.concatenate([red[r:r + 64, :], red[r + 384:r + 448, :]], axis=0).astype(F32).T
+                if part == 0:
+                    blk = blk * 0.125
+                k = part * 512 + cc * 256 + hp * 128
+                gq[:, k:k + 128] = blk
+    put(gq, gq_h)
+    for o in outs:
+        o.wait()
+
+
+def finish(y, wg, red, v):
+    sd = jax.ShapeDtypeStruct
+    any_ = pl.BlockSpec(memory_space=pl.ANY)
+    vm = pl.BlockSpec(memory_space=pltpu.VMEM)
+    one = sd((1, 128), F32)
+    big = (sd((128, 1536), F32), sd((128, 512), F32), sd((128, 2048), F32), sd((512, 512), F32))
+    return pl.pallas_call(
+        finish_body,
+        out_shape=(sd((1024, 512), BF16), sd((1024, 512), F32)) + big + (one, one, one, one, sd((4, 128), F32), one),
+        in_specs=[any_] * 3 + [vm],
+        out_specs=(any_,) * 6 + (vm,) * 6,
+        scratch_shapes=[pltpu.VMEM((1024, 512), BF16), pltpu.VMEM((ROWS, 128), BF16), pltpu.VMEM((1024, 512), F32),
+                        pltpu.VMEM((1024, 512), BF16)]
+        + [pltpu.VMEM(b.shape, F32) for b in big] + [pltpu.SemaphoreType.DMA((24,))],
+        compiler_params=pltpu.CompilerParams(vmem_limit_bytes=VLIM), name="finish",
+    )(y, wg, red, v)
+
+
+def on_chip(words, qkv_weight, out_weight, up_weight, down_weight, norm1_gain, norm1_bias, norm2_gain,
+            norm2_bias, up_bias, down_bias, cotangent, seg_map, off_map):
+    nz = lax.axis_size("group")
+    r = lambda v: v.reshape(-1, 128)
+    y, wg, red, v = layer(nz, words[0], cotangent[0], qkv_weight, out_weight, up_weight, down_weight.reshape(4, 128, 512),
+                          r(norm1_gain), r(norm1_bias), r(norm2_gain), r(norm2_bias), r(down_bias), r(up_bias),
+                          seg_map, off_map)
+    y, wg, gq, go, gu, gd, v1, v2, v3, v4, vu, vd = finish(y, wg, red, v)
+    f = lambda t: t.reshape(-1)
+    return y[None], wg[None], gq, go, gu, gd, f(v1), f(v2), f(v3), f(v4), f(vu), f(vd)
+
 
 HEADS = 8
 HEAD_DIM = 64
-BLK = 512
 
 
 eps = 1e-05
@@ -391,8 +1263,9 @@
 
 
 def solution(mesh):
+    chip = mesh.shape["ctx"] == 2 and mesh.shape["wshard"] == 4 and mesh.shape["group"] in (2, 4)
     return jax.shard_map(
-        on_device,
+        on_chip if chip else on_device,
         mesh=mesh,
         in_specs=(
             P(("group", "wshard"), "ctx", None),

time: 767 us -> 146 us (0.19)
  blocking collectives: 221 us -> 0 us
  Pallas kernels: 0 us -> 145 us
  matrix products: 144 us -> 0 us
  waiting for transfers between devices: 111 us -> 0 us
  loops' own time: 108 us -> 0 us
  local copies, waits for them, and re-layouts: 107 us -> 0 us
  other arithmetic: 45 us -> 0 us
  between operations: 15.8 us -> 0.82 us
    pallas_call x0 -> x2, Pallas kernels: none -> 145 us  [the longest x1 140 us: layer(): pl.pallas_call(functools.partial(body, nz, names), out_shape=(sd((1024, 5...]
    dot_general x54 -> x0, matrix products: 144 us -> none  [the longest x6 22.3 us: tile_back(): jnp.einsum('qhd,khd->hqk', split_heads(grad_tile), split_heads(value_tile...]
    psum x1 -> x0, blocking collectives: 130 us -> none  [on_device(): lax.psum((shards[0], shards[1], shards[2], shards[3], shards[4], shards[5...]
    another operation x19 -> x0, loops' own time: 108 us -> none  [the longest x2 30.6 us: attend_back(): lax.fori_loop(0, local_blocks * local_blocks, attend_visit_pair, (held_dk...]
    all_gather x7 -> x0, blocking collectives: 68.5 us -> none  [the longest x1 33.5 us: on_device(): lax.all_gather(down_bias, 'wshard', axis=0, tiled=True)]
    all_gather x5 -> x0, waiting for transfers between devices: 47.1 us -> none  [the longest x1 31.3 us: on_device(): shard_keys = lax.all_gather(key_rows, 'ctx', axis=0, tiled=True)]
    dynamic_slice x88 -> x0, local copies, waits for them, and re-layouts: 38.4 us -> none  [the longest x42 15.8 us: rows_of(): return lax.dynamic_slice_in_dim(array, block_id * BLK, BLK, 0)]
    reduce_scatter x4 -> x0, waiting for transfers between devices: 32.8 us -> none  [the longest x1 32.8 us: on_device(): lax.psum_scatter(grad_qkv.astype(jnp.bfloat16), 'wshard', scatter_dimensi...]
  transfers between devices with their start and end apart: 15 -> 0, of which waited for: 6 -> 0; matrix products, arithmetic and copies ran while one was open for 31% -> 0% of each run, Pallas kernels for 0% -> 0%
where the time goes in v2:
time: 146 us
  Pallas kernels  145 us (99%)
    pallas_call x1, Pallas kernels, layer(): pl.pallas_call(functools.partial(body, nz, names), out_shape=(sd((1024, 5...  140 us
    pallas_call x1, Pallas kernels, finish(): pl.pallas_call(finish_body, out_shape=(sd((1024, 512), BF16), sd((1024, 5...  5.14 us

profile of v2, /device:TPU:0, one launch (start us, length us, event | category | flops | bytes accessed | tf_op | source)
XLA Modules:
  0.0 145.5 jit_solution(13890601912352883719)
XLA Ops:
  0.6 139.6 %layer.1 = (bf16[1024,512]{1,0:T(8,128)(2,1)}, bf16[1024,512]{1,0:T(8,128)(2,1)}, bf16[6144,128]{1,0:T(8,128)(2,1)}, f32[16,128]{1,0:T(8,128)}) custom-call(bf16[1024,512]{1,0:T(8,128)(2,1)} %bitcast.17, bf16[1024,512]{1,0:T(8,128)(2,1)} %bitcast.18, bf16[128,1536]{1,0:T(8,128)(2,1)} %args_2_.4, bf16[128,512]{1,0:T(8,128)(2,1)} %args_3_.4, ...), custom_call_target="tpu_custom_call" | custom-call | tf_op jit(solution)/shard_map/layer/pallas_call | solution.py:774
  140.2 5.1 %finish.1 = (bf16[1024,512]{1,0:T(8,128)(2,1)}, f32[1024,512]{1,0:T(8,128)}, f32[128,1536]{1,0:T(8,128)}, f32[128,512]{1,0:T(8,128)}, f32[128,2048]{1,0:T(8,128)...) custom-call(bf16[1024,512]{1,0:T(8,128)(2,1)} %get-tuple-element.28., ...), custom_call_target="tpu_custom_call" | custom-call | tf_op jit(solution)/shard_map/finish/pallas_call | solution.py:855

commit v3 on v2

--- a/solution.py
+++ b/solution.py
@@ -17,7 +17,42 @@
 VLIM = 63 * 1024 * 1024
 FROWS, OROWS, QROWS = 1024, 512, 384
 OSTART, QSTART, ROWS = 4096, 4608, 6144
-NSEM = 240
+NSEM = 280
+CHUNKS = (("F0", FROWS, "xyz"), ("F1", FROWS, "xyz"), ("F2", FROWS, "yxz"), ("F3", FROWS, "yz"), ("O", OROWS, "yz"))
+
+
+PLAN = {
+    ("g", 0): ((0, 0),),
+    ("f", 1): ((0, 1),),
+    ("g", 1): ((1, 0),),
+    ("f", 2): ((1, 1),),
+    ("g", 2): ((2, 0),),
+    ("f", 3): ((0, 2), (2, 1),),
+    ("g", 3): ((3, 0),),
+    ("c", 0): ((1, 2), (9, 0),),
+    ("c", 1): ((3, 1), (0, 3), (9, 1),),
+    "go": ((4, 0), (9, 2),),
+    ("d", 0): ((4, 1), (2, 2), (9, 3),),
+    ("D", 0): ((0, 4), (1, 3), (9, 4),),
+    ("e", 0): ((9, 5),),
+    ("q", 0): ((5, 0), (2, 3),),
+    ("d", 1): ((3, 2), (0, 5), (5, 1), (9, 6),),
+    ("D", 1): ((4, 2), (1, 4), (9, 7),),
+    ("e", 1): ((2, 4), (5, 2),),
+    ("q", 1): ((6, 0),),
+    ("d", 2): ((6, 1),),
+    ("D", 2): ((3, 3),),
+    ("e", 2): ((4, 3),),
+    ("q", 2): ((7, 0), (6, 2), (3, 4), (1, 5),),
+    ("d", 3): ((4, 4), (7, 1), (2, 5),),
+    ("D", 3): ((5, 3),),
+    ("e", 3): ((6, 3), (7, 2),),
+    ("q", 3): ((8, 0),),
+    ("w", 0): ((8, 1),),
+    ("w", 1): ((3, 5),),
+    ("w", 2): ((4, 5),),
+    ("w", 3): ((8, 2),),
+}
 
 
 def dg(a, b, ca, cb):
@@ -40,6 +75,14 @@
 
 def al(v, n):
     return pl.multiple_of(v, n)
+
+
+def chunk_scratch(nz, rows, kind):
+    V = lambda *s: pltpu.VMEM(s, BF16)
+    held = rows if kind == "yz" else rows // 2
+    return dict(A=V(2, rows, 128), B=V(held if kind == "xyz" else rows, 128),
+                X=V(held // nz, 128) if kind == "yz" else V(2 if kind == "xyz" else 1, held, 128),
+                Z=V(nz - 1, held // nz, 128), T=V(held // nz, 128), H=V(held, 128))
 
 
 def scratch(nz):
@@ -56,10 +99,8 @@
         dkv=V(128, 2048, t=F32), xst=V(4, 2, 192, 512), dqt=V(1536, 1024),
         gv=V(4, 16, 128, t=F32), gvr=V(2, 16, 128, t=F32), gvy=V(16, 128, t=F32), gva=V(ne, 16, 128, t=F32),
         gg=V(8, 512, t=F32), gbu=V(4, 8, 512, t=F32),
-        FG=V(4, 4, FROWS, 128), FA=V(4, 2, FROWS, 128), FB=V(4, FROWS, 128), FX=V(4, FROWS // 2, 128),
-        FZ=V(4, nz - 1, FROWS // ne, 128), FT=V(4, FROWS // ne, 128), FH=V(4, FROWS // 2, 128),
-        OG=V(1, 4, OROWS, 128), OA=V(1, 2, OROWS, 128), OB=V(1, OROWS, 128), OX=V(1, OROWS // 2, 128),
-        OZ=V(1, nz - 1, OROWS // ne, 128), OT=V(1, OROWS // ne, 128), OH=V(1, OROWS // 2, 128),
+        FG=V(4, 4, FROWS, 128), OG=V(4, OROWS, 128),
+        **{f"{t}{q}": v for t, rows, kind in CHUNKS for q, v in chunk_scratch(nz, rows, kind).items()},
         QS=V(4, 4, 192, 128), QG=V(4, 2, QROWS, 128), QB=V(4, QROWS, 128), QC=V(4, ne - 1, QROWS // ne, 128),
         QT=V(4, QROWS // ne, 128),
     )
@@ -144,8 +185,8 @@
     m.gv[...] = jnp.zeros_like(m.gv)
     pl.semaphore_wait(bar, len(peers) + jnp.where(stay, 0, 1))
 
-    def swap(src, dst_, i, t, what):
-        rows = pl.ds(al(t * 256, 256), 256)
+    def swap(src, dst_, i, t, what, n=256):
+        rows = pl.ds(al(t * n, n), n)
 
         @pl.when(stay)
         def _():
@@ -157,7 +198,7 @@
             cp = remote(src.at[rows], dst_.at[rows], sw, i + t)
             cp.start() if what == "start" else cp.wait()
 
-    ix, idy, iy, iw = ct.take(4), ct.take(4), ct.take(4), ct.take(4)
+    ix, idy, iy, iw = ct.take(4), ct.take(4), ct.take(8), ct.take(8)
     for t in range(4):
         swap(words_h, m.xs, ix, t, "start")
     so_x = remote(m.so.at[0], m.so.at[1], sib, ct.take())
@@ -181,49 +222,44 @@
                 m.wt[r + 192:r + 256, mine] = blk[64:]
 
     other = 2 * oy + c
-    hs = g % 2
-    sl = dict(
-        wt=lambda s, f=None: m.wt.at[:, pl.ds(al(s * 128, 128), 128)],
-        wo=lambda s, f=None: m.wo.at[pl.ds(al(s * 128, 128), 128), :],
-        wu=lambda s, f=None: m.wu.at[:, pl.ds(al(s * 128, 128), 128), :] if f is None else
-        m.wu.at[pl.ds(2 * f, 2), pl.ds(al(s * 128, 128), 128), :],
-        wd=lambda s, f=None: m.wd.at[:, pl.ds(al(s * 128, 128), 128), :] if f is None else
-        m.wd.at[pl.ds(2 * f, 2), pl.ds(al(s * 128, 128), 128), :])
-    gath = {}
-    for n in ("wt", "wo"):
-        gath[n] = [remote(sl[n](w), sl[n](w), sib, ct.take()), remote(sl[n](w), sl[n](w), yn, ct.take()),
-                   remote(sl[n](other), sl[n](other), sib, ct.take())]
-    for n in ("wu", "wd"):
-        gath[n] = [remote(sl[n](w), sl[n](w), sib, ct.take()), remote(sl[n](w, hs), sl[n](w, hs), yn, ct.take()),
-                   remote(sl[n](other, hs), sl[n](other, hs), zp, ct.take()),
-                   remote(sl[n](other), sl[n](other), sib, ct.take())]
-
-    def g_start(n):
-        gath[n][0].start()
-        gath[n][1].start()
-
-    def g_z(n):
-        gath[n][1].wait_recv()
-        gath[n][2].start()
-
-    def g_forward(n):
-        gath[n][-2].wait_recv()
-        gath[n][-1].start()
-
-    def g_done(n):
-        gath[n][0].wait()
-        gath[n][1].wait_send()
-        if len(gath[n]) == 4:
-            gath[n][2].wait_send()
-        gath[n][-1].wait()
-
-    g_start("wt")
+
+    def shard(n, s, f):
+        v = pl.ds(al(s * 128, 128), 128)
+        if n == "wt":
+            return m.wt.at[:, v]
+        if n == "wo":
+            return m.wo.at[v, :]
+        return (m.wu if n == "wu" else m.wd).at[f, v, :]
+
+    pieces = [("wt", 0), ("wo", 0)] + [(n, f) for f in range(4) for n in ("wu", "wd")]
+    ig = {p: ct.take(3) for p in pieces}
+
+    def g_sib(p):
+        return remote(shard(p[0], w, p[1]), shard(p[0], w, p[1]), sib, ig[p])
+
+    def g_y(p):
+        return remote(shard(p[0], w, p[1]), shard(p[0], w, p[1]), yn, ig[p] + 1)
+
+    def g_fwd(p):
+        return remote(shard(p[0], other, p[1]), shard(p[0], other, p[1]), sib, ig[p] + 2)
+
+    def g_forward(*ps):
+        for p in ps:
+            g_y(p).wait_recv()
+            g_fwd(p).start()
+
+    g_y(("wt", 0)).start()
+    g_sib(("wt", 0)).start()
     l_wu.wait()
     for f in range(4):
         for s in range(4):
             m.wu[f, mine, s * 128:(s + 1) * 128] = m.wur[:, s * 512 + f * 128:s * 512 + (f + 1) * 128]
     l_wo.wait()
     l_wd.wait()
+    for p in pieces[1:]:
+        g_y(p).start()
+    for p in pieces[1:]:
+        g_sib(p).start()
     for v in vcs:
         v.wait()
     so_x.wait()
@@ -256,23 +292,35 @@
 
     wrows = pl.ds(al(c * 768, 256), 768)
 
-    def project(t, _=0):
-        a_piece(t).wait()
+    near, far = pl.ds(al(yi * 256, 256), 256), pl.ds(al(oy * 256, 256), 256)
+    part_of = (m.ya, m.da)
+
+    def words_of(t, feats):
+        half = pl.ds(al((t % 2) * 256, 256), 256)
+        return jnp.concatenate([m.a1[t // 2, half, feats], m.a1[2 + t // 2, half, feats]], axis=0)
+
+    def project(t, part=None):
         cols = pl.ds(al((t % 2) * 256, 256), 256)
-        av = jnp.concatenate([a_slot(0, t)[...], a_slot(1, t)[...]], axis=0)
-        res = dg(m.wt[wrows, :], av, 1, 1).astype(BF16)
+        res = dg(m.wt[wrows, far], words_of(t, far), 1, 1)
+        res = res + (dg(m.wt[wrows, near], words_of(t, near), 1, 1) if part is None else part[0:768, :])
+        res = res.astype(BF16)
         m.qkv[t // 2, :, cols] = res[:, :256]
         m.qkv[2 + t // 2, :, cols] = res[:, 256:]
-        return 0
-
-    lax.fori_loop(0, 3, norm1, 0)
-    g_forward("wt")
-    g_start("wo")
-    g_start("wu")
-    g_done("wt")
-    lax.fori_loop(0, 2, project, 0)
+
+    norm1(0)
+    g_sib(("wt", 0)).wait()
+    for t in range(2):
+        norm1(t + 1)
+        a_piece(t).wait()
+        part_of[t][0:768, :] = dg(m.wt[wrows, near], words_of(t, near), 1, 1)
+    g_forward(("wt", 0))
+    g_fwd(("wt", 0)).wait()
+    project(0, m.ya)
+    project(1, m.da)
     norm1(3)
-    lax.fori_loop(2, 4, project, 0)
+    for t in range(2, 4):
+        a_piece(t).wait()
+        project(t)
     for t in range(4):
         swap(cot_h, m.dys, idy, t, "start")
     so_s.wait()
@@ -313,16 +361,15 @@
 
         @pl.when(h == 0)
         def _():
-            g_forward("wo")
-            g_start("wd")
+            g_forward(*pieces[1:4])
 
         @pl.when(h == 2)
         def _():
-            g_z("wu")
+            g_forward(*pieces[4:6])
 
         @pl.when(h == 3)
         def _():
-            g_z("wd")
+            g_forward(*pieces[6:8])
         return 0
 
     lax.fori_loop(0, 4, fwd_head, 0)
@@ -334,91 +381,151 @@
         oxc.append(cp)
     for b in range(2):
         m.ot[b, pl.ds(al(c * 256, 256), 256), :] = m.o[canon_of(2 * c + b)].astype(BF16)
-    g_forward("wu")
-    g_done("wo")
+    g_fwd(("wo", 0)).wait()
+    g_sib(("wo", 0)).wait()
     for cp in oxc:
         cp.wait()
 
     class Chunk:
-        def __init__(self, tag, rows, start, count):
-            for q in "GABXZTH":
+        def __init__(self, k):
+            tag, self.rows, self.kind = CHUNKS[k]
+            self.G = m.FG.at[k] if k < 4 else m.OG
+            for q in "ABXZTH":
                 setattr(self, q, getattr(m, tag + q))
-            self.rows, self.start, self.half, self.p = rows, start, rows // 2, rows // ne
-            self.n = 6 + 2 * nz
-            self.i = ct.take(self.n * count)
-
-        def core(self, k, q):
-            return remote(self.G.at[k, 2 * q + oc], self.A.at[k, q], sib, self.i + k * self.n + q)
-
-        def y(self, k):
-            return remote(self.G.at[k, other], self.B.at[k], yn, self.i + k * self.n + 2)
-
-        def x(self, k):
-            return remote(self.G.at[k, w, pl.ds(al(ox * self.half, 64), self.half), :], self.X.at[k], xn,
-                          self.i + k * self.n + 3)
-
-        def z(self, k, d):
+            self.start = k * FROWS
+            self.held = self.rows if self.kind == "yz" else self.rows // 2
+            self.p = self.held // nz
+            self.lo = 0 if self.kind == "yz" else x * self.held
+            self.slots = (w, other) if self.kind == "xyz" else (w,)
+            self.i = ct.take(8 + 2 * nz)
+
+        def r(self, off, n):
+            return pl.ds(al(off, 16), n)
+
+        def core(self, q):
+            return remote(self.G.at[2 * q + oc], self.A.at[q], sib, self.i + q)
+
+        def y(self):
+            if self.kind == "xyz":
+                return remote(self.G.at[other, self.r(self.lo, self.held), :], self.B, yn, self.i + 2)
+            return remote(self.G.at[other], self.B, yn, self.i + 2)
+
+        def xs(self):
+            if self.kind == "yz":
+                return [remote(self.T, self.X, xn, self.i + 3)]
+            return [remote(self.G.at[v, self.r(ox * self.held, self.held), :], self.X.at[n], xn, self.i + 3 + n)
+                    for n, v in enumerate(self.slots)]
+
+        def z(self, d):
             q, dev = zpeer(d)
-            return remote(self.G.at[k, w, pl.ds(al(x * self.half + q * self.p, 16), self.p), :],
-                          self.Z.at[k, nz - 1 - d], dev, self.i + k * self.n + 3 + d)
-
-        def back(self, k, d):
-            return remote(self.T.at[k], self.H.at[k, pl.ds(al(g * self.p, 16), self.p), :], zpeer(d)[1],
-                          self.i + k * self.n + 2 + nz + d)
-
-        def at(self, k):
-            return red_out.at[pl.ds(al(self.start + k * self.rows + x * self.half, 16), self.half), :]
-
-        def xback(self, k):
-            return remote(self.H.at[k], self.at(k), xn, self.i + k * self.n + 2 + 2 * nz)
-
-        def keep(self, k):
-            return local(self.H.at[k], self.at(k), self.i + k * self.n + 3 + 2 * nz)
-
-        def s0(self, k):
+            return remote(self.G.at[w, self.r(self.lo + q * self.p, self.p), :], self.Z.at[nz - 1 - d], dev,
+                          self.i + 4 + d)
+
+        def back(self, d):
+            return remote(self.T, self.H.at[self.r(g * self.p, self.p), :], zpeer(d)[1], self.i + 3 + nz + d)
+
+        def at(self):
+            return red_out.at[self.r(self.start + self.lo, self.held), :]
+
+        def xback(self):
+            return remote(self.H, self.at(), xn, self.i + 3 + 2 * nz)
+
+        def keep(self):
+            return local(self.H, self.at(), self.i + 4 + 2 * nz)
+
+        def add(self, slot, rows, v):
+            self.G[slot, rows, :] = (self.G[slot, rows, :].astype(F32) + v.astype(F32)).astype(BF16)
+
+        def begin(self):
             for q in range(2):
-                self.core(k, q).start()
-
-        def s1(self, k):
+                self.core(q).start()
+
+        def add_core(self):
             for q in range(2):
-                self.core(k, q).wait()
-            self.G[k, other] = (self.G[k, other].astype(F32) + self.A[k, oy].astype(F32)).astype(BF16)
-            self.y(k).start()
-            self.G[k, w] = (self.G[k, w].astype(F32) + self.A[k, yi].astype(F32)).astype(BF16)
-
-        def s2(self, k):
-            self.y(k).wait()
-            self.G[k, w] = (self.G[k, w].astype(F32) + self.B[k].astype(F32)).astype(BF16)
-            self.x(k).start()
-
-        def s3(self, k):
-            self.x(k).wait()
-            hrows = pl.ds(al(x * self.half, 64), self.half)
-            self.G[k, w, hrows, :] = (self.G[k, w, hrows, :].astype(F32) + self.X[k].astype(F32)).astype(BF16)
+                self.core(q).wait()
+            whole = slice(0, self.rows)
+            self.add(other, whole, self.A[oy])
+            if self.kind != "xyz":
+                self.y().start()
+            self.add(w, whole, self.A[yi])
+            if self.kind == "xyz":
+                self.x_go()
+
+        def x_go(self):
+            for cp in self.xs():
+                cp.start()
+
+        def x_add(self):
+            for cp in self.xs():
+                cp.wait()
+            for n, v in reversed(list(enumerate(self.slots))):
+                self.add(v, self.r(self.lo, self.held), self.X[n])
+                if n == 1:
+                    self.y().start()
+
+        def y_add(self):
+            self.y().wait()
+            if self.kind == "xyz":
+                self.add(w, self.r(self.lo, self.held), self.B[...])
+            else:
+                self.add(w, slice(0, self.rows), self.B[...])
+
+        def z_go(self):
             for d in range(1, nz):
-                self.z(k, d).start()
-
-        def s4(self, k):
+                self.z(d).start()
+
+        def z_sum(self):
             for d in range(1, nz):
-                self.z(k, d).wait()
-            tot = self.G[k, w, pl.ds(al(x * self.half + g * self.p, 16), self.p), :].astype(F32)
+                self.z(d).wait()
+            tot = self.G[w, self.r(self.lo + g * self.p, self.p), :].astype(F32)
             for d in range(nz - 1):
-                tot = tot + self.Z[k, d].astype(F32)
-            tot = tot.astype(BF16)
-            self.T[k] = tot
-            self.H[k, pl.ds(al(g * self.p, 16), self.p), :] = tot
+                tot = tot + self.Z[d].astype(F32)
+            return tot.astype(BF16)
+
+        def z_back(self, tot):
+            self.T[...] = tot
+            self.H[self.r(g * self.p, self.p), :] = tot
             for d in range(1, nz):
-                self.back(k, d).start()
-
-        def s5(self, k):
-            for d in range(1, nz):
-                self.back(k, d).wait()
-            self.xback(k).start()
-            self.keep(k).start()
-
-        def s6(self, k):
-            self.xback(k).wait()
-            self.keep(k).wait()
+                self.back(d).start()
+
+        def step(self, n):
+            if n == 0:
+                self.begin()
+            elif n == 1:
+                self.add_core()
+            elif n == 2:
+                if self.kind == "xyz":
+                    self.x_add()
+                else:
+                    self.y_add()
+                    self.x_go() if self.kind == "yxz" else self.z_go()
+            elif n == 3:
+                if self.kind == "xyz":
+                    self.y_add()
+                    self.z_go()
+                elif self.kind == "yxz":
+                    self.x_add()
+                    self.z_go()
+                else:
+                    self.T[...] = self.z_sum()
+                    self.x_go()
+            elif n == 4:
+                if self.kind == "yz":
+                    for cp in self.xs():
+                        cp.wait()
+                    self.z_back((self.T[...].astype(F32) + self.X[...].astype(F32)).astype(BF16))
+                else:
+                    self.z_back(self.z_sum())
+            elif n == 5:
+                for d in range(1, nz):
+                    self.back(d).wait()
+                if self.kind != "yz":
+                    self.xback().start()
+                self.keep().start()
+            else:
+                if self.kind != "yz":
+                    self.xback().wait()
+                self.keep().wait()
 
     qi = ct.take(4 * (4 + 2 * ne))
     qn, qp = 4 + 2 * ne, QROWS // ne
@@ -475,8 +582,24 @@
             q_ag(k, d).wait()
         q_keep(k).wait()
 
-    FC = Chunk("F", FROWS, 0, 4)
-    OC = Chunk("O", OROWS, OSTART, 1)
+    chunks = [Chunk(k) for k in range(5)]
+    chain = (q0, q1, q2, q3, q4)
+
+    def events(key):
+        for k, n in PLAN.get(key, ()):
+            if k == 9:
+                swap(m.dup, y_out, iy, n, "start", 128)
+            elif k < 5:
+                chunks[k].step(n)
+            else:
+                chain[n](k - 5)
+
+    def when_events(tag, v, values):
+        for u in values:
+            if (tag, u) in PLAN:
+                @pl.when(v == u)
+                def _():
+                    events((tag, u))
 
     g2, b2, bd = row(2), row(3), row(4)
 
@@ -501,9 +624,12 @@
         return 0
 
     lax.fori_loop(0, 2, c1, 0)
-    g_forward("wd")
-    g_done("wu")
-    g_done("wd")
+    g_forward(*pieces[8:])
+    for p in pieces[2:]:
+        g_sib(p).wait()
+        g_fwd(p).wait()
+    for p in pieces:
+        g_y(p).wait_send()
 
     def c2(f, _):
         bu = jnp.concatenate([m.vec[s, pl.ds(5 + f, 1), :] for s in range(4)], axis=1)
@@ -522,14 +648,7 @@
         m.gbu[f, 0:1, :] = colsum(dv.astype(F32))
         m.da[...] += dg(dv, wuf, 1, 1)
 
-        @pl.when(f > 0)
-        def _():
-            FC.s1(f - 1)
-
-        @pl.when(f == 3)
-        def _():
-            FC.s2(0)
-
+        when_events("f", f, range(4))
         gd = dg(m.dyt[...], m.act[...], 1, 0).astype(BF16)
         for s in range(4):
             m.FG[f, s, 0:512, :] = gd[:, s * 128:(s + 1) * 128]
@@ -537,7 +656,7 @@
         for s in range(4):
             for b in range(4):
                 m.FG[f, s, 512 + b * 128:640 + b * 128, :] = gu[s * 128:(s + 1) * 128, b * 128:(b + 1) * 128]
-        FC.s0(f)
+        when_events("g", f, range(4))
         return 0
 
     lax.fori_loop(0, 4, c2, 0)
@@ -550,8 +669,6 @@
     def c3(t, _):
         rows = pl.ds(al(t * 512, 512), 512)
         yst[rows, :] = m.ya[rows, :].astype(BF16)
-        for u in range(2):
-            swap(yst, y_out, iy, 2 * t + u, "start")
         dav, nv, r = m.da[rows, :], m.n2[rows, :], m.rs[rows, 0:1]
         m.gg[2:3, :] += colsum(dav * nv)
         m.gg[3:4, :] += colsum(dav)
@@ -563,19 +680,15 @@
         d_piece(t).start()
         m.do[2 * c + t] = dg(m.wo[pl.ds(al(c * 256, 256), 256), :], dm, 1, 1).astype(BF16)
 
-        @pl.when(t == 0)
-        def _():
-            FC.s1(3)
+        when_events("c", t, range(2))
         return 0
 
     lax.fori_loop(0, 2, c3, 0)
     go = (dg(m.ot[0], dmid[0:512, :], 1, 0) + dg(m.ot[1], dmid[512:1024, :], 1, 0)).astype(BF16)
     for s in range(4):
         for b in range(4):
-            m.OG[0, s, b * 128:(b + 1) * 128, :] = go[s * 128:(s + 1) * 128, b * 128:(b + 1) * 128]
-    OC.s0(0)
-    FC.s2(1)
-    FC.s3(0)
+            m.OG[s, b * 128:(b + 1) * 128, :] = go[s * 128:(s + 1) * 128, b * 128:(b + 1) * 128]
+    events("go")
     for t in range(2):
         d_piece(t).wait()
 
@@ -602,7 +715,6 @@
         gq = gq.astype(BF16)
         for s in range(4):
             m.QS[h, s] = gq[:, s * 128:(s + 1) * 128]
-        q0(h)
 
     def bwd_head(h, _):
         hr = pl.ds(al(h * HD, HD), HD)
@@ -632,96 +744,41 @@
             else:
                 m.dkv[0:64, :L] += dk
                 m.dkv[64:128, :L] += dv
+            if i in (6, 4):
+                when_events("dD"[i == 4], h, range(4))
         for j in range(4):
             m.dq[j, rows_of(h, 1), :] = m.dkv[0:64, j * BLK:(j + 1) * BLK].astype(BF16)
             m.dq[j, rows_of(h, 2), :] = m.dkv[64:128, j * BLK:(j + 1) * BLK].astype(BF16)
         x_start(h)
+        when_events("e", h, range(4))
         q_grad(h)
-
-        @pl.when(h > 0)
-        def _():
-            FC.s5(h - 1)
-            q1(h - 1)
-
-        FC.s4(h)
-
-        @pl.when(h < 3)
-        def _():
-            FC.s3(h + 1)
-
-        @pl.when(h < 2)
-        def _():
-            FC.s2(h + 2)
-
-        @pl.when(h > 1)
-        def _():
-            q2(h - 2)
-
-        @pl.when(h == 0)
-        def _():
-            OC.s1(0)
-
-        @pl.when(h == 1)
-        def _():
-            OC.s2(0)
-
-        @pl.when(h == 2)
-        def _():
-            OC.s3(0)
-
-        @pl.when(h == 3)
-        def _():
-            OC.s4(0)
-            q3(0)
+        when_events("q", h, range(4))
         return 0
 
     lax.fori_loop(0, 4, bwd_head, 0)
 
-    def e0(t, _):
+    def x_wait(h, _):
+        for b in range(2):
+            x_piece(h, b).wait()
+        return 0
+
+    lax.fori_loop(0, 4, x_wait, 0)
+    wgst = m.dys
+
+    def e1(t, _):
         rows = pl.ds(al(t * 256, 256), 256)
         xv = m.xs[rows, :].astype(F32)
         xc = xv - rowmean(xv)
         r = lax.rsqrt(rowmean(xc * xc) + EPS)
-        m.n2[rows, :] = xc * r
-        m.rs[rows, :] = jnp.broadcast_to(r, (256, 128))
-        return 0
-
-    lax.fori_loop(0, 4, e0, 0)
-    q1(3)
-
-    def x_wait(h, _):
-        for b in range(2):
-            x_piece(h, b).wait()
-        return 0
-
-    lax.fori_loop(0, 4, x_wait, 0)
-    wgst = m.dys
-
-    def e1(t, _):
-        rows = pl.ds(al(t * 256, 256), 256)
+        nv = xc * r
         dav = dg(m.dqt[:, rows], m.wt[...], 0, 0)
-        nv, r = m.n2[rows, :], m.rs[rows, 0:1]
         m.gg[0:1, :] += colsum(dav * nv)
         m.gg[1:2, :] += colsum(dav)
         gr = dav * g1
         dn = r * (gr - rowmean(gr) - nv * rowmean(gr * nv))
         wgst[rows, :] = (dmid[rows, :].astype(F32) + dn).astype(BF16)
-        swap(wgst, wg_out, iw, t, "start")
-
-        @pl.when(t == 0)
-        def _():
-            q2(2)
-            q3(1)
-
-        @pl.when(t == 1)
-        def _():
-            FC.s5(3)
-            OC.s5(0)
-
-        @pl.when(t == 2)
-        def _():
-            q2(3)
-            q3(2)
+        swap(wgst, wg_out, iw, t, "start", 128)
+        when_events("w", t, range(4))
         return 0
 
     lax.fori_loop(0, 4, e1, 0)
@@ -736,30 +793,36 @@
     va = [remote(m.gv.at[w], m.gva.at[e], peer(d)[1], iv + d - 1) for d in range(1, ne)]
     for cp in vx:
         cp.start()
+    for t in range(4, 6):
+        swap(wgst, wg_out, iw, t, "start", 128)
     for cp in vx:
         cp.wait()
     for q in range(2):
         m.gv[2 * q + c] = m.gv[2 * q + c] + m.gvr[q]
     vy.start()
-    q3(3)
+    q3(2)
     vy.wait()
     m.gv[w] = m.gv[w] + m.gvy[...]
     m.gva[e] = m.gv[w]
     for cp in va:
         cp.start()
+    q3(3)
+    for t in range(6, 8):
+        swap(wgst, wg_out, iw, t, "start", 128)
     for cp in va:
         cp.wait()
     tot = m.gva[0]
     for d in range(1, ne):
         tot = tot + m.gva[d]
     vec_out[...] = tot
-    OC.s6(0)
+    for k in range(5):
+        chunks[k].step(6)
 
     def fin(t, _):
-        FC.s6(t)
         q4(t)
-        swap(yst, y_out, iy, t, "wait")
-        swap(wgst, wg_out, iw, t, "wait")
+        for u in range(2):
+            swap(m.dup, y_out, iy, 2 * t + u, "wait", 128)
+            swap(wgst, wg_out, iw, 2 * t + u, "wait", 128)
         return 0
 
     lax.fori_loop(0, 4, fin, 0)

time: 146 us -> 137 us (0.938)
  Pallas kernels: 145 us -> 136 us
    pallas_call x1, Pallas kernels: 140 us -> 130 us  [layer(): pl.pallas_call(functools.partial(body, nz, names), out_shape=(sd((1024, 5...]
where the time goes in v3:
time: 137 us; the launch traced here: 136 us
  Pallas kernels  136 us (99%)
    pallas_call x1, Pallas kernels, layer(): pl.pallas_call(functools.partial(body, nz, names), out_shape=(sd((1024, 5...  130 us
    pallas_call x1, Pallas kernels, finish(): pl.pallas_call(finish_body, out_shape=(sd((1024, 512), BF16), sd((1024, 5...  5.14 us

profile of v3, /device:TPU:0, one launch (start us, length us, event | category | flops | bytes accessed | tf_op | source)
XLA Modules:
  0.0 136.4 jit_solution(4118224613931698501)
XLA Ops:
  0.6 130.5 %layer.1 = (bf16[1024,512]{1,0:T(8,128)(2,1)}, bf16[1024,512]{1,0:T(8,128)(2,1)}, bf16[6144,128]{1,0:T(8,128)(2,1)}, f32[16,128]{1,0:T(8,128)}) custom-call(bf16[1024,512]{1,0:T(8,128)(2,1)} %bitcast.17, bf16[1024,512]{1,0:T(8,128)(2,1)} %bitcast.18, bf16[128,1536]{1,0:T(8,128)(2,1)} %args_2_.4, bf16[128,512]{1,0:T(8,128)(2,1)} %args_3_.4, ...), custom_call_target="tpu_custom_call" | custom-call | tf_op jit(solution)/shard_map/layer/pallas_call | solution.py:837
  131.1 5.1 %finish.1 = (bf16[1024,512]{1,0:T(8,128)(2,1)}, f32[1024,512]{1,0:T(8,128)}, f32[128,1536]{1,0:T(8,128)}, f32[128,512]{1,0:T(8,128)}, f32[128,2048]{1,0:T(8,128)...) custom-call(bf16[1024,512]{1,0:T(8,128)(2,1)} %get-tuple-element.28., ...), custom_call_target="tpu_custom_call" | custom-call | tf_op jit(solution)/shard_map/finish/pallas_call | solution.py:918

commit v4 on v3

--- a/solution.py
+++ b/solution.py
@@ -17,8 +17,8 @@
 VLIM = 63 * 1024 * 1024
 FROWS, OROWS, QROWS = 1024, 512, 384
 OSTART, QSTART, ROWS = 4096, 4608, 6144
-NSEM = 280
-CHUNKS = (("F0", FROWS, "xyz"), ("F1", FROWS, "xyz"), ("F2", FROWS, "yxz"), ("F3", FROWS, "yz"), ("O", OROWS, "yz"))
+NSEND, NRECV = 64, 96
+CHUNKS = (("F0", FROWS, "yxz"), ("F1", FROWS, "yxz"), ("F2", FROWS, "yxz"), ("F3", FROWS, "yxz"), ("O", OROWS, "yxz"))
 
 
 PLAN = {
@@ -32,26 +32,25 @@
     ("c", 0): ((1, 2), (9, 0),),
     ("c", 1): ((3, 1), (0, 3), (9, 1),),
     "go": ((4, 0), (9, 2),),
-    ("d", 0): ((4, 1), (2, 2), (9, 3),),
-    ("D", 0): ((0, 4), (1, 3), (9, 4),),
-    ("e", 0): ((9, 5),),
-    ("q", 0): ((5, 0), (2, 3),),
-    ("d", 1): ((3, 2), (0, 5), (5, 1), (9, 6),),
-    ("D", 1): ((4, 2), (1, 4), (9, 7),),
-    ("e", 1): ((2, 4), (5, 2),),
+    ("d", 0): ((2, 2), (1, 3), (4, 1), (0, 4), (9, 3),),
+    ("D", 0): ((9, 4),),
+    ("e", 0): ((3, 2), (9, 5),),
+    ("q", 0): ((5, 0), (2, 3), (1, 4), (4, 2),),
+    ("d", 1): ((5, 1), (0, 5), (9, 6),),
+    ("D", 1): ((3, 3), (2, 4), (9, 7),),
+    ("e", 1): ((4, 3), (5, 2), (1, 5),),
     ("q", 1): ((6, 0),),
-    ("d", 2): ((6, 1),),
-    ("D", 2): ((3, 3),),
-    ("e", 2): ((4, 3),),
-    ("q", 2): ((7, 0), (6, 2), (3, 4), (1, 5),),
-    ("d", 3): ((4, 4), (7, 1), (2, 5),),
-    ("D", 3): ((5, 3),),
-    ("e", 3): ((6, 3), (7, 2),),
-    ("q", 3): ((8, 0),),
+    ("d", 2): ((3, 4), (6, 1),),
+    ("D", 2): ((2, 5), (4, 4),),
+    ("e", 2): ((5, 3), (6, 2),),
+    ("q", 2): ((7, 0),),
+    ("d", 3): ((3, 5), (7, 1), (4, 5),),
+    ("e", 3): ((6, 3),),
+    ("q", 3): ((8, 0), (7, 2),),
     ("w", 0): ((8, 1),),
-    ("w", 1): ((3, 5),),
-    ("w", 2): ((4, 5),),
+    ("w", 2): ((7, 3),),
     ("w", 3): ((8, 2),),
+    "tail": ((8, 3),),
 }
 
 
@@ -91,7 +90,8 @@
     return dict(
         xs=V(1024, 512), dys=V(1024, 512), wqr=V(128, 1536), wur=V(128, 2048), wt=V(1536, 512), wo=V(512, 512),
         wu=V(4, 512, 512), wd=V(4, 512, 512), vown=V(16, 128, t=F32), vec=V(4, 16, 128, t=F32),
-        so=V(2, 8, 128, t=jnp.int32), sm=pltpu.SMEM((8, 128), jnp.int32),
+        so=V(2, 8, 128, t=jnp.int32), sseg=V(1, 4, t=jnp.int32), soff=V(1, 4, t=jnp.int32),
+        s1g=V(1, 128), s1b=V(1, 128), s2g=V(1, 128), s2b=V(1, 128), sbd=V(1, 128), sbu=V(4, 128), sm=pltpu.SMEM((8, 128), jnp.int32),
         a1=V(4, 512, 512), qkv=V(4, 768, 512), o=V(4, 256, 512, t=F32), lse=V(4, 8, 512, t=F32),
         ost=V(2, 256, 512), ot=V(2, 512, 512), n2=V(1024, 512, t=F32), rs=V(1024, 128, t=F32), a2=V(1024, 512),
         a2t=V(512, 1024), dyt=V(512, 1024), ya=V(1024, 512, t=F32), da=V(1024, 512, t=F32),
@@ -107,12 +107,12 @@
 
 
 class Count:
-    def __init__(self):
-        self.n = 0
+    def __init__(self, most):
+        self.n, self.most = 0, most
 
     def take(self, k=1):
         self.n += k
-        assert self.n <= NSEM
+        assert self.n <= self.most
         return self.n - k
 
 
@@ -126,7 +126,7 @@
     y_out, wg_out, red_out, vec_out = args[14:18]
     m = Ns(dict(zip(names, args[18:18 + len(names)])))
     send, recv = args[18 + len(names):]
-    ct = Count()
+    cs, cr = Count(NSEND), Count(NRECV)
     ne = 2 * nz
     g, x, w = lax.axis_index("group"), lax.axis_index("ctx"), lax.axis_index("wshard")
     yi, c = w // 2, w % 2
@@ -149,22 +149,24 @@
         q = (g + d) % nz
         return q, (q, x, w)
 
-    def remote(src, dst_, dev, i):
-        return pltpu.make_async_remote_copy(src_ref=src, dst_ref=dst_, send_sem=send.at[i], recv_sem=recv.at[i],
+    def remote(src, dst_, dev, i, j):
+        return pltpu.make_async_remote_copy(src_ref=src, dst_ref=dst_, send_sem=send.at[i], recv_sem=recv.at[j],
                                             device_id=dev, device_id_type=MESH)
 
     def local(src, dst_, i):
         return pltpu.make_async_copy(src, dst_, send.at[i])
 
+    def sent(ref, i):
+        pltpu.make_async_copy(ref, ref, send.at[i]).wait()
+
+    def got(ref, j):
+        pltpu.make_async_copy(ref, ref, recv.at[j]).wait()
+
     def begin(src, dst_):
-        cp = local(src, dst_, ct.take())
+        cp = local(src, dst_, cs.take())
         cp.start()
         return cp
 
-    l_wq = begin(wq_h, m.wqr)
-    l_wo = begin(wo_h, m.wo.at[pl.ds(al(w * 128, 128), 128), :])
-    l_wu = begin(wu_h, m.wur)
-    l_wd = begin(wd_h, m.wd.at[:, pl.ds(al(w * 128, 128), 128), :])
     bar = pltpu.get_barrier_semaphore()
     peers = [sib, yn, diag] + [peer(d)[1] for d in range(1, ne)]
     for p in peers:
@@ -174,38 +176,52 @@
     def _():
         pl.semaphore_signal(bar, inc=1, device_id=sw, device_id_type=MESH)
 
+    l_wq = begin(wq_h, m.wqr)
+    l_small = [begin(a, b) for a, b in zip((n1g, n1b, n2g, n2b, bdr, bur, seg_r, off_r),
+                                           (m.s1g, m.s1b, m.s2g, m.s2b, m.sbd, m.sbu, m.sseg, m.soff))]
+    l_wo = begin(wo_h, m.wo.at[pl.ds(al(w * 128, 128), 128), :])
+    l_wu = begin(wu_h, m.wur)
+    l_wd = begin(wd_h, m.wd.at[:, pl.ds(al(w * 128, 128), 128), :])
     m.vown[...] = jnp.zeros_like(m.vown)
-    for k, r in enumerate((n1g, n1b, n2g, n2b, bdr)):
-        m.vown[k:k + 1, :] = r[...].astype(F32)
-    m.vown[5:9, :] = bur[...].astype(F32)
     m.so[0] = jnp.zeros((8, 128), jnp.int32)
-    m.so[0, 0:1, 0:4] = seg_r[...] * 2 + off_r[...]
     m.gg[...] = jnp.zeros_like(m.gg)
     m.gbu[...] = jnp.zeros_like(m.gbu)
     m.gv[...] = jnp.zeros_like(m.gv)
     pl.semaphore_wait(bar, len(peers) + jnp.where(stay, 0, 1))
 
-    def swap(src, dst_, i, t, what, n=256):
+    def swap_go(src, dst_, ij, t, n, k=0):
         rows = pl.ds(al(t * n, n), n)
 
         @pl.when(stay)
         def _():
-            cp = local(src.at[rows], dst_.at[rows], i + t)
-            cp.start() if what == "start" else cp.wait()
+            local(src.at[rows], dst_.at[rows], ij[0] + k).start()
 
         @pl.when(moves)
         def _():
-            cp = remote(src.at[rows], dst_.at[rows], sw, i + t)
-            cp.start() if what == "start" else cp.wait()
-
-    ix, idy, iy, iw = ct.take(4), ct.take(4), ct.take(8), ct.take(8)
+            remote(src.at[rows], dst_.at[rows], sw, ij[0] + k, ij[1] + k).start()
+
+    def swap_wait(ref, ij, k=0):
+        sent(ref, ij[0] + k)
+
+        @pl.when(moves)
+        def _():
+            got(ref, ij[1] + k)
+
+    def pair(k=1):
+        return cs.take(k), cr.take(k)
+
+    ix, idy, iy, iw = pair(4), pair(), pair(), pair()
     for t in range(4):
-        swap(words_h, m.xs, ix, t, "start")
-    so_x = remote(m.so.at[0], m.so.at[1], sib, ct.take())
-    so_x.start()
-    vcs = [remote(m.vown, m.vec.at[w], p, ct.take()) for p in (sib, yn, diag)]
-    for v in vcs:
-        v.start()
+        swap_go(words_h, m.xs, ix, t, 256, t)
+    for cp in l_small:
+        cp.wait()
+    for k, r in enumerate((m.s1g, m.s1b, m.s2g, m.s2b, m.sbd)):
+        m.vown[k:k + 1, :] = r[...].astype(F32)
+    m.vown[5:9, :] = m.sbu[...].astype(F32)
+    m.so[0, 0:1, 0:4] = m.sseg[...] * 2 + m.soff[...]
+    so_x = remote(m.so.at[0], m.so.at[1], sib, *pair())
+    ivc = pair()
+    vcs = [remote(m.vown, m.vec.at[w], p, *ivc) for p in (sib, yn, diag)]
     m.vec[w] = m.vown[...]
 
     mine = pl.ds(al(w * 128, 128), 128)
@@ -232,24 +248,40 @@
         return (m.wu if n == "wu" else m.wd).at[f, v, :]
 
     pieces = [("wt", 0), ("wo", 0)] + [(n, f) for f in range(4) for n in ("wu", "wd")]
-    ig = {p: ct.take(3) for p in pieces}
+    big2 = m.wu.at[0:2, 0:128, :]
+    big8 = m.wu.at[:, 0:256, :]
+    ig = dict(wt=(pair(3)), wo=(pair(3)))
+    isib, iys, ifs = pair(), cs.take(), cs.take()
+    iyr, ifr = cr.take(4), cr.take(4)
+
+    def g_sems(p, k):
+        n, f = p
+        if n in ig:
+            return ig[n][0] + k, ig[n][1] + k
+        return (isib, (iys, iyr + f), (ifs, ifr + f))[k]
 
     def g_sib(p):
-        return remote(shard(p[0], w, p[1]), shard(p[0], w, p[1]), sib, ig[p])
+        return remote(shard(p[0], w, p[1]), shard(p[0], w, p[1]), sib, *g_sems(p, 0))
 
     def g_y(p):
-        return remote(shard(p[0], w, p[1]), shard(p[0], w, p[1]), yn, ig[p] + 1)
+        return remote(shard(p[0], w, p[1]), shard(p[0], w, p[1]), yn, *g_sems(p, 1))
 
     def g_fwd(p):
-        return remote(shard(p[0], other, p[1]), shard(p[0], other, p[1]), sib, ig[p] + 2)
+        return remote(shard(p[0], other, p[1]), shard(p[0], other, p[1]), sib, *g_sems(p, 2))
 
     def g_forward(*ps):
         for p in ps:
-            g_y(p).wait_recv()
+            if p[0] in ig:
+                g_y(p).wait_recv()
+            elif p[0] == "wu":
+                got(big2, iyr + p[1])
             g_fwd(p).start()
 
     g_y(("wt", 0)).start()
     g_sib(("wt", 0)).start()
+    for v in vcs:
+        v.start()
+    so_x.start()
     l_wu.wait()
     for f in range(4):
         for s in range(4):
@@ -260,11 +292,11 @@
         g_y(p).start()
     for p in pieces[1:]:
         g_sib(p).start()
-    for v in vcs:
-        v.wait()
+    sent(m.vec.at[0:3], ivc[0])
+    got(m.vec.at[0:3], ivc[1])
     so_x.wait()
     m.so[0] = jnp.where(stay, m.so[0], m.so[1])
-    so_s = local(m.so.at[0], m.sm, ct.take())
+    so_s = local(m.so.at[0], m.sm, cs.take())
     so_s.start()
 
     def row(k):
@@ -272,17 +304,17 @@
 
     g1, b1 = row(0), row(1)
 
-    ia = ct.take(4)
+    ia = pair(4)
 
     def a_slot(core, t):
         return m.a1.at[2 * core + t // 2, pl.ds(al((t % 2) * 256, 256), 256), :]
 
     def a_piece(t):
-        return remote(a_slot(c, t), a_slot(c, t), sib, ia + t)
+        return remote(a_slot(c, t), a_slot(c, t), sib, ia[0] + t, ia[1] + t)
 
     def norm1(t, _=0):
         rows = pl.ds(al(t * 256, 256), 256)
-        swap(words_h, m.xs, ix, t, "wait")
+        swap_wait(m.xs.at[rows], ix, t)
         xv = m.xs[rows, :].astype(F32)
         xc = xv - rowmean(xv)
         r = lax.rsqrt(rowmean(xc * xc) + EPS)
@@ -322,7 +354,7 @@
         a_piece(t).wait()
         project(t)
     for t in range(4):
-        swap(cot_h, m.dys, idy, t, "start")
+        swap_go(cot_h, m.dys, idy, t, 256)
     so_s.wait()
     canon = [m.sm[0, b] for b in range(4)]
     phys = [jnp.minimum(sum(jnp.where(canon[b] == k, b, 0) for b in range(1, 4)), 3) for k in range(4)]
@@ -373,18 +405,16 @@
         return 0
 
     lax.fori_loop(0, 4, fwd_head, 0)
-    oxc = []
+    iox = pair()
     for b in range(2):
         m.ost[b] = m.o[canon_of(2 * oc + b)].astype(BF16)
-        cp = remote(m.ost.at[b], m.ot.at[b, pl.ds(al(c * 256, 256), 256), :], sib, ct.take())
-        cp.start()
-        oxc.append(cp)
+        remote(m.ost.at[b], m.ot.at[b, pl.ds(al(c * 256, 256), 256), :], sib, *iox).start()
     for b in range(2):
         m.ot[b, pl.ds(al(c * 256, 256), 256), :] = m.o[canon_of(2 * c + b)].astype(BF16)
     g_fwd(("wo", 0)).wait()
     g_sib(("wo", 0)).wait()
-    for cp in oxc:
-        cp.wait()
+    sent(m.ost, iox[0])
+    got(m.ost, iox[1])
 
     class Chunk:
         def __init__(self, k):
@@ -397,41 +427,42 @@
             self.p = self.held // nz
             self.lo = 0 if self.kind == "yz" else x * self.held
             self.slots = (w, other) if self.kind == "xyz" else (w,)
-            self.i = ct.take(8 + 2 * nz)
+            self.i, self.keeping = cs.take(), cs.take()
+            self.j = cr.take(6)
 
         def r(self, off, n):
             return pl.ds(al(off, 16), n)
 
         def core(self, q):
-            return remote(self.G.at[2 * q + oc], self.A.at[q], sib, self.i + q)
+            return remote(self.G.at[2 * q + oc], self.A.at[q], sib, self.i, self.j)
 
         def y(self):
             if self.kind == "xyz":
-                return remote(self.G.at[other, self.r(self.lo, self.held), :], self.B, yn, self.i + 2)
-            return remote(self.G.at[other], self.B, yn, self.i + 2)
+                return remote(self.G.at[other, self.r(self.lo, self.held), :], self.B, yn, self.i, self.j + 1)
+            return remote(self.G.at[other], self.B, yn, self.i, self.j + 1)
 
         def xs(self):
             if self.kind == "yz":
-                return [remote(self.T, self.X, xn, self.i + 3)]
-            return [remote(self.G.at[v, self.r(ox * self.held, self.held), :], self.X.at[n], xn, self.i + 3 + n)
+                return [remote(self.T, self.X, xn, self.i, self.j + 2)]
+            return [remote(self.G.at[v, self.r(ox * self.held, self.held), :], self.X.at[n], xn, self.i, self.j + 2)
                     for n, v in enumerate(self.slots)]
 
         def z(self, d):
             q, dev = zpeer(d)
             return remote(self.G.at[w, self.r(self.lo + q * self.p, self.p), :], self.Z.at[nz - 1 - d], dev,
-                          self.i + 4 + d)
+                          self.i, self.j + 3)
 
         def back(self, d):
-            return remote(self.T, self.H.at[self.r(g * self.p, self.p), :], zpeer(d)[1], self.i + 3 + nz + d)
+            return remote(self.T, self.H.at[self.r(g * self.p, self.p), :], zpeer(d)[1], self.i, self.j + 4)
 
         def at(self):
             return red_out.at[self.r(self.start + self.lo, self.held), :]
 
         def xback(self):
-            return remote(self.H, self.at(), xn, self.i + 3 + 2 * nz)
+            return remote(self.H, self.at(), xn, self.i, self.j + 5)
 
         def keep(self):
-            return local(self.H, self.at(), self.i + 4 + 2 * nz)
+            return local(self.H, self.at(), self.keeping)
 
         def add(self, slot, rows, v):
             self.G[slot, rows, :] = (self.G[slot, rows, :].astype(F32) + v.astype(F32)).astype(BF16)
@@ -441,8 +472,8 @@
                 self.core(q).start()
 
         def add_core(self):
-            for q in range(2):
-                self.core(q).wait()
+            sent(self.A, self.i)
+            got(self.A, self.j)
             whole = slice(0, self.rows)
             self.add(other, whole, self.A[oy])
             if self.kind != "xyz":
@@ -455,9 +486,12 @@
             for cp in self.xs():
                 cp.start()
 
+        def x_wait(self):
+            sent(self.X, self.i)
+            got(self.X, self.j + 2)
+
         def x_add(self):
-            for cp in self.xs():
-                cp.wait()
+            self.x_wait()
             for n, v in reversed(list(enumerate(self.slots))):
                 self.add(v, self.r(self.lo, self.held), self.X[n])
                 if n == 1:
@@ -475,8 +509,8 @@
                 self.z(d).start()
 
         def z_sum(self):
-            for d in range(1, nz):
-                self.z(d).wait()
+            sent(self.Z, self.i)
+            got(self.Z, self.j + 3)
             tot = self.G[w, self.r(self.lo + g * self.p, self.p), :].astype(F32)
             for d in range(nz - 1):
                 tot = tot + self.Z[d].astype(F32)
@@ -511,14 +545,13 @@
                     self.x_go()
             elif n == 4:
                 if self.kind == "yz":
-                    for cp in self.xs():
-                        cp.wait()
+                    self.x_wait()
                     self.z_back((self.T[...].astype(F32) + self.X[...].astype(F32)).astype(BF16))
                 else:
                     self.z_back(self.z_sum())
             elif n == 5:
-                for d in range(1, nz):
-                    self.back(d).wait()
+                sent(self.Z, self.i)
+                got(self.Z, self.j + 4)
                 if self.kind != "yz":
                     self.xback().start()
                 self.keep().start()
@@ -527,27 +560,26 @@
                     self.xback().wait()
                 self.keep().wait()
 
-    qi = ct.take(4 * (4 + 2 * ne))
-    qn, qp = 4 + 2 * ne, QROWS // ne
+    qs, qk, qr, qp = cs.take(4), cs.take(4), cr.take(16), QROWS // ne
 
     def q_core(k, q):
-        return remote(m.QS.at[k, 2 * q + oc], m.QG.at[k, q, pl.ds(al(c * 192, 64), 192), :], sib, qi + k * qn + q)
+        return remote(m.QS.at[k, 2 * q + oc], m.QG.at[k, q, pl.ds(al(c * 192, 64), 192), :], sib, qs + k, qr + 4 * k)
 
     def q_y(k):
-        return remote(m.QG.at[k, oy], m.QB.at[k], yn, qi + k * qn + 2)
+        return remote(m.QG.at[k, oy], m.QB.at[k], yn, qs + k, qr + 4 * k + 1)
 
     def q_rs(k, d):
         q, dev = peer(d)
-        return remote(m.QG.at[k, yi, pl.ds(al(q * qp, 16), qp), :], m.QC.at[k, ne - 1 - d], dev, qi + k * qn + 3 + d)
+        return remote(m.QG.at[k, yi, pl.ds(al(q * qp, 16), qp), :], m.QC.at[k, ne - 1 - d], dev, qs + k, qr + 4 * k + 2)
 
     def q_at(k):
         return red_out.at[pl.ds(al(QSTART + k * QROWS + e * qp, 16), qp), :]
 
     def q_ag(k, d):
-        return remote(m.QT.at[k], q_at(k), peer(d)[1], qi + k * qn + 2 + ne + d)
+        return remote(m.QT.at[k], q_at(k), peer(d)[1], qs + k, qr + 4 * k + 3)
 
     def q_keep(k):
-        return local(m.QT.at[k], q_at(k), qi + k * qn + 3)
+        return local(m.QT.at[k], q_at(k), qk + k)
 
     def q0(k):
         for q in range(2):
@@ -556,8 +588,9 @@
             m.QG[k, q, pl.ds(al(c * 192, 64), 192), :] = m.QS[k, 2 * q + c]
 
     def q1(k):
-        for q in range(2):
-            q_core(k, q).wait()
+        half = m.QG.at[k, :, 0:192, :]
+        sent(half, qs + k)
+        got(half, qr + 4 * k)
         q_y(k).start()
 
     def q2(k):
@@ -567,8 +600,8 @@
             q_rs(k, d).start()
 
     def q3(k):
-        for d in range(1, ne):
-            q_rs(k, d).wait()
+        sent(m.QC.at[k], qs + k)
+        got(m.QC.at[k], qr + 4 * k + 2)
         tot = m.QG[k, yi, pl.ds(al(e * qp, 16), qp), :].astype(F32)
         for d in range(ne - 1):
             tot = tot + m.QC[k, d].astype(F32)
@@ -578,8 +611,8 @@
         q_keep(k).start()
 
     def q4(k):
-        for d in range(1, ne):
-            q_ag(k, d).wait()
+        sent(m.QC.at[k], qs + k)
+        got(m.QC.at[k], qr + 4 * k + 3)
         q_keep(k).wait()
 
     chunks = [Chunk(k) for k in range(5)]
@@ -588,7 +621,7 @@
     def events(key):
         for k, n in PLAN.get(key, ()):
             if k == 9:
-                swap(m.dup, y_out, iy, n, "start", 128)
+                swap_go(m.dup, y_out, iy, n, 128)
             elif k < 5:
                 chunks[k].step(n)
             else:
@@ -605,8 +638,6 @@
 
     def c1(t, _):
         rows = pl.ds(al(t * 512, 512), 512)
-        for u in range(2):
-            swap(cot_h, m.dys, idy, 2 * t + u, "wait")
         mid = m.xs[rows, :].astype(F32) + dg(m.ot[t], m.wo[...], 0, 0)
         xc = mid - rowmean(mid)
         r = lax.rsqrt(rowmean(xc * xc) + EPS)
@@ -623,15 +654,17 @@
         m.da[rows, :] = jnp.zeros((512, 512), F32)
         return 0
 
+    swap_wait(m.dys, idy)
     lax.fori_loop(0, 2, c1, 0)
-    g_forward(*pieces[8:])
-    for p in pieces[2:]:
-        g_sib(p).wait()
-        g_fwd(p).wait()
-    for p in pieces:
-        g_y(p).wait_send()
 
     def c2(f, _):
+        for u in range(4):
+            @pl.when(f == u)
+            def _():
+                if u == 0:
+                    sent(big8, isib[0])
+                    got(big8, isib[1])
+                got(big2, ifr + u)
         bu = jnp.concatenate([m.vec[s, pl.ds(5 + f, 1), :] for s in range(4)], axis=1)
         wuf, wdf = m.wu[f], m.wd[f]
         up = dg(m.a2[...], wuf, 1, 0) + bu
@@ -648,6 +681,10 @@
         m.gbu[f, 0:1, :] = colsum(dv.astype(F32))
         m.da[...] += dg(dv, wuf, 1, 1)
 
+        @pl.when(f == 0)
+        def _():
+            g_forward(*pieces[8:])
+
         when_events("f", f, range(4))
         gd = dg(m.dyt[...], m.act[...], 1, 0).astype(BF16)
         for s in range(4):
@@ -660,11 +697,15 @@
         return 0
 
     lax.fori_loop(0, 4, c2, 0)
+    for p in pieces[:2]:
+        g_y(p).wait_send()
+    sent(big8, iys)
+    sent(big8, ifs)
     yst, dmid = m.dup, m.act
-    idx = ct.take(2)
+    idx = pair()
 
     def d_piece(t):
-        return remote(m.dst.at[t], m.do.at[2 * c + t], sib, idx + t)
+        return remote(m.dst.at[t], m.do.at[2 * c + t], sib, *idx)
 
     def c3(t, _):
         rows = pl.ds(al(t * 512, 512), 512)
@@ -689,14 +730,14 @@
         for b in range(4):
             m.OG[s, b * 128:(b + 1) * 128, :] = go[s * 128:(s + 1) * 128, b * 128:(b + 1) * 128]
     events("go")
-    for t in range(2):
-        d_piece(t).wait()
-
-    ixq = ct.take(8)
+    sent(m.dst, idx[0])
+    got(m.dst, idx[1])
+
+    ixq = pair()
 
     def x_piece(h, b):
         return remote(m.xst.at[h, b], m.dqt.at[pl.ds(al(c * 768 + h * 192, 64), 192), pl.ds(b * 512, 512)], sib,
-                      ixq + h * 2 + b)
+                      *ixq)
 
     def x_start(h):
         hrows = pl.ds(al(h * 192, 64), 192)
@@ -757,12 +798,8 @@
 
     lax.fori_loop(0, 4, bwd_head, 0)
 
-    def x_wait(h, _):
-        for b in range(2):
-            x_piece(h, b).wait()
-        return 0
-
-    lax.fori_loop(0, 4, x_wait, 0)
+    sent(m.xst, ixq[0])
+    got(m.xst, ixq[1])
     wgst = m.dys
 
     def e1(t, _):
@@ -777,7 +814,7 @@
         gr = dav * g1
         dn = r * (gr - rowmean(gr) - nv * rowmean(gr * nv))
         wgst[rows, :] = (dmid[rows, :].astype(F32) + dn).astype(BF16)
-        swap(wgst, wg_out, iw, t, "start", 128)
+        swap_go(wgst, wg_out, iw, t, 128)
         when_events("w", t, range(4))
         return 0
 
@@ -787,30 +824,29 @@
             m.gv[s, k:k + 1, :] = m.gg[k:k + 1, s * 128:(s + 1) * 128]
         for f in range(4):
             m.gv[s, 5 + f:6 + f, :] = m.gbu[f, 0:1, s * 128:(s + 1) * 128]
-    vx = [remote(m.gv.at[2 * q + oc], m.gvr.at[q], sib, ct.take()) for q in range(2)]
-    vy = remote(m.gv.at[other], m.gvy, yn, ct.take())
-    iv = ct.take(ne - 1)
-    va = [remote(m.gv.at[w], m.gva.at[e], peer(d)[1], iv + d - 1) for d in range(1, ne)]
+    ivx, ivy, iva = pair(), pair(), pair()
+    vx = [remote(m.gv.at[2 * q + oc], m.gvr.at[q], sib, *ivx) for q in range(2)]
+    vy = remote(m.gv.at[other], m.gvy, yn, *ivy)
+    va = [remote(m.gv.at[w], m.gva.at[e], peer(d)[1], *iva) for d in range(1, ne)]
     for cp in vx:
         cp.start()
     for t in range(4, 6):
-        swap(wgst, wg_out, iw, t, "start", 128)
-    for cp in vx:
-        cp.wait()
+        swap_go(wgst, wg_out, iw, t, 128)
+    sent(m.gvr, ivx[0])
+    got(m.gvr, ivx[1])
     for q in range(2):
         m.gv[2 * q + c] = m.gv[2 * q + c] + m.gvr[q]
     vy.start()
-    q3(2)
+    events("tail")
     vy.wait()
     m.gv[w] = m.gv[w] + m.gvy[...]
     m.gva[e] = m.gv[w]
     for cp in va:
         cp.start()
-    q3(3)
     for t in range(6, 8):
-        swap(wgst, wg_out, iw, t, "start", 128)
-    for cp in va:
-        cp.wait()
+        swap_go(wgst, wg_out, iw, t, 128)
+    sent(m.gva.at[0:ne - 1], iva[0])
+    got(m.gva.at[0:ne - 1], iva[1])
     tot = m.gva[0]
     for d in range(1, ne):
         tot = tot + m.gva[d]
@@ -820,12 +856,11 @@
 
     def fin(t, _):
         q4(t)
-        for u in range(2):
-            swap(m.dup, y_out, iy, 2 * t + u, "wait", 128)
-            swap(wgst, wg_out, iw, 2 * t + u, "wait", 128)
         return 0
 
     lax.fori_loop(0, 4, fin, 0)
+    swap_wait(m.dup, iy)
+    swap_wait(wgst, iw)
 
 
 def layer(nz, *ops):
@@ -837,9 +872,9 @@
     return pl.pallas_call(
         functools.partial(body, nz, names),
         out_shape=(sd((1024, 512), BF16), sd((1024, 512), BF16), sd((ROWS, 128), BF16), sd((16, 128), F32)),
-        in_specs=[any_] * 6 + [vm] * 8,
+        in_specs=[any_] * 14,
         out_specs=(any_, any_, any_, vm),
-        scratch_shapes=[sc[n] for n in names] + [pltpu.SemaphoreType.DMA((NSEM,)), pltpu.SemaphoreType.DMA((NSEM,))],
+        scratch_shapes=[sc[n] for n in names] + [pltpu.SemaphoreType.DMA((NSEND,)), pltpu.SemaphoreType.DMA((NRECV,))],
         compiler_params=pltpu.CompilerParams(collective_id=0, has_side_effects=True, vmem_limit_bytes=VLIM),
         name="layer",
     )(*ops)

time: 137 us -> 132 us (0.964)
  Pallas kernels: 136 us -> 130 us
    pallas_call x1, Pallas kernels: 130 us -> 125 us  [layer(): pl.pallas_call(functools.partial(body, nz, names), out_shape=(sd((1024, 5...]
where the time goes in v4:
time: 132 us; the launch traced here: 131 us
  Pallas kernels  130 us (98%)
    pallas_call x1, Pallas kernels, layer(): pl.pallas_call(functools.partial(body, nz, names), out_shape=(sd((1024, 5...  125 us
    pallas_call x1, Pallas kernels, finish(): pl.pallas_call(finish_body, out_shape=(sd((1024, 512), BF16), sd((1024, 5...  5.14 us

profile of v4, /device:TPU:0, one launch (start us, length us, event | category | flops | bytes accessed | tf_op | source)
XLA Modules:
  0.0 130.5 jit_solution(6070822222293429902)
XLA Ops:
  0.6 124.5 %layer.1 = (bf16[1024,512]{1,0:T(8,128)(2,1)}, bf16[1024,512]{1,0:T(8,128)(2,1)}, bf16[6144,128]{1,0:T(8,128)(2,1)}, f32[16,128]{1,0:T(8,128)}) custom-call(bf16[1024,512]{1,0:T(8,128)(2,1)} %bitcast.17, bf16[1024,512]{1,0:T(8,128)(2,1)} %bitcast.18, bf16[128,1536]{1,0:T(8,128)(2,1)} %args_2_.4, bf16[128,512]{1,0:T(8,128)(2,1)} %args_3_.4, ...), custom_call_target="tpu_custom_call" | custom-call | tf_op jit(solution)/shard_map/layer/pallas_call | solution.py:872
  125.2 5.1 %finish.1 = (bf16[1024,512]{1,0:T(8,128)(2,1)}, f32[1024,512]{1,0:T(8,128)}, f32[128,1536]{1,0:T(8,128)}, f32[128,512]{1,0:T(8,128)}, f32[128,2048]{1,0:T(8,128)...) custom-call(bf16[1024,512]{1,0:T(8,128)(2,1)} %get-tuple-element.28., ...), custom_call_target="tpu_custom_call" | custom-call | tf_op jit(solution)/shard_map/finish/pallas_call | solution.py:953

commit v5 on v4

--- a/solution.py
+++ b/solution.py
@@ -18,7 +18,7 @@
 FROWS, OROWS, QROWS = 1024, 512, 384
 OSTART, QSTART, ROWS = 4096, 4608, 6144
 NSEND, NRECV = 64, 96
-CHUNKS = (("F0", FROWS, "yxz"), ("F1", FROWS, "yxz"), ("F2", FROWS, "yxz"), ("F3", FROWS, "yxz"), ("O", OROWS, "yxz"))
+CHUNKS = (("F0", FROWS, "xyz"), ("F1", FROWS, "yxz"), ("F2", FROWS, "xyz"), ("F3", FROWS, "yxz"), ("O", OROWS, "yxz"))
 
 
 PLAN = {
@@ -29,27 +29,27 @@
     ("g", 2): ((2, 0),),
     ("f", 3): ((0, 2), (2, 1),),
     ("g", 3): ((3, 0),),
-    ("c", 0): ((1, 2), (9, 0),),
-    ("c", 1): ((3, 1), (0, 3), (9, 1),),
+    ("c", 0): ((1, 2), (3, 1), (9, 0),),
+    ("c", 1): ((0, 3), (9, 1),),
     "go": ((4, 0), (9, 2),),
-    ("d", 0): ((2, 2), (1, 3), (4, 1), (0, 4), (9, 3),),
-    ("D", 0): ((9, 4),),
-    ("e", 0): ((3, 2), (9, 5),),
-    ("q", 0): ((5, 0), (2, 3), (1, 4), (4, 2),),
-    ("d", 1): ((5, 1), (0, 5), (9, 6),),
-    ("D", 1): ((3, 3), (2, 4), (9, 7),),
-    ("e", 1): ((4, 3), (5, 2), (1, 5),),
-    ("q", 1): ((6, 0),),
-    ("d", 2): ((3, 4), (6, 1),),
-    ("D", 2): ((2, 5), (4, 4),),
-    ("e", 2): ((5, 3), (6, 2),),
-    ("q", 2): ((7, 0),),
-    ("d", 3): ((3, 5), (7, 1), (4, 5),),
+    ("d", 0): ((2, 2), (4, 1), (1, 3), (0, 4), (9, 3),),
+    ("D", 0): ((3, 2), (9, 4),),
+    ("e", 0): ((9, 5),),
+    ("q", 0): ((5, 0), (2, 3), (1, 4),),
+    ("d", 1): ((5, 1), (4, 2), (0, 5), (9, 6),),
+    ("D", 1): ((3, 3), (9, 7),),
+    ("e", 1): ((2, 4),),
+    ("q", 1): ((6, 0), (5, 2), (4, 3), (1, 5),),
+    ("d", 2): ((6, 1), (3, 4),),
+    ("e", 2): ((2, 5),),
+    ("q", 2): ((7, 0), (6, 2), (5, 3),),
+    ("d", 3): ((4, 4), (7, 1),),
+    ("D", 3): ((3, 5),),
     ("e", 3): ((6, 3),),
     ("q", 3): ((8, 0), (7, 2),),
-    ("w", 0): ((8, 1),),
+    "x": ((4, 5), (8, 1),),
+    ("w", 1): ((8, 2),),
     ("w", 2): ((7, 3),),
-    ("w", 3): ((8, 2),),
     "tail": ((8, 3),),
 }
 
@@ -800,6 +800,7 @@
 
     sent(m.xst, ixq[0])
     got(m.xst, ixq[1])
+    events("x")
     wgst = m.dys
 
     def e1(t, _):

time: 132 us -> 128 us (0.970)
  Pallas kernels: 130 us -> 125 us
    pallas_call x1, Pallas kernels: 125 us -> 120 us  [layer(): pl.pallas_call(functools.partial(body, nz, names), out_shape=(sd((1024, 5...]
where the time goes in v5:
time: 128 us; the launch traced here: 126 us
  Pallas kernels  125 us (98%)
    pallas_call x1, Pallas kernels, layer(): pl.pallas_call(functools.partial(body, nz, names), out_shape=(sd((1024, 5...  120 us
    pallas_call x1, Pallas kernels, finish(): pl.pallas_call(finish_body, out_shape=(sd((1024, 512), BF16), sd((1024, 5...  5.14 us

profile of v5, /device:TPU:0, one launch (start us, length us, event | category | flops | bytes accessed | tf_op | source)
XLA Modules:
  0.0 126.0 jit_solution(14598918766419283610)
XLA Ops:
  0.6 120.0 %layer.1 = (bf16[1024,512]{1,0:T(8,128)(2,1)}, bf16[1024,512]{1,0:T(8,128)(2,1)}, bf16[6144,128]{1,0:T(8,128)(2,1)}, f32[16,128]{1,0:T(8,128)}) custom-call(bf16[1024,512]{1,0:T(8,128)(2,1)} %bitcast.17, bf16[1024,512]{1,0:T(8,128)(2,1)} %bitcast.18, bf16[128,1536]{1,0:T(8,128)(2,1)} %args_2_.4, bf16[128,512]{1,0:T(8,128)(2,1)} %args_3_.4, ...), custom_call_target="tpu_custom_call" | custom-call | tf_op jit(solution)/shard_map/layer/pallas_call | solution.py:873
  120.7 5.1 %finish.1 = (bf16[1024,512]{1,0:T(8,128)(2,1)}, f32[1024,512]{1,0:T(8,128)}, f32[128,1536]{1,0:T(8,128)}, f32[128,512]{1,0:T(8,128)}, f32[128,2048]{1,0:T(8,128)...) custom-call(bf16[1024,512]{1,0:T(8,128)(2,1)} %get-tuple-element.28., ...), custom_call_target="tpu_custom_call" | custom-call | tf_op jit(solution)/shard_map/finish/pallas_call | solution.py:954

commit v6 on v5

--- a/solution.py
+++ b/solution.py
@@ -17,7 +17,7 @@
 VLIM = 63 * 1024 * 1024
 FROWS, OROWS, QROWS = 1024, 512, 384
 OSTART, QSTART, ROWS = 4096, 4608, 6144
-NSEND, NRECV = 64, 96
+NSEND, NRECV = 66, 90
 CHUNKS = (("F0", FROWS, "xyz"), ("F1", FROWS, "yxz"), ("F2", FROWS, "xyz"), ("F3", FROWS, "yxz"), ("O", OROWS, "yxz"))
 
 
@@ -36,8 +36,8 @@
     ("D", 0): ((3, 2), (9, 4),),
     ("e", 0): ((9, 5),),
     ("q", 0): ((5, 0), (2, 3), (1, 4),),
-    ("d", 1): ((5, 1), (4, 2), (0, 5), (9, 6),),
-    ("D", 1): ((3, 3), (9, 7),),
+    ("d", 1): ((5, 1), (4, 2), (0, 5), (3, 3), (9, 6),),
+    ("D", 1): ((9, 7),),
     ("e", 1): ((2, 4),),
     ("q", 1): ((6, 0), (5, 2), (4, 3), (1, 5),),
     ("d", 2): ((6, 1), (3, 4),),
@@ -88,7 +88,7 @@
     ne = 2 * nz
     V = lambda *s, t=BF16: pltpu.VMEM(s, t)
     return dict(
-        xs=V(1024, 512), dys=V(1024, 512), wqr=V(128, 1536), wur=V(128, 2048), wt=V(1536, 512), wo=V(512, 512),
+        xs=V(1024, 512), dys=V(1024, 512), wt=V(1536, 512), wo=V(512, 512),
         wu=V(4, 512, 512), wd=V(4, 512, 512), vown=V(16, 128, t=F32), vec=V(4, 16, 128, t=F32),
         so=V(2, 8, 128, t=jnp.int32), sseg=V(1, 4, t=jnp.int32), soff=V(1, 4, t=jnp.int32),
         s1g=V(1, 128), s1b=V(1, 128), s2g=V(1, 128), s2b=V(1, 128), sbd=V(1, 128), sbu=V(4, 128), sm=pltpu.SMEM((8, 128), jnp.int32),
@@ -98,7 +98,7 @@
         act=V(1024, 512), dup=V(1024, 512), do=V(4, 256, 512), dst=V(2, 256, 512), dq=V(4, 768, 512),
         dkv=V(128, 2048, t=F32), xst=V(4, 2, 192, 512), dqt=V(1536, 1024),
         gv=V(4, 16, 128, t=F32), gvr=V(2, 16, 128, t=F32), gvy=V(16, 128, t=F32), gva=V(ne, 16, 128, t=F32),
-        gg=V(8, 512, t=F32), gbu=V(4, 8, 512, t=F32),
+        n1=V(1024, 512, t=F32), r1=V(1024, 128, t=F32), gg=V(8, 512, t=F32), gbu=V(4, 8, 512, t=F32),
         FG=V(4, 4, FROWS, 128), OG=V(4, OROWS, 128),
         **{f"{t}{q}": v for t, rows, kind in CHUNKS for q, v in chunk_scratch(nz, rows, kind).items()},
         QS=V(4, 4, 192, 128), QG=V(4, 2, QROWS, 128), QB=V(4, QROWS, 128), QC=V(4, ne - 1, QROWS // ne, 128),
@@ -176,11 +176,11 @@
     def _():
         pl.semaphore_signal(bar, inc=1, device_id=sw, device_id_type=MESH)
 
-    l_wq = begin(wq_h, m.wqr)
+    l_wq = [begin(wq_h.at[:, pl.ds(k * 512, 512)], m.act.at[pl.ds(k * 128, 128), :]) for k in range(3)]
     l_small = [begin(a, b) for a, b in zip((n1g, n1b, n2g, n2b, bdr, bur, seg_r, off_r),
                                            (m.s1g, m.s1b, m.s2g, m.s2b, m.sbd, m.sbu, m.sseg, m.soff))]
     l_wo = begin(wo_h, m.wo.at[pl.ds(al(w * 128, 128), 128), :])
-    l_wu = begin(wu_h, m.wur)
+    l_wu = [begin(wu_h.at[:, pl.ds(k * 512, 512)], m.dup.at[pl.ds(k * 128, 128), :]) for k in range(4)]
     l_wd = begin(wd_h, m.wd.at[:, pl.ds(al(w * 128, 128), 128), :])
     m.vown[...] = jnp.zeros_like(m.vown)
     m.so[0] = jnp.zeros((8, 128), jnp.int32)
@@ -225,12 +225,13 @@
     m.vec[w] = m.vown[...]
 
     mine = pl.ds(al(w * 128, 128), 128)
-    l_wq.wait()
+    for cp in l_wq:
+        cp.wait()
     for cc in range(2):
         for hp in range(2):
             for part in range(3):
                 b = (part * 4 + cc * 2 + hp) * 128
-                blk = m.wqr[:, b:b + 128].T
+                blk = m.act[part * 128:(part + 1) * 128, b - part * 512:b - part * 512 + 128].T
                 if part == 0:
                     blk = (blk.astype(F32) * 0.125).astype(BF16)
                 r = cc * 768 + hp * 384 + part * 64
@@ -282,10 +283,11 @@
     for v in vcs:
         v.start()
     so_x.start()
-    l_wu.wait()
+    for cp in l_wu:
+        cp.wait()
     for f in range(4):
         for s in range(4):
-            m.wu[f, mine, s * 128:(s + 1) * 128] = m.wur[:, s * 512 + f * 128:s * 512 + (f + 1) * 128]
+            m.wu[f, mine, s * 128:(s + 1) * 128] = m.dup[s * 128:(s + 1) * 128, f * 128:(f + 1) * 128]
     l_wo.wait()
     l_wd.wait()
     for p in pieces[1:]:
@@ -318,8 +320,11 @@
         xv = m.xs[rows, :].astype(F32)
         xc = xv - rowmean(xv)
         r = lax.rsqrt(rowmean(xc * xc) + EPS)
-        a_slot(c, t)[...] = (xc * r * g1 + b1).astype(BF16)
+        nv = xc * r
+        a_slot(c, t)[...] = (nv * g1 + b1).astype(BF16)
         a_piece(t).start()
+        m.n1[rows, :] = nv
+        m.r1[rows, :] = jnp.broadcast_to(r, (256, 128))
         return 0
 
     wrows = pl.ds(al(c * 768, 256), 768)
@@ -378,14 +383,13 @@
         top = mx[0]
         for j in range(1, 4):
             top = jnp.concatenate([top[:, :j * BLK], jnp.maximum(top[:, j * BLK:], mx[j])], axis=1)
-        acc = tot = None
+        acc = None
         for j in range(4):
-            p = jnp.exp(s[j] - top[:, j * BLK:])
-            lj = colsum(p)
-            a = dg(m.qkv[phys[j], rows_of(h, 2), :], p.astype(BF16), 1, 0)
+            p = jnp.exp(s[j] - top[:, j * BLK:]).astype(BF16)
+            a = dg(jnp.concatenate([m.qkv[phys[j], rows_of(h, 2), :], jnp.ones((16, BLK), BF16)], axis=0), p, 1, 0)
             acc = a if acc is None else jnp.concatenate([acc[:, :j * BLK], acc[:, j * BLK:] + a], axis=1)
-            tot = lj if tot is None else jnp.concatenate([tot[:, :j * BLK], tot[:, j * BLK:] + lj], axis=1)
-        ov = acc * (1.0 / tot)
+        tot = acc[HD:HD + 1]
+        ov = acc[:HD] * (1.0 / tot)
         ls = top + jnp.log(tot)
         for i in range(4):
             m.o[i, pl.ds(al(h * HD, HD), HD), :] = ov[:, i * BLK:(i + 1) * BLK]
@@ -805,10 +809,7 @@
 
     def e1(t, _):
         rows = pl.ds(al(t * 256, 256), 256)
-        xv = m.xs[rows, :].astype(F32)
-        xc = xv - rowmean(xv)
-        r = lax.rsqrt(rowmean(xc * xc) + EPS)
-        nv = xc * r
+        nv, r = m.n1[rows, :], m.r1[rows, 0:1]
         dav = dg(m.dqt[:, rows], m.wt[...], 0, 0)
         m.gg[0:1, :] += colsum(dav * nv)
         m.gg[1:2, :] += colsum(dav)

time: 128 us -> 127 us (level)
  no operation moved by 1% of the time
where the time goes in v6:
time: 127 us; the launch traced here: 125 us
  Pallas kernels  124 us (98%)
    pallas_call x1, Pallas kernels, layer(): pl.pallas_call(functools.partial(body, nz, names), out_shape=(sd((1024, 5...  119 us
    pallas_call x1, Pallas kernels, finish(): pl.pallas_call(finish_body, out_shape=(sd((1024, 512), BF16), sd((1024, 5...  5.14 us

profile of v6, /device:TPU:0, one launch (start us, length us, event | category | flops | bytes accessed | tf_op | source)
XLA Modules:
  0.0 124.8 jit_solution(3861810234040361542)
XLA Ops:
  0.6 118.8 %layer.1 = (bf16[1024,512]{1,0:T(8,128)(2,1)}, bf16[1024,512]{1,0:T(8,128)(2,1)}, bf16[6144,128]{1,0:T(8,128)(2,1)}, f32[16,128]{1,0:T(8,128)}) custom-call(bf16[1024,512]{1,0:T(8,128)(2,1)} %bitcast.17, bf16[1024,512]{1,0:T(8,128)(2,1)} %bitcast.18, bf16[128,1536]{1,0:T(8,128)(2,1)} %args_2_.4, bf16[128,512]{1,0:T(8,128)(2,1)} %args_3_.4, ...), custom_call_target="tpu_custom_call" | custom-call | tf_op jit(solution)/shard_map/layer/pallas_call | solution.py:874
  119.5 5.1 %finish.1 = (bf16[1024,512]{1,0:T(8,128)(2,1)}, f32[1024,512]{1,0:T(8,128)}, f32[128,1536]{1,0:T(8,128)}, f32[128,512]{1,0:T(8,128)}, f32[128,2048]{1,0:T(8,128)...) custom-call(bf16[1024,512]{1,0:T(8,128)(2,1)} %get-tuple-element.28., ...), custom_call_target="tpu_custom_call" | custom-call | tf_op jit(solution)/shard_map/finish/pallas_call | solution.py:955

commit v7 on v6

--- a/solution.py
+++ b/solution.py
@@ -18,7 +18,7 @@
 FROWS, OROWS, QROWS = 1024, 512, 384
 OSTART, QSTART, ROWS = 4096, 4608, 6144
 NSEND, NRECV = 66, 90
-CHUNKS = (("F0", FROWS, "xyz"), ("F1", FROWS, "yxz"), ("F2", FROWS, "xyz"), ("F3", FROWS, "yxz"), ("O", OROWS, "yxz"))
+CHUNKS = (("F0", FROWS, "yxz"), ("F1", FROWS, "xyz"), ("F2", FROWS, "xyz"), ("F3", FROWS, "yxz"), ("O", OROWS, "yxz"))
 
 
 PLAN = {
@@ -32,24 +32,22 @@
     ("c", 0): ((1, 2), (3, 1), (9, 0),),
     ("c", 1): ((0, 3), (9, 1),),
     "go": ((4, 0), (9, 2),),
-    ("d", 0): ((2, 2), (4, 1), (1, 3), (0, 4), (9, 3),),
-    ("D", 0): ((3, 2), (9, 4),),
-    ("e", 0): ((9, 5),),
-    ("q", 0): ((5, 0), (2, 3), (1, 4),),
-    ("d", 1): ((5, 1), (4, 2), (0, 5), (3, 3), (9, 6),),
-    ("D", 1): ((9, 7),),
-    ("e", 1): ((2, 4),),
-    ("q", 1): ((6, 0), (5, 2), (4, 3), (1, 5),),
-    ("d", 2): ((6, 1), (3, 4),),
-    ("e", 2): ((2, 5),),
-    ("q", 2): ((7, 0), (6, 2), (5, 3),),
-    ("d", 3): ((4, 4), (7, 1),),
-    ("D", 3): ((3, 5),),
-    ("e", 3): ((6, 3),),
-    ("q", 3): ((8, 0), (7, 2),),
+    ("d", 0): ((1, 3), (4, 1), (9, 3),),
+    ("D", 0): ((0, 4), (2, 2), (9, 4),),
+    ("e", 0): ((3, 2), (9, 5),),
+    ("q", 0): ((5, 0), (1, 4),),
+    ("d", 1): ((4, 2), (5, 1), (0, 5), (9, 6),),
+    ("D", 1): ((2, 3), (9, 7),),
+    ("e", 1): ((1, 5), (3, 3),),
+    ("q", 1): ((6, 0), (5, 2), (4, 3),),
+    ("d", 2): ((2, 4), (6, 1),),
+    ("D", 2): ((3, 4),),
+    ("q", 2): ((7, 0), (6, 2), (4, 4),),
+    ("d", 3): ((7, 1), (5, 3), (2, 5),),
+    ("e", 3): ((3, 5),),
+    ("q", 3): ((8, 0), (7, 2), (6, 3),),
     "x": ((4, 5), (8, 1),),
-    ("w", 1): ((8, 2),),
-    ("w", 2): ((7, 3),),
+    ("w", 1): ((7, 3), (8, 2),),
     "tail": ((8, 3),),
 }
 

time: 127 us -> 131 us (1.031)
  Pallas kernels: 124 us -> 127 us
    pallas_call x1, Pallas kernels: 119 us -> 122 us  [layer(): pl.pallas_call(functools.partial(body, nz, names), out_shape=(sd((1024, 5...]
where the time goes in v7:
time: 131 us; the launch traced here: 128 us
  Pallas kernels  127 us (97%)
    pallas_call x1, Pallas kernels, layer(): pl.pallas_call(functools.partial(body, nz, names), out_shape=(sd((1024, 5...  122 us
    pallas_call x1, Pallas kernels, finish(): pl.pallas_call(finish_body, out_shape=(sd((1024, 512), BF16), sd((1024, 5...  5.14 us

profile of v7, /device:TPU:0, one launch (start us, length us, event | category | flops | bytes accessed | tf_op | source)
XLA Modules:
  0.0 128.1 jit_solution(11322779157681372563)
XLA Ops:
  0.6 122.1 %layer.1 = (bf16[1024,512]{1,0:T(8,128)(2,1)}, bf16[1024,512]{1,0:T(8,128)(2,1)}, bf16[6144,128]{1,0:T(8,128)(2,1)}, f32[16,128]{1,0:T(8,128)}) custom-call(bf16[1024,512]{1,0:T(8,128)(2,1)} %bitcast.17, bf16[1024,512]{1,0:T(8,128)(2,1)} %bitcast.18, bf16[128,1536]{1,0:T(8,128)(2,1)} %args_2_.4, bf16[128,512]{1,0:T(8,128)(2,1)} %args_3_.4, ...), custom_call_target="tpu_custom_call" | custom-call | tf_op jit(solution)/shard_map/layer/pallas_call | solution.py:872
  122.8 5.1 %finish.1 = (bf16[1024,512]{1,0:T(8,128)(2,1)}, f32[1024,512]{1,0:T(8,128)}, f32[128,1536]{1,0:T(8,128)}, f32[128,512]{1,0:T(8,128)}, f32[128,2048]{1,0:T(8,128)...) custom-call(bf16[1024,512]{1,0:T(8,128)(2,1)} %get-tuple-element.28., ...), custom_call_target="tpu_custom_call" | custom-call | tf_op jit(solution)/shard_map/finish/pallas_call | solution.py:953
